TPU v7x, 32 devices: a whole 2x2x4 slice. The times are simulated.
32 devices in a mesh: user: 8 (over y, x, core), item: 4 (over z).
Axes of the slice: x: 2, y: 2, z: 4, core: 2. Of those that a mesh axis runs over, the one named last changes fastest.
Arguments:
- users: float32 [8192, 256], P(('user', 'item')), may hold values from -1.5 to 1.5
- user_accum: float32 [8192, 256], P(('user', 'item')), may hold values from 0.1 to 10
- items: float32 [8192, 256], P(('user', 'item')), may hold values from -1.5 to 1.5
- item_accum: float32 [8192, 256], P(('user', 'item')), may hold values from 0.1 to 10
- ratings: int32 [2, 8192, 1024], P(None, 'user', 'item'), may hold values from 0 to 1
- tile_mask: int32 [2, 64, 8], P(None, 'user', 'item'), may hold values 0 or 1
Outputs:
- users_out: float32 [8192, 256], P(('user', 'item'))
- items_out: float32 [8192, 256], P(('user', 'item'))
All inputs are finite; a program needn't handle non-finite values. No bound on the sum of `tile_mask` on one device may be relied on, other than what follows from the above.
Results may differ from a plain program's by a relative error of at most 0.013.
Values may be sent and summed in bfloat16 or wider, within the bound.
No kernel may reach another device: no remote copies, remote signals or barrier semaphores. Data moves between devices by JAX's collectives and lax.ppermute only.
A program may use at most 64 MiB of HBM per device.

v0:
```python
import jax
import jax.numpy as jnp
from jax import lax
from jax.sharding import PartitionSpec as P


def shifted(array, axis, by):
    count = lax.axis_size(axis)
    return lax.ppermute(array, axis, [(i, (i + by) % count) for i in range(count)])


def adagrad(param, accum, grad):
    accum = accum + grad * grad
    return (param - 0.25 * grad / (jnp.sqrt(accum) + 1e-06), accum)


def expand_mask(mask, rows, cols):
    tile_side = rows // mask.shape[0]
    full = jnp.broadcast_to(
        mask.astype(jnp.float32)[:, None, :, None],
        (mask.shape[0], tile_side, mask.shape[1], tile_side),
    )
    return full.reshape(rows, cols)


def local_grads(user_bf, item_rows, rates, mask):
    item_bf = item_rows.astype(jnp.bfloat16)
    logits = lax.dot_general(
        user_bf, item_bf, (((1,), (1,)), ((), ())), preferred_element_type=jnp.float32
    )
    observed = expand_mask(mask, user_bf.shape[0], item_rows.shape[0])
    errors = (observed * (jax.nn.sigmoid(logits) - rates.astype(jnp.float32))).astype(jnp.bfloat16)
    user_part = jnp.dot(errors, item_bf, preferred_element_type=jnp.float32)
    item_grad = (
        lax.dot_general(
            errors, user_bf, (((0,), (0,)), ((), ())), preferred_element_type=jnp.float32
        )
        + 0.1 * item_rows
    )
    return (user_part, item_grad)


def body(users, user_accum, items, item_accum, ratings, tile_mask):
    strata = ratings.shape[0]
    last_turn = strata - 1
    item_state = jnp.stack((items, item_accum))
    for stratum in range(strata):
        user_bf = lax.all_gather(users.astype(jnp.bfloat16), "item", axis=0, tiled=True)
        user_part, item_grad = local_grads(
            user_bf, item_state[0], ratings[stratum], tile_mask[stratum]
        )
        user_grad = (
            lax.psum_scatter(user_part, "item", scatter_dimension=0, tiled=True) + 0.1 * users
        )
        users, user_accum = adagrad(users, user_accum, user_grad)
        new_items, new_iacc = adagrad(item_state[0], item_state[1], item_grad)
        item_state = jnp.stack((new_items, new_iacc))
        if stratum < last_turn:
            item_state = shifted(item_state, "user", 1)
    item_state = shifted(item_state, "user", -last_turn)
    return (users, item_state[0])


def solution(mesh):
    return jax.shard_map(
        body,
        mesh=mesh,
        in_specs=(
            P(("user", "item"), None),
            P(("user", "item"), None),
            P(("user", "item"), None),
            P(("user", "item"), None),
            P(None, "user", "item"),
            P(None, "user", "item"),
        ),
        out_specs=(P(("user", "item"), None), P(("user", "item"), None)),
        check_vma=False,
    )
```

profile of v0, /device:TPU:0, one launch (start us, length us, event | category | flops | bytes accessed | tf_op | source)
XLA Modules:
  0.0 112.9 jit_solution(14660859512536045529)
XLA Ops:
  7.2 0.0 copy-start.3
  7.2 0.0 reduce-scatter.3.cloned.1.call-start
  7.2 0.7 convert_bitcast_fusion
  8.0 0.1 copy.8
  8.0 1.0 convert_element_type.52
  9.0 17.4 %all_gather.6 = bf16[1024,256]{1,0:T(8,128)(2,1)S(1)} all-gather(bf16[256,256]{1,0:T(8,128)(2,1)S(1)} %convert_element_type.52), channel_id=1, replica_groups=mesh['user'=8,'item'=4] {'item'}, dimensions={0}, use_global_device_ids=true | all-gather | bytes 655360 | tf_op jit(solution)/shard_map/all_gather | solution.py:48
  26.4 0.3 broadcast_in_dim.4
  26.7 0.0 copy-done.3
  26.7 1.7 %fusion.10 = bf16[1024,256]{1,0:T(8,128)(2,1)S(1)} fusion(bf16[1024,256]{1,0:T(8,128)(2,1)S(1)} %all_gather.6, f32[128,8,2,128]{3,2,1,0:T(2,128)S(1)} %bitcast.56, s32[2,1024,256]{2,1,0:T(8,128)} %param.10, f32[256,256]{1,0:T(8,128)S(1)} %copy-done.3), kind=kOutput, calls=%fused_computation.12 | convolution fusion | flops 136118272 | bytes 3407872 | tf_op jit(solution)/shard_map/dot_general | solution.py:28
  28.5 0.0 copy-start.5
  28.5 1.3 %fusion.16 = f32[1024,256]{1,0:T(8,128)} fusion(bf16[1024,256]{1,0:T(8,128)(2,1)S(1)} %fusion.10, f32[256,256]{1,0:T(8,128)S(1)} %copy-done.3), kind=kOutput, calls=%fused_computation.32 | convolution fusion | flops 134283264 | bytes 1835008 | tf_op jit(solution)/shard_map/dot_general | solution.py:33
  29.8 0.0 reduce-scatter.3.cloned.1.call-update
  29.8 0.0 copy-start
  29.8 0.0 copy-start.1
  29.8 0.0 reduce-scatter.5.cloned.1.call-start
  29.8 0.0 copy-done.5
  29.9 0.4 subtract_bitcast_fusion.1
  30.3 0.1 collective-permute-start
  30.4 0.1 copy.9
  30.5 28.5 %reduce-scatter.3.cloned.1.call-done = f32[256,256]{1,0:T(8,128)} async-done(((f32[1024,256]{1,0:T(8,128)}), f32[256,256]{1,0:T(8,128)}) %reduce-scatter.3.cloned.1.call-update) | async-done | bytes 262160 | tf_op jit(solution)/shard_map/reduce_scatter | solution.py:53
  59.0 0.0 copy-done
  59.0 0.0 copy-done.1
  59.0 0.0 copy-start.4
  59.0 1.2 %fusion.15 = bf16[256,256]{1,0:T(8,128)(2,1)S(1)} fusion(f32[256,256]{1,0:T(8,128)S(1)} %copy-done, f32[256,256]{1,0:T(8,128)S(1)} %copy-done.1, f32[256,256]{1,0:T(8,128)} %reduce-scatter.3.cloned.1.call-done), kind=kLoop, calls=%fused_computation.31 | loop fusion | flops 589824 | bytes 917504 | tf_op jit(solution)/shard_map/convert_element_type | solution.py:48
  60.2 16.0 %all_gather.7 = bf16[1024,256]{1,0:T(8,128)(2,1)S(1)} all-gather(bf16[256,256]{1,0:T(8,128)(2,1)S(1)} %fusion.15), channel_id=1, replica_groups=mesh['user'=8,'item'=4] {'item'}, dimensions={0}, use_global_device_ids=true | all-gather | bytes 655360 | tf_op jit(solution)/shard_map/all_gather | solution.py:48
  76.2 0.0 collective-permute-done
  76.2 0.3 broadcast_in_dim.5
  76.6 0.0 copy-done.4
  76.6 0.5 fusion.11
  77.1 1.3 %fusion.19 = f32[1024,256]{1,0:T(8,128)} fusion(bf16[1024,256]{1,0:T(8,128)(2,1)S(1)} %fusion.11, f32[2,256,256]{2,1,0:T(8,128)S(1)} %collective-permute-done), kind=kOutput, calls=%fused_computation.35 | convolution fusion | flops 134217728 | bytes 1703936 | tf_op jit(solution)/shard_map/dot_general | solution.py:33
  78.4 0.0 reduce-scatter.5.cloned.1.call-update
  78.4 0.0 copy-start.2
  78.4 0.4 subtract_bitcast_fusion
  78.9 0.1 collective-permute-start.1
  78.9 6.7 %collective-permute-done.1 = f32[2,256,256]{2,1,0:T(8,128)S(1)} collective-permute-done((f32[2,256,256]{2,1,0:T(8,128)S(1)}, f32[2,256,256]{2,1,0:T(8,128)S(1)}, u32[]{:S(2)}, u32[]{:S(2)}) %collective-permute-start.1) | collective-permute-done | bytes 524320 | tf_op jit(solution)/shard_map/ppermute | solution.py:9
  85.6 0.7 slice_bitcast_fusion
  86.3 17.8 %reduce-scatter.5.cloned.1.call-done = f32[256,256]{1,0:T(8,128)} async-done(((f32[1024,256]{1,0:T(8,128)}), f32[256,256]{1,0:T(8,128)}) %reduce-scatter.5.cloned.1.call-update) | async-done | bytes 262160 | tf_op jit(solution)/shard_map/reduce_scatter | solution.py:53
  104.1 0.0 copy-done.2
  104.1 1.9 %divide_subtract_fusion = f32[256,256]{1,0:T(8,128)} fusion(f32[256,256]{1,0:T(8,128)} %reduce-scatter.5.cloned.1.call-done, f32[256,256]{1,0:T(8,128)S(1)} %copy-done.1, f32[256,256]{1,0:T(8,128)S(1)} %copy-done.2, f32[256,256]{1,0:T(8,128)S(1)} %copy-done), kind=kLoop, calls=%fused_computation.23 | loop fusion | flops 1048576 | bytes 1310720 | tf_op jit(solution)/shard_map/sub | solution.py:14
  (2 shorter events, 0.1 us)
Async XLA Ops:
  7.2 19.6 %copy-start.3 = (f32[256,256]{1,0:T(8,128)S(1)}, f32[256,256]{1,0:T(8,128)}, u32[]{:S(2)}) copy-start(f32[256,256]{1,0:T(8,128)} %param.8) | copy-start | bytes 786436
  7.2 51.8 %reduce-scatter.3.cloned.1.call-start = ((), (), s32[]{:S(2)}) async-start(), calls=%async_computation.2 | async-start | bytes 1310720 | tf_op jit(solution)/shard_map/reduce_scatter | solution.py:53
  28.5 1.4 %copy-start.5 = (f32[256,256]{1,0:T(8,128)S(1)}, f32[256,256]{1,0:T(8,128)}, u32[]{:S(2)}) copy-start(f32[256,256]{1,0:T(8,128)} %param.9) | copy-start | bytes 786436
  29.8 29.2 %copy-start = (f32[256,256]{1,0:T(8,128)S(1)}, f32[256,256]{1,0:T(8,128)}, u32[]{:S(2)}) copy-start(f32[256,256]{1,0:T(8,128)} %param.6) | copy-start | bytes 786436
  29.8 29.2 %copy-start.1 = (f32[256,256]{1,0:T(8,128)S(1)}, f32[256,256]{1,0:T(8,128)}, u32[]{:S(2)}) copy-start(f32[256,256]{1,0:T(8,128)} %param.7) | copy-start | bytes 786436
  29.8 74.3 %reduce-scatter.5.cloned.1.call-start = ((), (), s32[]{:S(2)}) async-start(), calls=%async_computation.3 | async-start | bytes 1310720 | tf_op jit(solution)/shard_map/reduce_scatter | solution.py:53
  30.3 45.9 %collective-permute-start = (f32[2,256,256]{2,1,0:T(8,128)S(1)}, f32[2,256,256]{2,1,0:T(8,128)S(1)}, u32[]{:S(2)}, u32[]{:S(2)}) collective-permute-start(f32[2,256,256]{2,1,0:T(8,128)S(1)} %pad_maximum_fusion), channel_id=1, source_target_pairs={{0,4},{4,8},{8,12},{12,16},{16,20},{20,24},{24,28},{28,0},{1,5},{5... | collective-permute-start | bytes 1572872 | tf_op jit(solution)/shard_map/ppermute | solution.py:9
  59.0 17.6 %copy-start.4 = (s32[2,1024,256]{2,1,0:T(8,128)S(1)}, s32[2,1024,256]{2,1,0:T(8,128)}, u32[]{:S(2)}) copy-start(s32[2,1024,256]{2,1,0:T(8,128)} %param.10) | copy-start | bytes 6291460
  78.4 25.7 %copy-start.2 = (f32[256,256]{1,0:T(8,128)S(1)}, f32[256,256]{1,0:T(8,128)}, u32[]{:S(2)}) copy-start(f32[256,256]{1,0:T(8,128)} %reduce-scatter.3.cloned.1.call-done) | copy-start | bytes 786436
  78.9 6.8 %collective-permute-start.1 = (f32[2,256,256]{2,1,0:T(8,128)S(1)}, f32[2,256,256]{2,1,0:T(8,128)S(1)}, u32[]{:S(2)}, u32[]{:S(2)}) collective-permute-start(f32[2,256,256]{2,1,0:T(8,128)S(1)} %pad_maximum_fusion.1), channel_id=1, source_target_pairs={{0,28},{4,0},{8,4},{12,8},{16,12},{20,16},{24,20},{28,24},{1,29},{... | collective-permute-start | bytes 1572872 | tf_op jit(solution)/shard_map/ppermute | solution.py:9
Sparse Core Ops, SparseCore 0:
  29.9 29.0 reduce-scatter.2
  78.5 25.5 reduce-scatter.4
where the time goes:
time: 113 us
  waiting for transfers between devices  53 us (47%)
  blocking collectives  33.4 us (30%)
  between operations  14.2 us (13%)
  matrix products  5.62 us (5%)
  other arithmetic  4.96 us (4%)
  local copies, waits for them, and re-layouts  1.59 us (1%)
    reduce_scatter x2, waiting for transfers between devices, body(): lax.psum_scatter(user_part, 'item', scatter_dimension=0, tiled=True)  46.3 us
    all_gather x2, blocking collectives, body(): lax.all_gather(users.astype(jnp.bfloat16), 'item', axis=0, tiled=True)  33.4 us
    ppermute x2, waiting for transfers between devices, shifted(): lax.ppermute(array, axis, [(i, (i + by) % count) for i in range(count)])  6.69 us
    dot_general x2, matrix products, local_grads(): user_part = jnp.dot(errors, item_bf, preferred_element_type=jnp.float32)  2.55 us
  transfers between devices with their start and end apart: 4, of which 3 were waited for; matrix products, arithmetic and copies ran while one was open for 3% of the time, Pallas kernels for 0%

commit v1 on v0

v1 whole, which is shorter than its diff:
```python
import jax
import jax.numpy as jnp
from jax import lax
from jax.sharding import PartitionSpec as P

BF = jnp.bfloat16
F32 = jnp.float32


def adagrad(param, accum, grad):
    accum = accum + grad * grad
    return (param - 0.25 * grad / (jnp.sqrt(accum) + 1e-06), accum)


def move(array, by_user, item_map):
    n_user, n_item = lax.axis_size("user"), lax.axis_size("item")
    if by_user == 0:
        return lax.ppermute(array, "item", [(z, item_map(z)) for z in range(n_item)])
    pairs = [
        (u * n_item + z, (u + by_user) % n_user * n_item + item_map(z))
        for u in range(n_user)
        for z in range(n_item)
    ]
    return lax.ppermute(array, ("user", "item"), pairs)


def dot(a, b, ca, cb):
    return lax.dot_general(a, b, (((ca,), (cb,)), ((), ())), preferred_element_type=F32)


def body(users, user_accum, items, item_accum, ratings, tile_mask):
    strata, block_users, cols = ratings.shape
    rows, rank = users.shape
    n = lax.axis_size("item")
    z = lax.axis_index("item")
    group = n // 2
    side = block_users // tile_mask.shape[1]
    other = z ^ 1

    def shard(array, first, k):
        return lax.dynamic_slice_in_dim(array, lax.rem(first + 2 * k, n) * rows, rows, 0)

    wide = jnp.repeat(tile_mask, side, axis=2).astype(BF).reshape(-1, cols)
    first_items = items.astype(BF)
    both = move(jnp.concatenate((first_items, wide)), 0, lambda i: i ^ 1)
    mine_wide = wide.reshape(strata, -1, cols)
    other_wide = both[cols:].reshape(strata, -1, cols)

    def observed(masks, first, k):
        return shard(jnp.repeat(masks, side, axis=0), first, k)

    rates, seen = [], []
    for s in range(strata):
        sent = [shard(ratings[s], other, k).astype(BF) for k in range(group)]
        got = [move(t, 0, lambda i: i ^ 1) for t in sent]
        rates.append([
            jnp.concatenate((shard(ratings[s], z, k).astype(BF), got[k]), axis=1)
            for k in range(group)
        ])
        seen.append([
            jnp.concatenate((observed(mine_wide[s], z, k), observed(other_wide[s], z, k)), axis=1)
            for k in range(group)
        ])

    for s in range(strata):
        users_bf = users.astype(BF)
        shards = [users_bf] + [
            move(users_bf, 0, lambda i, k=k: (i - 2 * k) % n) for k in range(1, group)
        ]
        if s == 0:
            pair = jnp.concatenate((first_items, both[:cols]))
        else:
            items_bf = items.astype(BF)
            pair = jnp.concatenate(
                (move(items_bf, s, lambda i: i), move(items_bf, s, lambda i: i ^ 1))
            )
        user_grad = 0.1 * users
        item_part = 0.0
        for k in reversed(range(group)):
            logits = dot(shards[k], pair, 1, 1)
            errors = (
                seen[s][k].astype(F32) * (jax.nn.sigmoid(logits) - rates[s][k].astype(F32))
            ).astype(BF)
            part = dot(errors, pair, 1, 0)
            if k:
                part = move(part.astype(BF), 0, lambda i: (i + 2 * k) % n).astype(F32)
            user_grad = user_grad + part
            item_part = item_part + dot(errors, shards[k], 0, 0)
        near, far = item_part[:cols], item_part[cols:].astype(BF)
        if s:
            near = move(near.astype(BF), -s, lambda i: i).astype(F32)
        far = move(far, -s, lambda i: i ^ 1).astype(F32)
        item_grad = near + far + 0.1 * items
        users, user_accum = adagrad(users, user_accum, user_grad)
        items, item_accum = adagrad(items, item_accum, item_grad)
    return (users, items)


def solution(mesh):
    rows = P(("user", "item"), None)
    blocks = P(None, "user", "item")
    return jax.shard_map(
        body,
        mesh=mesh,
        in_specs=(rows, rows, rows, rows, blocks, blocks),
        out_specs=(rows, rows),
        check_vma=False,
    )
```

time: 113 us -> 53.8 us (0.48)
  waiting for transfers between devices: 53 us -> 17.2 us
  blocking collectives: 33.4 us -> 0 us
  starting transfers between devices: 0.2 us -> 20.5 us
  between operations: 14.2 us -> 1.06 us
  matrix products: 5.62 us -> 9.01 us
  other arithmetic: 4.96 us -> 2.06 us
  local copies, waits for them, and re-layouts: 1.59 us -> 3.72 us
    reduce_scatter x2 -> x0, waiting for transfers between devices: 46.3 us -> none  [body(): lax.psum_scatter(user_part, 'item', scatter_dimension=0, tiled=True)]
    all_gather x2 -> x0, blocking collectives: 33.4 us -> none  [body(): lax.all_gather(users.astype(jnp.bfloat16), 'item', axis=0, tiled=True)]
    ppermute x2 -> x14, starting transfers between devices: 0.12 us -> 20.5 us  [the longest x10 17.8 us: move(): lax.ppermute(array, 'item', [(z, item_map(z)) for z in range(n_item)])]
    ppermute x2 -> x14, waiting for transfers between devices: 6.69 us -> 17.2 us  [the longest x10 11.4 us: move(): lax.ppermute(array, 'item', [(z, item_map(z)) for z in range(n_item)])]
    dot_general x6 -> x12, matrix products: 5.62 us -> 9.01 us  [dot(): lax.dot_general(a, b, (((ca,), (cb,)), ((), ())), preferred_element_type=...]
    convert_element_type x3 -> x9, other arithmetic: 2.95 us -> 1.01 us  [the longest x2 0.69 us: body(): sent = [shard(ratings[s], other, k).astype(BF) for k in range(group)]]
    slice x0 -> x7, local copies, waits for them, and re-layouts: none -> 1.86 us  [the longest x1 1.68 us: body(): ratings[s]]
  transfers between devices with their start and end apart: 4 -> 14, of which waited for: 3 -> 9; matrix products, arithmetic and copies ran while one was open for 3% -> 19% of each run, Pallas kernels for 0% -> 0%
where the time goes in v1:
time: 53.8 us; the launch traced here: 53.5 us
  starting transfers between devices  20.5 us (38%)
  waiting for transfers between devices  17.2 us (32%)
  matrix products  9.01 us (17%)
  local copies, waits for them, and re-layouts  3.72 us (7%)
  other arithmetic  2.06 us (4%)
  between operations  1.06 us (2%)
    ppermute x10, starting transfers between devices, move(): lax.ppermute(array, 'item', [(z, item_map(z)) for z in range(n_item)])  17.8 us
    ppermute x10, waiting for transfers between devices, move(): lax.ppermute(array, 'item', [(z, item_map(z)) for z in range(n_item)])  11.4 us
    dot_general x12, matrix products, dot(): lax.dot_general(a, b, (((ca,), (cb,)), ((), ())), preferred_element_type=...  9.01 us
    ppermute x4, waiting for transfers between devices, move(): return lax.ppermute(array, ('user', 'item'), pairs)  5.81 us
    ppermute x4, starting transfers between devices, move(): return lax.ppermute(array, ('user', 'item'), pairs)  2.71 us
    slice x1, local copies, waits for them, and re-layouts, body(): ratings[s]  1.68 us
  transfers between devices with their start and end apart: 14, of which 9 were waited for; matrix products, arithmetic and copies ran while one was open for 19% of the time, Pallas kernels for 0%

profile of v1, /device:TPU:0, one launch (start us, length us, event | category | flops | bytes accessed | tf_op | source)
XLA Modules:
  0.0 53.5 jit_solution(13540977601245511451)
XLA Ops:
  0.7 1.7 %fusion.35 = (s32[1,1024,256]{2,1,0:T(8,128)S(1)}, s32[1,1024,256]{2,1,0:T(8,128)S(1)}) fusion(s32[2,1024,256]{2,1,0:T(8,128)} %param.10), kind=kLoop, calls=%fused_computation.82 | loop fusion | bytes 4194304 | tf_op jit(solution)/shard_map/slice | solution.py:57
  2.4 0.1 constant_dynamic-slice_fusion.9
  2.5 0.1 copy.14
  2.7 3.1 %collective-permute-start.4 = (bf16[256,256]{0,1:T(8,128)(2,1)S(1)}, bf16[256,256]{0,1:T(8,128)(2,1)}, u32[]{:S(2)}, u32[]{:S(2)}) collective-permute-start(bf16[256,256]{0,1:T(8,128)(2,1)S(1)} %convert_bitcast_fusion), channel_id=1, source_target_pairs={{0,1},{1,0},{2,3},{3,2},{4,5},{5,4},{6,7},{7,6},{8,9},{9,8},{10,11... | collective-permute-start | bytes 393224 | tf_op jit(solution)/shard_map/ppermute | solution.py:18
  5.8 0.1 broadcast_bitcast_fusion
  5.9 0.6 %collective-permute-start = (bf16[272,256]{1,0:T(8,128)(2,1)S(1)}, bf16[272,256]{1,0:T(8,128)(2,1)S(1)}, u32[]{:S(2)}, u32[]{:S(2)}) collective-permute-start(bf16[272,256]{1,0:T(8,128)(2,1)S(1)} %pad_maximum_fusion.1), channel_id=1, source_target_pairs={{0,1},{1,0},{2,3},{3,2},{4,5},{5,4},{6,7},{7,6},{8,9},{9,8},{10,11... | collective-permute-start | bytes 417800 | tf_op jit(solution)/shard_map/ppermute | solution.py:18
  6.5 0.1 copy.12
  6.7 0.7 %convert_bitcast_fusion.2 = bf16[256,256]{0,1:T(8,128)(2,1)} fusion(s32[1,256,256]{1,2,0:T(8,128)S(1)} %copy.12), kind=kLoop, calls=%fused_computation.59 | loop fusion | flops 65536 | bytes 393216 | tf_op jit(solution)/shard_map/convert_element_type | solution.py:54
  7.4 1.5 %collective-permute-start.2 = (bf16[256,256]{0,1:T(8,128)(2,1)}, bf16[256,256]{0,1:T(8,128)(2,1)}, u32[]{:S(2)}, u32[]{:S(2)}) collective-permute-start(bf16[256,256]{0,1:T(8,128)(2,1)} %convert_bitcast_fusion.2), channel_id=1, source_target_pairs={{0,1},{1,0},{2,3},{3,2},{4,5},{5,4},{6,7},{7,6},{8,9},{9,8},{10,11... | collective-permute-start | bytes 393224 | tf_op jit(solution)/shard_map/ppermute | solution.py:18
  8.8 2.7 %collective-permute-start.1 = (bf16[256,256]{1,0:T(8,128)(2,1)S(1)}, bf16[256,256]{1,0:T(8,128)(2,1)}, u32[]{:S(2)}, u32[]{:S(2)}) collective-permute-start(bf16[256,256]{1,0:T(8,128)(2,1)S(1)} %convert_element_type.134), channel_id=1, source_target_pairs={{0,2},{1,3},{2,0},{3,1},{4,6},{5,7},{6,4},{7,5},{8,10},{9,11},{10,... | collective-permute-start | bytes 393224 | tf_op jit(solution)/shard_map/ppermute | solution.py:18
  11.5 0.1 fusion.28
  11.6 0.6 %collective-permute-start.11 = (bf16[256,256]{1,0:T(8,128)(2,1)S(1)}, bf16[256,256]{1,0:T(8,128)(2,1)}, u32[]{:S(2)}, u32[]{:S(2)}) collective-permute-start(bf16[256,256]{1,0:T(8,128)(2,1)S(1)} %get-tuple-element.5), channel_id=1, source_target_pairs={{0,1},{1,0},{2,3},{3,2},{4,5},{5,4},{6,7},{7,6},{8,9},{9,8},{10,11... | collective-permute-start | bytes 393224 | tf_op jit(solution)/shard_map/ppermute | solution.py:18
  12.2 0.1 copy.13
  12.4 0.1 copy.11
  12.6 0.3 broadcast_in_dim.24
  13.0 0.1 copy.20
  13.1 2.8 %collective-permute-done = bf16[272,256]{1,0:T(8,128)(2,1)S(1)} collective-permute-done((bf16[272,256]{1,0:T(8,128)(2,1)S(1)}, bf16[272,256]{1,0:T(8,128)(2,1)S(1)}, u32[]{:S(2)}, u32[]{:S(2)}) %collective-permute-start) | collective-permute-done | bytes 139296 | tf_op jit(solution)/shard_map/ppermute | solution.py:18
  15.9 0.1 copy.8
  16.1 0.3 broadcast_in_dim.26
  16.4 0.1 copy.19
  16.6 1.3 %fusion.24 = bf16[256,512]{0,1:T(8,128)(2,1)S(1)} fusion(bf16[256,256]{1,0:T(8,128)(2,1)S(1)} %convert_element_type.134, bf16[256,256]{0,1:T(8,128)(2,1)S(1)} %get-tuple-element.19, bf16[256,256]{0,1:T(8,128)(2,1)S(1)} %get-tuple-element.17, bf16[256,256]{0,1:T(8,128)(2,1)} %collective-permute-done.4, bf16[256,256]{0,1:T(8,128)(2,1)S(1)} %convert_bitcast_fusion.1, ...), kind=kOutput, calls=%fused_computation.30 | convolution fusion | flops 69468160 | bytes 1179648 | tf_op jit(solution)/shard_map/dot_general | solution.py:28
  17.8 0.2 fusion.38
  18.1 0.8 %collective-permute-done.2 = bf16[256,256]{0,1:T(8,128)(2,1)} collective-permute-done((bf16[256,256]{0,1:T(8,128)(2,1)}, bf16[256,256]{0,1:T(8,128)(2,1)}, u32[]{:S(2)}, u32[]{:S(2)}) %collective-permute-start.2) | collective-permute-done | bytes 131104 | tf_op jit(solution)/shard_map/ppermute | solution.py:18
  18.8 1.3 %fusion.25 = bf16[256,512]{0,1:T(8,128)(2,1)S(1)} fusion(bf16[256,256]{1,0:T(8,128)(2,1)} %collective-permute-done.1, bf16[256,256]{0,1:T(8,128)(2,1)S(1)} %get-tuple-element.18, bf16[256,256]{0,1:T(8,128)(2,1)S(1)} %get-tuple-element.16, bf16[256,256]{0,1:T(8,128)(2,1)} %collective-permute-done.2, bf16[256,256]{0,1:T(8,128)(2,1)S(1)} %convert_bitcast_fusion.3, ...), kind=kOutput, calls=%fused_computation.31 | convolution fusion | flops 69468160 | bytes 1179648 | tf_op jit(solution)/shard_map/dot_general | solution.py:28
  20.2 1.2 %convolution_add_fusion.1 = f32[512,256]{1,0:T(8,128)S(1)} fusion(f32[512,256]{1,0:T(8,128)S(1)} %fusion.38, bf16[256,512]{0,1:T(8,128)(2,1)S(1)} %fusion.25, bf16[256,256]{1,0:T(8,128)(2,1)} %collective-permute-done.1), kind=kOutput, calls=%fused_computation.27 | convolution fusion | flops 67239936 | bytes 1441792 | tf_op jit(solution)/shard_map/dot_general | solution.py:28
  21.4 3.1 %collective-permute-start.6 = (bf16[256,256]{1,0:T(8,128)(2,1)S(1)}, bf16[256,256]{1,0:T(8,128)(2,1)S(1)}, u32[]{:S(2)}, u32[]{:S(2)}) collective-permute-start(bf16[256,256]{1,0:T(8,128)(2,1)S(1)} %slice.99), channel_id=1, source_target_pairs={{0,1},{1,0},{2,3},{3,2},{4,5},{5,4},{6,7},{7,6},{8,9},{9,8},{10,11... | collective-permute-start | bytes 393224 | tf_op jit(solution)/shard_map/ppermute | solution.py:18
  24.5 0.3 convolution_convert_fusion.1
  24.8 1.6 %collective-permute-start.3 = (bf16[256,256]{1,0:T(8,128)(2,1)S(1)}, bf16[256,256]{1,0:T(8,128)(2,1)S(1)}, u32[]{:S(2)}, u32[]{:S(2)}) collective-permute-start(bf16[256,256]{1,0:T(8,128)(2,1)S(1)} %convolution_convert_fusion.1), channel_id=1, source_target_pairs={{0,2},{1,3},{2,0},{3,1},{4,6},{5,7},{6,4},{7,5},{8,10},{9,11},{10,... | collective-permute-start | bytes 393224 | tf_op jit(solution)/shard_map/ppermute | solution.py:18
  26.6 2.2 %collective-permute-done.6 = bf16[256,256]{1,0:T(8,128)(2,1)S(1)} collective-permute-done((bf16[256,256]{1,0:T(8,128)(2,1)S(1)}, bf16[256,256]{1,0:T(8,128)(2,1)S(1)}, u32[]{:S(2)}, u32[]{:S(2)}) %collective-permute-start.6) | collective-permute-done | bytes 131104 | tf_op jit(solution)/shard_map/ppermute | solution.py:18
  28.7 0.2 fusion.34
  29.0 2.0 %collective-permute-start.8 = (bf16[256,256]{1,0:T(8,128)(2,1)S(1)}, bf16[256,256]{1,0:T(8,128)(2,1)S(1)}, u32[]{:S(2)}, u32[]{:S(2)}) collective-permute-start(bf16[256,256]{1,0:T(8,128)(2,1)S(1)} %fusion.34), channel_id=1, source_target_pairs={{0,5},{1,4},{2,7},{3,6},{4,9},{5,8},{6,11},{7,10},{8,13},{9,12},{1... | collective-permute-start | bytes 393224 | tf_op jit(solution)/shard_map/ppermute | solution.py:24
  30.9 1.2 %collective-permute-done.3 = bf16[256,256]{1,0:T(8,128)(2,1)S(1)} collective-permute-done((bf16[256,256]{1,0:T(8,128)(2,1)S(1)}, bf16[256,256]{1,0:T(8,128)(2,1)S(1)}, u32[]{:S(2)}, u32[]{:S(2)}) %collective-permute-start.3) | collective-permute-done | bytes 131104 | tf_op jit(solution)/shard_map/ppermute | solution.py:18
  32.1 0.4 fusion.32
  32.5 1.4 %collective-permute-start.5 = (bf16[256,256]{1,0:T(8,128)(2,1)S(1)}, bf16[256,256]{1,0:T(8,128)(2,1)S(1)}, u32[]{:S(2)}, u32[]{:S(2)}) collective-permute-start(bf16[256,256]{1,0:T(8,128)(2,1)S(1)} %get-tuple-element.26), channel_id=1, source_target_pairs={{0,2},{1,3},{2,0},{3,1},{4,6},{5,7},{6,4},{7,5},{8,10},{9,11},{10,... | collective-permute-start | bytes 393224 | tf_op jit(solution)/shard_map/ppermute | solution.py:18
  33.9 1.2 %collective-permute-done.7 = bf16[256,256]{1,0:T(8,128)(2,1)S(1)} collective-permute-done((bf16[256,256]{1,0:T(8,128)(2,1)S(1)}, bf16[256,256]{1,0:T(8,128)(2,1)S(1)}, u32[]{:S(2)}, u32[]{:S(2)}) %collective-permute-start.7) | collective-permute-done | bytes 131104 | tf_op jit(solution)/shard_map/ppermute | solution.py:24
  35.1 2.5 %collective-permute-done.8 = bf16[256,256]{1,0:T(8,128)(2,1)S(1)} collective-permute-done((bf16[256,256]{1,0:T(8,128)(2,1)S(1)}, bf16[256,256]{1,0:T(8,128)(2,1)S(1)}, u32[]{:S(2)}, u32[]{:S(2)}) %collective-permute-start.8) | collective-permute-done | bytes 131104 | tf_op jit(solution)/shard_map/ppermute | solution.py:24
  37.6 1.3 %fusion.22 = bf16[256,512]{1,0:T(8,128)(2,1)S(1)} fusion(bf16[256,256]{1,0:T(8,128)(2,1)S(1)} %get-tuple-element.26, bf16[512,256]{1,0:T(8,128)(2,1)S(1)} %constant_dynamic-update-slice_fusion, bf16[256,256]{1,0:T(8,128)(2,1)S(1)} %get-tuple-element.15, bf16[256,256]{1,0:T(8,128)(2,1)S(1)} %get-tuple-element.28, ...), kind=kOutput, calls=%fused_computation.28 | convolution fusion | flops 68943872 | bytes 1179648 | tf_op jit(solution)/shard_map/dot_general | solution.py:28
  38.9 0.3 fusion.39
  39.2 1.7 %collective-permute-done.5 = bf16[256,256]{1,0:T(8,128)(2,1)S(1)} collective-permute-done((bf16[256,256]{1,0:T(8,128)(2,1)S(1)}, bf16[256,256]{1,0:T(8,128)(2,1)S(1)}, u32[]{:S(2)}, u32[]{:S(2)}) %collective-permute-start.5) | collective-permute-done | bytes 131104 | tf_op jit(solution)/shard_map/ppermute | solution.py:18
  40.8 1.3 %fusion.23 = bf16[256,512]{1,0:T(8,128)(2,1)S(1)} fusion(bf16[256,256]{1,0:T(8,128)(2,1)S(1)} %collective-permute-done.5, bf16[512,256]{1,0:T(8,128)(2,1)S(1)} %constant_dynamic-update-slice_fusion, bf16[256,256]{1,0:T(8,128)(2,1)S(1)} %get-tuple-element.14, bf16[256,256]{1,0:T(8,128)(2,1)S(1)} %get-tuple-element.29, ...), kind=kOutput, calls=%fused_computation.29 | convolution fusion | flops 68943872 | bytes 1179648 | tf_op jit(solution)/shard_map/dot_general | solution.py:28
  42.1 0.3 fusion.26
  42.4 0.6 %collective-permute-start.13 = (bf16[256,256]{1,0:T(8,128)(2,1)S(1)}, bf16[256,256]{1,0:T(8,128)(2,1)S(1)}, u32[]{:S(2)}, u32[]{:S(2)}) collective-permute-start(bf16[256,256]{1,0:T(8,128)(2,1)S(1)} %get-tuple-element.21), channel_id=1, source_target_pairs={{0,29},{1,28},{2,31},{3,30},{4,1},{5,0},{6,3},{7,2},{8,5},{9,4},{1... | collective-permute-start | bytes 393224 | tf_op jit(solution)/shard_map/ppermute | solution.py:24
  43.1 0.2 convolution_convert_fusion
  43.3 3.1 %collective-permute-start.10 = (bf16[256,256]{1,0:T(8,128)(2,1)S(1)}, bf16[256,256]{1,0:T(8,128)(2,1)S(1)}, u32[]{:S(2)}, u32[]{:S(2)}) collective-permute-start(bf16[256,256]{1,0:T(8,128)(2,1)S(1)} %convolution_convert_fusion), channel_id=1, source_target_pairs={{0,2},{1,3},{2,0},{3,1},{4,6},{5,7},{6,4},{7,5},{8,10},{9,11},{10,... | collective-permute-start | bytes 393224 | tf_op jit(solution)/shard_map/ppermute | solution.py:18
  46.4 2.2 %collective-permute-done.13 = bf16[256,256]{1,0:T(8,128)(2,1)S(1)} collective-permute-done((bf16[256,256]{1,0:T(8,128)(2,1)S(1)}, bf16[256,256]{1,0:T(8,128)(2,1)S(1)}, u32[]{:S(2)}, u32[]{:S(2)}) %collective-permute-start.13) | collective-permute-done | bytes 131104 | tf_op jit(solution)/shard_map/ppermute | solution.py:24
  48.5 1.0 %divide_subtract_fusion = f32[256,256]{1,0:T(8,128)} fusion(bf16[256,256]{1,0:T(8,128)(2,1)S(1)} %collective-permute-done.13, bf16[256,256]{1,0:T(8,128)(2,1)S(1)} %collective-permute-done.12, f32[256,256]{1,0:T(8,128)S(1)} %copy-done.1, f32[256,256]{1,0:T(8,128)S(1)} %copy-done, bf16[256,256]{1,0:T(8,128)(2,1)S(1)} %collective-permute-done.6, ...), kind=kLoop, calls=%fused_computation.41 | loop fusion | flops 1376256 | bytes 1441792 | tf_op jit(solution)/shard_map/sub | solution.py:12
  49.6 2.8 %collective-permute-done.10 = bf16[256,256]{1,0:T(8,128)(2,1)S(1)} collective-permute-done((bf16[256,256]{1,0:T(8,128)(2,1)S(1)}, bf16[256,256]{1,0:T(8,128)(2,1)S(1)}, u32[]{:S(2)}, u32[]{:S(2)}) %collective-permute-start.10) | collective-permute-done | bytes 131104 | tf_op jit(solution)/shard_map/ppermute | solution.py:18
  52.4 1.1 %divide_subtract_fusion.1 = f32[256,256]{1,0:T(8,128)} fusion(bf16[256,256]{1,0:T(8,128)(2,1)S(1)} %collective-permute-done.10, f32[256,256]{1,0:T(8,128)S(1)} %copy-done.4, f32[256,256]{1,0:T(8,128)S(1)} %get-tuple-element.27, bf16[256,256]{1,0:T(8,128)(2,1)S(1)} %collective-permute-done.3, f32[256,256]{1,0:T(8,128)S(1)} %copy-done.2, ...), kind=kOutput, calls=%fused_computation.42 | convolution fusion | flops 68419584 | bytes 1835008 | tf_op jit(solution)/shard_map/dot_general | solution.py:28
  (39 shorter events, 0.6 us)
Async XLA Ops:
  2.3 3.4 %copy-start = (f32[256,256]{1,0:T(8,128)S(1)}, f32[256,256]{1,0:T(8,128)}, u32[]{:S(2)}) copy-start(f32[256,256]{1,0:T(8,128)} %param.8) | copy-start | bytes 786436
  2.4 3.5 %copy-start.3 = (s32[2,8,2]{1,2,0:T(2,128)S(1)}, s32[2,8,2]{1,2,0:T(2,128)}, u32[]{:S(2)}) copy-start(s32[2,8,2]{1,2,0:T(2,128)} %param.11) | copy-start | bytes 388
  2.5 6.3 %copy-start.2 = (f32[256,256]{1,0:T(8,128)S(1)}, f32[256,256]{1,0:T(8,128)}, u32[]{:S(2)}) copy-start(f32[256,256]{1,0:T(8,128)} %param.6) | copy-start | bytes 786436
  2.7 13.9 %collective-permute-start.4 = (bf16[256,256]{0,1:T(8,128)(2,1)S(1)}, bf16[256,256]{0,1:T(8,128)(2,1)}, u32[]{:S(2)}, u32[]{:S(2)}) collective-permute-start(bf16[256,256]{0,1:T(8,128)(2,1)S(1)} %convert_bitcast_fusion), channel_id=1, source_target_pairs={{0,1},{1,0},{2,3},{3,2},{4,5},{5,4},{6,7},{7,6},{8,9},{9,8},{10,11... | collective-permute-start | bytes 393224 | tf_op jit(solution)/shard_map/ppermute | solution.py:18
  5.9 10.0 %collective-permute-start = (bf16[272,256]{1,0:T(8,128)(2,1)S(1)}, bf16[272,256]{1,0:T(8,128)(2,1)S(1)}, u32[]{:S(2)}, u32[]{:S(2)}) collective-permute-start(bf16[272,256]{1,0:T(8,128)(2,1)S(1)} %pad_maximum_fusion.1), channel_id=1, source_target_pairs={{0,1},{1,0},{2,3},{3,2},{4,5},{5,4},{6,7},{7,6},{8,9},{9,8},{10,11... | collective-permute-start | bytes 417800 | tf_op jit(solution)/shard_map/ppermute | solution.py:18
  7.4 11.5 %collective-permute-start.2 = (bf16[256,256]{0,1:T(8,128)(2,1)}, bf16[256,256]{0,1:T(8,128)(2,1)}, u32[]{:S(2)}, u32[]{:S(2)}) collective-permute-start(bf16[256,256]{0,1:T(8,128)(2,1)} %convert_bitcast_fusion.2), channel_id=1, source_target_pairs={{0,1},{1,0},{2,3},{3,2},{4,5},{5,4},{6,7},{7,6},{8,9},{9,8},{10,11... | collective-permute-start | bytes 393224 | tf_op jit(solution)/shard_map/ppermute | solution.py:18
  8.8 10.0 %collective-permute-start.1 = (bf16[256,256]{1,0:T(8,128)(2,1)S(1)}, bf16[256,256]{1,0:T(8,128)(2,1)}, u32[]{:S(2)}, u32[]{:S(2)}) collective-permute-start(bf16[256,256]{1,0:T(8,128)(2,1)S(1)} %convert_element_type.134), channel_id=1, source_target_pairs={{0,2},{1,3},{2,0},{3,1},{4,6},{5,7},{6,4},{7,5},{8,10},{9,11},{10,... | collective-permute-start | bytes 393224 | tf_op jit(solution)/shard_map/ppermute | solution.py:18
  11.6 26.0 %collective-permute-start.11 = (bf16[256,256]{1,0:T(8,128)(2,1)S(1)}, bf16[256,256]{1,0:T(8,128)(2,1)}, u32[]{:S(2)}, u32[]{:S(2)}) collective-permute-start(bf16[256,256]{1,0:T(8,128)(2,1)S(1)} %get-tuple-element.5), channel_id=1, source_target_pairs={{0,1},{1,0},{2,3},{3,2},{4,5},{5,4},{6,7},{7,6},{8,9},{9,8},{10,11... | collective-permute-start | bytes 393224 | tf_op jit(solution)/shard_map/ppermute | solution.py:18
  15.9 23.2 %collective-permute-start.9 = (bf16[256,256]{1,0:T(8,128)(2,1)S(1)}, bf16[256,256]{1,0:T(8,128)(2,1)}, u32[]{:S(2)}, u32[]{:S(2)}) collective-permute-start(bf16[256,256]{1,0:T(8,128)(2,1)S(1)} %get-tuple-element.7), channel_id=1, source_target_pairs={{0,1},{1,0},{2,3},{3,2},{4,5},{5,4},{6,7},{7,6},{8,9},{9,8},{10,11... | collective-permute-start | bytes 393224 | tf_op jit(solution)/shard_map/ppermute | solution.py:18
  20.2 8.5 %copy-start.1 = (f32[256,256]{1,0:T(8,128)S(1)}, f32[256,256]{1,0:T(8,128)}, u32[]{:S(2)}) copy-start(f32[256,256]{1,0:T(8,128)} %param.9) | copy-start | bytes 786436
  21.4 10.8 %copy-start.4 = (f32[256,256]{1,0:T(8,128)S(1)}, f32[256,256]{1,0:T(8,128)}, u32[]{:S(2)}) copy-start(f32[256,256]{1,0:T(8,128)} %param.7) | copy-start | bytes 786436
  21.4 7.3 %collective-permute-start.6 = (bf16[256,256]{1,0:T(8,128)(2,1)S(1)}, bf16[256,256]{1,0:T(8,128)(2,1)S(1)}, u32[]{:S(2)}, u32[]{:S(2)}) collective-permute-start(bf16[256,256]{1,0:T(8,128)(2,1)S(1)} %slice.99), channel_id=1, source_target_pairs={{0,1},{1,0},{2,3},{3,2},{4,5},{5,4},{6,7},{7,6},{8,9},{9,8},{10,11... | collective-permute-start | bytes 393224 | tf_op jit(solution)/shard_map/ppermute | solution.py:18
  24.8 7.3 %collective-permute-start.3 = (bf16[256,256]{1,0:T(8,128)(2,1)S(1)}, bf16[256,256]{1,0:T(8,128)(2,1)S(1)}, u32[]{:S(2)}, u32[]{:S(2)}) collective-permute-start(bf16[256,256]{1,0:T(8,128)(2,1)S(1)} %convolution_convert_fusion.1), channel_id=1, source_target_pairs={{0,2},{1,3},{2,0},{3,1},{4,6},{5,7},{6,4},{7,5},{8,10},{9,11},{10,... | collective-permute-start | bytes 393224 | tf_op jit(solution)/shard_map/ppermute | solution.py:18
  28.9 6.2 %collective-permute-start.7 = (bf16[256,256]{1,0:T(8,128)(2,1)S(1)}, bf16[256,256]{1,0:T(8,128)(2,1)S(1)}, u32[]{:S(2)}, u32[]{:S(2)}) collective-permute-start(bf16[256,256]{1,0:T(8,128)(2,1)S(1)} %fusion.34), channel_id=1, source_target_pairs={{0,4},{1,5},{2,6},{3,7},{4,8},{5,9},{6,10},{7,11},{8,12},{9,13},{1... | collective-permute-start | bytes 393224 | tf_op jit(solution)/shard_map/ppermute | solution.py:24
  29.0 8.6 %collective-permute-start.8 = (bf16[256,256]{1,0:T(8,128)(2,1)S(1)}, bf16[256,256]{1,0:T(8,128)(2,1)S(1)}, u32[]{:S(2)}, u32[]{:S(2)}) collective-permute-start(bf16[256,256]{1,0:T(8,128)(2,1)S(1)} %fusion.34), channel_id=1, source_target_pairs={{0,5},{1,4},{2,7},{3,6},{4,9},{5,8},{6,11},{7,10},{8,13},{9,12},{1... | collective-permute-start | bytes 393224 | tf_op jit(solution)/shard_map/ppermute | solution.py:24
  32.5 8.3 %collective-permute-start.5 = (bf16[256,256]{1,0:T(8,128)(2,1)S(1)}, bf16[256,256]{1,0:T(8,128)(2,1)S(1)}, u32[]{:S(2)}, u32[]{:S(2)}) collective-permute-start(bf16[256,256]{1,0:T(8,128)(2,1)S(1)} %get-tuple-element.26), channel_id=1, source_target_pairs={{0,2},{1,3},{2,0},{3,1},{4,6},{5,7},{6,4},{7,5},{8,10},{9,11},{10,... | collective-permute-start | bytes 393224 | tf_op jit(solution)/shard_map/ppermute | solution.py:18
  42.4 4.0 %collective-permute-start.12 = (bf16[256,256]{1,0:T(8,128)(2,1)S(1)}, bf16[256,256]{1,0:T(8,128)(2,1)S(1)}, u32[]{:S(2)}, u32[]{:S(2)}) collective-permute-start(bf16[256,256]{1,0:T(8,128)(2,1)S(1)} %get-tuple-element.20), channel_id=1, source_target_pairs={{0,28},{1,29},{2,30},{3,31},{4,0},{5,1},{6,2},{7,3},{8,4},{9,5},{1... | collective-permute-start | bytes 393224 | tf_op jit(solution)/shard_map/ppermute | solution.py:24
  42.4 6.1 %collective-permute-start.13 = (bf16[256,256]{1,0:T(8,128)(2,1)S(1)}, bf16[256,256]{1,0:T(8,128)(2,1)S(1)}, u32[]{:S(2)}, u32[]{:S(2)}) collective-permute-start(bf16[256,256]{1,0:T(8,128)(2,1)S(1)} %get-tuple-element.21), channel_id=1, source_target_pairs={{0,29},{1,28},{2,31},{3,30},{4,1},{5,0},{6,3},{7,2},{8,5},{9,4},{1... | collective-permute-start | bytes 393224 | tf_op jit(solution)/shard_map/ppermute | solution.py:24
  43.3 9.1 %collective-permute-start.10 = (bf16[256,256]{1,0:T(8,128)(2,1)S(1)}, bf16[256,256]{1,0:T(8,128)(2,1)S(1)}, u32[]{:S(2)}, u32[]{:S(2)}) collective-permute-start(bf16[256,256]{1,0:T(8,128)(2,1)S(1)} %convolution_convert_fusion), channel_id=1, source_target_pairs={{0,2},{1,3},{2,0},{3,1},{4,6},{5,7},{6,4},{7,5},{8,10},{9,11},{10,... | collective-permute-start | bytes 393224 | tf_op jit(solution)/shard_map/ppermute | solution.py:18

commit v2 on v1

v2 whole, which is shorter than its diff:
```python
import functools

import jax
import jax.numpy as jnp
from jax import lax
from jax.experimental import pallas as pl
from jax.experimental.pallas import tpu as pltpu
from jax.sharding import PartitionSpec as P


BF = jnp.bfloat16
F32 = jnp.float32
FIRST_PARAMS = pltpu.CompilerParams(vmem_limit_bytes=16<<20)
REST_PARAMS = pltpu.CompilerParams(vmem_limit_bytes=16 << 20)


def adagrad(param, accum, grad):
    accum = accum + grad * grad
    return (param - 0.25 * grad / (jnp.sqrt(accum) + 1e-06), accum)


def move(array, by_user, item_map):
    n_user, n_item = lax.axis_size("user"), lax.axis_size("item")
    if by_user == 0:
        return lax.ppermute(array, "item", [(z, item_map(z)) for z in range(n_item)])
    pairs = [
        (u * n_item + z, (u + by_user) % n_user * n_item + item_map(z))
        for u in range(n_user)
        for z in range(n_item)
    ]
    return lax.ppermute(array, ("user", "item"), pairs)


def dot(a, b, ca, cb):
    return lax.dot_general(a, b, (((ca,), (cb,)), ((), ())), preferred_element_type=F32)


def shard_kernel(k, first_tile, side, carried, *refs):
    if carried:
        u, near, far, rate_near, rate_far, seen_near, seen_far, near_in, far_in = refs[:9]
    else:
        u, near, far, rate_near, rate_far, seen_near, seen_far = refs[:7]
    part, near_out, far_out = refs[-3:]
    rows = u.shape[0]
    shard = lax.rem(lax.axis_index("item") + 2 * k, lax.axis_size("item"))
    chunk = min(rows, side)

    def errors(items, rates, seen):
        tiles, cols = seen.shape
        masks = seen[...].astype(F32)
        at = lax.broadcasted_iota(jnp.int32, (tiles, cols), 0)
        bands = []
        for t in range(0, rows, chunk):
            tile = first_tile + (shard * rows + t) // side
            row = jnp.sum(jnp.where(at == tile, masks, 0.0), axis=0, keepdims=True)
            bands.append(jnp.broadcast_to(row, (chunk, cols)))
        observed = jnp.concatenate(bands, axis=0) if len(bands) > 1 else bands[0]
        logits = dot(u[...], items[...], 1, 1)
        return (observed * (jax.nn.sigmoid(logits) - rates[...].astype(F32))).astype(BF)

    e_near = errors(near, rate_near, seen_near)
    e_far = errors(far, rate_far, seen_far)
    part[...] = (dot(e_near, near[...], 1, 0) + dot(e_far, far[...], 1, 0)).astype(part.dtype)
    g_near = dot(e_near, u[...], 0, 0)
    g_far = dot(e_far, u[...], 0, 0)
    if carried:
        g_near = g_near + near_in[...]
        g_far = g_far + far_in[...]
    near_out[...] = g_near.astype(near_out.dtype)
    far_out[...] = g_far.astype(far_out.dtype)


def shard_grads(k, first_tile, side, part_type, item_types, args, carry):
    u, near = args[0], args[1]
    rows, rank = u.shape
    cols = near.shape[0]
    spec = pl.BlockSpec(memory_space=pltpu.VMEM)
    operands = args + carry
    return pl.pallas_call(
        functools.partial(shard_kernel, k, first_tile, side, bool(carry)),
        out_shape=(
            jax.ShapeDtypeStruct((rows, rank), part_type),
            jax.ShapeDtypeStruct((cols, rank), item_types[0]),
            jax.ShapeDtypeStruct((cols, rank), item_types[1]),
        ),
        in_specs=[spec] * len(operands),
        out_specs=(spec,) * 3,
        compiler_params=pltpu.CompilerParams(vmem_limit_bytes=16 << 20),
        cost_estimate=pl.CostEstimate(
            flops=12 * rows * cols * rank, bytes_accessed=0, transcendentals=2 * rows * cols
        ),
        name="shard_grads",
    )(*operands)


def fetch(sources, buffers, sems):
    copies = [
        pltpu.make_async_copy(src, buf, sems.at[i])
        for i, (src, buf) in enumerate(zip(sources, buffers))
    ]
    for copy in copies:
        copy.start()
    return copies


def share(ratings, s, first, k, rows, n):
    at = pl.multiple_of(lax.rem(first + 2 * k, n) * rows, rows)
    return ratings.at[s, pl.ds(at, rows), :]


def first_kernel(group, rows, side, *refs):
    users, items, ratings, masks = refs[:4]
    users_bf, items_bf, wide = refs[4:7]
    sent = refs[7 : 7 + group]
    scratch = refs[7 + group :]
    sems = scratch[-1]
    n = lax.axis_size("item")
    other = lax.axis_index("item") ^ 1
    order = list(range(1, group)) + [0]
    sources = [items, users, masks] + [share(ratings, 0, other, k, rows, n) for k in order]
    copies = fetch(sources, scratch[:-1], sems)
    for i, out in enumerate((items_bf, users_bf)):
        copies[i].wait()
        out[...] = scratch[i][...].astype(BF)
    copies[2].wait()
    strata, across, tiles = masks.shape
    eye = lax.broadcasted_iota(jnp.int32, (tiles, tiles), 0) == lax.broadcasted_iota(
        jnp.int32, (tiles, tiles), 1
    )
    for s in range(strata):
        band = scratch[2][s].astype(F32)
        parts = []
        for c in range(across):
            spread = jnp.where(eye, jnp.broadcast_to(band[c : c + 1], (tiles, tiles)), 0.0)
            parts.append(jnp.broadcast_to(jnp.sum(spread, axis=1, keepdims=True), (tiles, side)))
        wide[pl.ds(s * tiles, tiles), :] = jnp.concatenate(parts, axis=1)
    for i, out in enumerate(sent):
        copies[3 + i].wait()
        out[pl.ds(0, rows), :] = scratch[3 + i][...].astype(F32).astype(BF)
    sent[0][pl.ds(rows, strata * tiles), :] = wide[...].astype(BF)


def first_sends(users, items, ratings, tile_mask, group, side):
    rows, _ = users.shape
    cols = ratings.shape[2]
    masks = tile_mask.transpose(0, 2, 1)
    wide = (tile_mask.shape[0] * tile_mask.shape[1], cols)
    vmem = pl.BlockSpec(memory_space=pltpu.VMEM)
    out_shape = [
        jax.ShapeDtypeStruct(users.shape, BF),
        jax.ShapeDtypeStruct(items.shape, BF),
        jax.ShapeDtypeStruct(wide, F32),
        jax.ShapeDtypeStruct((rows + wide[0], cols), BF),
    ] + [jax.ShapeDtypeStruct((rows, cols), BF)] * (group - 1)
    return pl.pallas_call(
        functools.partial(first_kernel, group, rows, side),
        out_shape=tuple(out_shape),
        in_specs=[pl.BlockSpec(memory_space=pltpu.HBM)] * 4,
        out_specs=(vmem,) * len(out_shape),
        scratch_shapes=[
            pltpu.VMEM(items.shape, F32),
            pltpu.VMEM(users.shape, F32),
            pltpu.VMEM(masks.shape, jnp.int32),
        ]
        + [pltpu.VMEM((rows, cols), jnp.int32)] * group
        + [pltpu.SemaphoreType.DMA((3 + group,))],
        compiler_params=FIRST_PARAMS,
        name="first_sends",
    )(*(pltpu.with_memory_space_constraint(a, pltpu.HBM) for a in (users, items, ratings, masks)))


def rest_kernel(picks, rows, ratings, *refs):
    outs, bufs, sems = refs[: len(picks)], refs[len(picks) : -1], refs[-1]
    n = lax.axis_size("item")
    z = lax.axis_index("item")
    copies = fetch(
        [share(ratings, s, z ^ 1 if away else z, k, rows, n) for s, k, away in picks], bufs, sems
    )
    for copy, buf, out in zip(copies, bufs, outs):
        copy.wait()
        out[...] = buf[...].astype(F32).astype(BF)


def rest_of_ratings(ratings, picks, rows):
    cols = ratings.shape[2]
    vmem = pl.BlockSpec(memory_space=pltpu.VMEM)
    return pl.pallas_call(
        functools.partial(rest_kernel, picks, rows),
        out_shape=(jax.ShapeDtypeStruct((rows, cols), BF),) * len(picks),
        in_specs=[pl.BlockSpec(memory_space=pltpu.HBM)],
        out_specs=(vmem,) * len(picks),
        scratch_shapes=[pltpu.VMEM((rows, cols), jnp.int32)] * len(picks)
        + [pltpu.SemaphoreType.DMA((len(picks),))],
        compiler_params=REST_PARAMS,
        name="rest_of_ratings",
    )(ratings)


def body(users, user_accum, items, item_accum, ratings, tile_mask):
    strata, block_users, _ = ratings.shape
    rows, _ = users.shape
    n = lax.axis_size("item")
    group = n // 2
    tiles = tile_mask.shape[1]
    side = block_users // tiles
    order = list(range(1, group)) + [0]

    first_users, first_items, wide, *sends = first_sends(
        users, items, ratings, tile_mask, group, side
    )
    shards = {0: first_users}
    for k in range(1, group):
        shards[k] = move(first_users, 0, lambda i: (i - 2 * k) % n)
    near, far = first_items, move(first_items, 0, lambda i: i ^ 1)

    picks = [(s, k, True) for s in range(1, strata) for k in order]
    picks += [(s, k, False) for s in range(strata) for k in order]
    rest = dict(zip(picks, rest_of_ratings(ratings, picks, rows)))
    rest.update({(0, k, True): t for k, t in zip(order, sends)})
    rates = {}
    for s in range(strata):
        for k in order:
            got = move(rest[s, k, True], 0, lambda i: i ^ 1)
            if s == 0 and k == order[0]:
                got, far_wide = got[:rows], got[rows:]
            rates[s, k] = (rest[s, k, False], got)

    for s in range(strata):
        if s:
            users_bf = users.astype(BF)
            shards = {0: users_bf}
            for k in range(1, group):
                shards[k] = move(users_bf, 0, lambda i: (i - 2 * k) % n)
            items_bf = items.astype(BF)
            near = move(items_bf, s, lambda i: i)
            far = move(items_bf, s, lambda i: i ^ 1)
        user_grad = 0.1 * users
        carry = ()
        turn = order
        for k in turn:
            last = k == turn[-1]
            part, g_near, g_far = shard_grads(
                k,
                s * tiles,
                side,
                BF if k else F32,
                (BF if last and s else F32, BF if last else F32),
                (shards[k], near, far, *rates[s, k], wide, far_wide),
                carry,
            )
            carry = (g_near, g_far)
            if k:
                part = move(part, 0, lambda i: (i + 2 * k) % n).astype(F32)
            user_grad = user_grad + part
        g_near, g_far = carry
        if s:
            g_near = move(g_near, -s, lambda i: i).astype(F32)
        g_far = move(g_far, -s, lambda i: i ^ 1).astype(F32)
        item_grad = g_near + g_far + 0.1 * items
        users, user_accum = adagrad(users, user_accum, user_grad)
        items, item_accum = adagrad(items, item_accum, item_grad)
    return (users, items)


def solution(mesh):
    rows = P(("user", "item"), None)
    blocks = P(None, "user", "item")

    return jax.shard_map(
        body,
        mesh=mesh,
        in_specs=(rows, rows, rows, rows, blocks, blocks),
        out_specs=(rows, rows),
        check_vma=False,
    )
```

time: 53.8 us -> 51.1 us (0.950)
  matrix products: 9.01 us -> 0 us
  waiting for transfers between devices: 17.2 us -> 21.6 us
  Pallas kernels: 0 us -> 4.02 us
  local copies, waits for them, and re-layouts: 3.72 us -> 0.04 us
  starting transfers between devices: 20.5 us -> 22.1 us
    dot_general x12 -> x0, matrix products: 9.01 us -> none  [dot(): lax.dot_general(a, b, (((ca,), (cb,)), ((), ())), preferred_element_type=...]
    ppermute x10, waiting for transfers between devices: 11.4 us -> 19.1 us  [move(): lax.ppermute(array, 'item', [(z, item_map(z)) for z in range(n_item)])]
    pallas_call x0 -> x6, Pallas kernels: none -> 4.02 us  [the longest x4 2.35 us: shard_grads(): pl.pallas_call(functools.partial(shard_kernel, k, first_tile, side, bool(...]
    ppermute x4, waiting for transfers between devices: 5.81 us -> 2.52 us  [move(): return lax.ppermute(array, ('user', 'item'), pairs)]
    slice x7 -> x2, local copies, waits for them, and re-layouts: 1.86 us -> 0.01 us  [body(): got, far_wide = (got[:rows], got[rows:])]
    ppermute x10, starting transfers between devices: 17.8 us -> 19.5 us  [move(): lax.ppermute(array, 'item', [(z, item_map(z)) for z in range(n_item)])]
    sub x1 -> x2, other arithmetic: 1.04 us -> 2.09 us  [adagrad(): return (param - 0.25 * grad / (jnp.sqrt(accum) + 1e-06), accum)]
    convert_element_type x7 -> x0, other arithmetic: 0.82 us -> none  [the longest x2 0.69 us: body(): sent = [shard(ratings[s], other, k).astype(BF) for k in range(group)]]
  transfers between devices with their start and end apart: 14 -> 14, of which waited for: 9 -> 10; matrix products, arithmetic and copies ran while one was open for 19% -> 3% of each run, Pallas kernels for 0% -> 3%
where the time goes in v2:
time: 51.1 us; the launch traced here: 51 us
  starting transfers between devices  22.1 us (43%)
  waiting for transfers between devices  21.6 us (42%)
  Pallas kernels  4.02 us (8%)
  other arithmetic  2.46 us (5%)
  between operations  0.73 us (1%)
    ppermute x10, starting transfers between devices, move(): lax.ppermute(array, 'item', [(z, item_map(z)) for z in range(n_item)])  19.5 us
    ppermute x10, waiting for transfers between devices, move(): lax.ppermute(array, 'item', [(z, item_map(z)) for z in range(n_item)])  19.1 us
    ppermute x4, starting transfers between devices, move(): return lax.ppermute(array, ('user', 'item'), pairs)  2.58 us
    ppermute x4, waiting for transfers between devices, move(): return lax.ppermute(array, ('user', 'item'), pairs)  2.52 us
    pallas_call x4, Pallas kernels, shard_grads(): pl.pallas_call(functools.partial(shard_kernel, k, first_tile, side, bool(...  2.35 us
    sub x2, other arithmetic, adagrad(): return (param - 0.25 * grad / (jnp.sqrt(accum) + 1e-06), accum)  2.09 us
    pallas_call x1, Pallas kernels, first_sends(): pl.pallas_call(functools.partial(first_kernel, group, rows, side), out_sh...  1.41 us
  transfers between devices with their start and end apart: 14, of which 10 were waited for; matrix products, arithmetic and copies ran while one was open for 3% of the time, Pallas kernels for 3%

profile of v2, /device:TPU:0, one launch (start us, length us, event | category | flops | bytes accessed | tf_op | source)
XLA Modules:
  0.0 51.0 jit_solution(1894775377419601406)
XLA Ops:
  0.6 0.0 copy-start
  0.6 1.4 %first_sends.1 = (bf16[256,256]{1,0:T(8,128)(2,1)S(1)}, bf16[256,256]{1,0:T(8,128)(2,1)S(1)}, f32[16,256]{1,0:T(8,128)S(1)}, bf16[272,256]{1,0:T(8,128)(2,1)S(1)}, bf16[256,256]{1,0:T(8,128)(2,1)S(1)}) custom-call(f32[256,256]{1,0:T(8,128)} %refs_0_.1, f32[256,256]{1,0:T(8,128)} %refs_1_.1, s32[2,1024,256]{2,1,0:T(8,128)} %ratings.1, s32[2,2,8]{2,1,0:T(2,128)} %bitcast.1), custom_call_target="tpu_custom_call" | custom-call | tf_op jit(solution)/shard_map/first_sends/pallas_call | solution.py:155
  2.1 3.1 %collective-permute-start.2 = (bf16[272,256]{1,0:T(8,128)(2,1)S(1)}, bf16[272,256]{1,0:T(8,128)(2,1)S(1)}, u32[]{:S(2)}, u32[]{:S(2)}) collective-permute-start(bf16[272,256]{1,0:T(8,128)(2,1)S(1)} %get-tuple-element.28), channel_id=1, source_target_pairs={{0,1},{1,0},{2,3},{3,2},{4,5},{5,4},{6,7},{7,6},{8,9},{9,8},{10,11... | collective-permute-start | bytes 417800 | tf_op jit(solution)/shard_map/ppermute | solution.py:25
  5.2 2.6 %collective-permute-start = (bf16[256,256]{1,0:T(8,128)(2,1)S(1)}, bf16[256,256]{1,0:T(8,128)(2,1)S(1)}, u32[]{:S(2)}, u32[]{:S(2)}) collective-permute-start(bf16[256,256]{1,0:T(8,128)(2,1)S(1)} %get-tuple-element.25.refs_0_), channel_id=1, source_target_pairs={{0,2},{1,3},{2,0},{3,1},{4,6},{5,7},{6,4},{7,5},{8,10},{9,11},{10,... | collective-permute-start | bytes 393224 | tf_op jit(solution)/shard_map/ppermute | solution.py:25
  7.8 0.4 collective-permute-start.1
  8.2 0.0 copy-start.1
  8.2 0.0 copy-start.3
  8.2 1.6 %collective-permute-start.4 = (bf16[256,256]{1,0:T(8,128)(2,1)S(1)}, bf16[256,256]{1,0:T(8,128)(2,1)S(1)}, u32[]{:S(2)}, u32[]{:S(2)}) collective-permute-start(bf16[256,256]{1,0:T(8,128)(2,1)S(1)} %get-tuple-element.32), channel_id=1, source_target_pairs={{0,1},{1,0},{2,3},{3,2},{4,5},{5,4},{6,7},{7,6},{8,9},{9,8},{10,11... | collective-permute-start | bytes 393224 | tf_op jit(solution)/shard_map/ppermute | solution.py:25
  9.8 0.0 copy-done
  9.8 0.3 rest_of_ratings.1
  10.1 0.0 copy-start.2
  10.1 0.0 copy-start.4
  10.1 2.0 %collective-permute-done.2 = bf16[272,256]{1,0:T(8,128)(2,1)S(1)} collective-permute-done((bf16[272,256]{1,0:T(8,128)(2,1)S(1)}, bf16[272,256]{1,0:T(8,128)(2,1)S(1)}, u32[]{:S(2)}, u32[]{:S(2)}) %collective-permute-start.2) | collective-permute-done | bytes 139296 | tf_op jit(solution)/shard_map/ppermute | solution.py:25
  12.1 0.1 collective-permute-done.refs_0_
  12.2 2.8 %collective-permute-done.1.refs_2_ = bf16[256,256]{1,0:T(8,128)(2,1)S(1)} collective-permute-done((bf16[256,256]{1,0:T(8,128)(2,1)S(1)}, bf16[256,256]{1,0:T(8,128)(2,1)S(1)}, u32[]{:S(2)}, u32[]{:S(2)}) %collective-permute-start.1) | collective-permute-done | bytes 131104 | tf_op jit(solution)/shard_map/ppermute | solution.py:25
  15.0 0.6 %shard_grads.4 = (bf16[256,256]{1,0:T(8,128)(2,1)S(1)}, f32[256,256]{1,0:T(8,128)S(1)}, f32[256,256]{1,0:T(8,128)S(1)}) custom-call(bf16[256,256]{1,0:T(8,128)(2,1)S(1)} %collective-permute-done.refs_0_, bf16[256,256]{1,0:T(8,128)(2,1)S(1)} %get-tuple-element.26.refs_1_, bf16[256,256]{1,0:T(8,128)(2,1)S(1)} %collective-permute-done.1.refs_2_, ...), custom_call_target="tpu_custom_call" | custom-call | flops 201326592 | tf_op jit(solution)/shard_map/shard_grads/pallas_call | solution.py:79
  15.6 1.7 %collective-permute-done.4.refs_4_ = bf16[256,256]{1,0:T(8,128)(2,1)S(1)} collective-permute-done((bf16[256,256]{1,0:T(8,128)(2,1)S(1)}, bf16[256,256]{1,0:T(8,128)(2,1)S(1)}, u32[]{:S(2)}, u32[]{:S(2)}) %collective-permute-start.4) | collective-permute-done | bytes 131104 | tf_op jit(solution)/shard_map/ppermute | solution.py:25
  17.3 0.6 %shard_grads.5 = (f32[256,256]{1,0:T(8,128)S(1)}, f32[256,256]{1,0:T(8,128)S(1)}, bf16[256,256]{1,0:T(8,128)(2,1)S(1)}) custom-call(bf16[256,256]{1,0:T(8,128)(2,1)S(1)} %get-tuple-element.25.refs_0_, bf16[256,256]{1,0:T(8,128)(2,1)S(1)} %get-tuple-element.26.refs_1_, bf16[256,256]{1,0:T(8,128)(2,1)S(1)} %collective-permute-done.1.refs_2_, ...), custom_call_target="tpu_custom_call" | custom-call | flops 201326592 | tf_op jit(solution)/shard_map/shard_grads/pallas_call | solution.py:79
  17.9 1.8 %collective-permute-start.6 = (bf16[256,256]{1,0:T(8,128)(2,1)S(1)}, bf16[256,256]{1,0:T(8,128)(2,1)S(1)}, u32[]{:S(2)}, u32[]{:S(2)}) collective-permute-start(bf16[256,256]{1,0:T(8,128)(2,1)S(1)} %get-tuple-element.37), channel_id=1, source_target_pairs={{0,1},{1,0},{2,3},{3,2},{4,5},{5,4},{6,7},{7,6},{8,9},{9,8},{10,11... | collective-permute-start | bytes 393224 | tf_op jit(solution)/shard_map/ppermute | solution.py:25
  19.7 0.2 collective-permute-start.9
  20.0 2.8 %collective-permute-start.3 = (bf16[256,256]{1,0:T(8,128)(2,1)S(1)}, bf16[256,256]{1,0:T(8,128)(2,1)S(1)}, u32[]{:S(2)}, u32[]{:S(2)}) collective-permute-start(bf16[256,256]{1,0:T(8,128)(2,1)S(1)} %get-tuple-element.30), channel_id=1, source_target_pairs={{0,2},{1,3},{2,0},{3,1},{4,6},{5,7},{6,4},{7,5},{8,10},{9,11},{10,... | collective-permute-start | bytes 393224 | tf_op jit(solution)/shard_map/ppermute | solution.py:25
  22.7 4.4 %collective-permute-done.6 = bf16[256,256]{1,0:T(8,128)(2,1)S(1)} collective-permute-done((bf16[256,256]{1,0:T(8,128)(2,1)S(1)}, bf16[256,256]{1,0:T(8,128)(2,1)S(1)}, u32[]{:S(2)}, u32[]{:S(2)}) %collective-permute-start.6) | collective-permute-done | bytes 131104 | tf_op jit(solution)/shard_map/ppermute | solution.py:25
  27.1 0.0 copy-done.1
  27.1 0.0 copy-done.3
  27.1 0.2 fusion.1
  27.3 0.1 collective-permute-start.8
  27.4 0.6 %collective-permute-start.7 = (bf16[256,256]{1,0:T(8,128)(2,1)S(1)}, bf16[256,256]{1,0:T(8,128)(2,1)S(1)}, u32[]{:S(2)}, u32[]{:S(2)}) collective-permute-start(bf16[256,256]{1,0:T(8,128)(2,1)S(1)} %fusion.1), channel_id=1, source_target_pairs={{0,4},{1,5},{2,6},{3,7},{4,8},{5,9},{6,10},{7,11},{8,12},{9,13},{1... | collective-permute-start | bytes 393224 | tf_op jit(solution)/shard_map/ppermute | solution.py:31
  28.0 0.0 collective-permute-done.3
  28.0 0.0 copy-done.2
  28.0 0.0 copy-done.4
  28.0 0.2 fusion.refs_0_
  28.2 3.5 %collective-permute-start.5 = (bf16[256,256]{1,0:T(8,128)(2,1)S(1)}, bf16[256,256]{1,0:T(8,128)(2,1)S(1)}, u32[]{:S(2)}, u32[]{:S(2)}) collective-permute-start(bf16[256,256]{1,0:T(8,128)(2,1)S(1)} %fusion.refs_0_), channel_id=1, source_target_pairs={{0,2},{1,3},{2,0},{3,1},{4,6},{5,7},{6,4},{7,5},{8,10},{9,11},{10,... | collective-permute-start | bytes 393224 | tf_op jit(solution)/shard_map/ppermute | solution.py:25
  31.7 1.3 %collective-permute-start.11 = (bf16[256,256]{1,0:T(8,128)(2,1)S(1)}, bf16[256,256]{1,0:T(8,128)(2,1)S(1)}, u32[]{:S(2)}, u32[]{:S(2)}) collective-permute-start(bf16[256,256]{1,0:T(8,128)(2,1)S(1)} %get-tuple-element.42), channel_id=1, source_target_pairs={{0,1},{1,0},{2,3},{3,2},{4,5},{5,4},{6,7},{7,6},{8,9},{9,8},{10,11... | collective-permute-start | bytes 393224 | tf_op jit(solution)/shard_map/ppermute | solution.py:25
  33.0 0.0 collective-permute-done.9.refs_4_
  33.0 0.7 %collective-permute-done.8.refs_2_ = bf16[256,256]{1,0:T(8,128)(2,1)S(1)} collective-permute-done((bf16[256,256]{1,0:T(8,128)(2,1)S(1)}, bf16[256,256]{1,0:T(8,128)(2,1)S(1)}, u32[]{:S(2)}, u32[]{:S(2)}) %collective-permute-start.8) | collective-permute-done | bytes 131104 | tf_op jit(solution)/shard_map/ppermute | solution.py:31
  33.6 0.5 collective-permute-done.7.refs_1_
  34.1 4.4 %collective-permute-done.5.refs_0_ = bf16[256,256]{1,0:T(8,128)(2,1)S(1)} collective-permute-done((bf16[256,256]{1,0:T(8,128)(2,1)S(1)}, bf16[256,256]{1,0:T(8,128)(2,1)S(1)}, u32[]{:S(2)}, u32[]{:S(2)}) %collective-permute-start.5) | collective-permute-done | bytes 131104 | tf_op jit(solution)/shard_map/ppermute | solution.py:25
  38.5 0.6 %shard_grads.6 = (bf16[256,256]{1,0:T(8,128)(2,1)S(1)}, f32[256,256]{1,0:T(8,128)S(1)}, f32[256,256]{1,0:T(8,128)S(1)}) custom-call(bf16[256,256]{1,0:T(8,128)(2,1)S(1)} %collective-permute-done.5.refs_0_, bf16[256,256]{1,0:T(8,128)(2,1)S(1)} %collective-permute-done.7.refs_1_, bf16[256,256]{1,0:T(8,128)(2,1)S(1)} %collective-permute-done.8.refs_2_, ...), custom_call_target="tpu_custom_call" | custom-call | flops 201326592 | tf_op jit(solution)/shard_map/shard_grads/pallas_call | solution.py:79
  39.1 0.0 collective-permute-done.11.refs_4_
  39.1 0.6 %shard_grads.7 = (f32[256,256]{1,0:T(8,128)S(1)}, bf16[256,256]{1,0:T(8,128)(2,1)S(1)}, bf16[256,256]{1,0:T(8,128)(2,1)S(1)}) custom-call(bf16[256,256]{1,0:T(8,128)(2,1)S(1)} %fusion.refs_0_, bf16[256,256]{1,0:T(8,128)(2,1)S(1)} %collective-permute-done.7.refs_1_, bf16[256,256]{1,0:T(8,128)(2,1)S(1)} %collective-permute-done.8.refs_2_, ...), custom_call_target="tpu_custom_call" | custom-call | flops 201326592 | tf_op jit(solution)/shard_map/shard_grads/pallas_call | solution.py:79
  39.7 0.1 collective-permute-start.12
  39.8 1.8 %collective-permute-start.13 = (bf16[256,256]{1,0:T(8,128)(2,1)S(1)}, bf16[256,256]{1,0:T(8,128)(2,1)S(1)}, u32[]{:S(2)}, u32[]{:S(2)}) collective-permute-start(bf16[256,256]{1,0:T(8,128)(2,1)S(1)} %get-tuple-element.47), channel_id=1, source_target_pairs={{0,29},{1,28},{2,31},{3,30},{4,1},{5,0},{6,3},{7,2},{8,5},{9,4},{1... | collective-permute-start | bytes 393224 | tf_op jit(solution)/shard_map/ppermute | solution.py:31
  41.6 2.2 %collective-permute-start.10 = (bf16[256,256]{1,0:T(8,128)(2,1)S(1)}, bf16[256,256]{1,0:T(8,128)(2,1)S(1)}, u32[]{:S(2)}, u32[]{:S(2)}) collective-permute-start(bf16[256,256]{1,0:T(8,128)(2,1)S(1)} %get-tuple-element.40), channel_id=1, source_target_pairs={{0,2},{1,3},{2,0},{3,1},{4,6},{5,7},{6,4},{7,5},{8,10},{9,11},{10,... | collective-permute-start | bytes 393224 | tf_op jit(solution)/shard_map/ppermute | solution.py:25
  43.8 0.0 collective-permute-done.12
  43.8 1.4 %collective-permute-done.13 = bf16[256,256]{1,0:T(8,128)(2,1)S(1)} collective-permute-done((bf16[256,256]{1,0:T(8,128)(2,1)S(1)}, bf16[256,256]{1,0:T(8,128)(2,1)S(1)}, u32[]{:S(2)}, u32[]{:S(2)}) %collective-permute-start.13) | collective-permute-done | bytes 131104 | tf_op jit(solution)/shard_map/ppermute | solution.py:31
  45.2 1.0 %divide_subtract_fusion = f32[256,256]{1,0:T(8,128)} fusion(bf16[256,256]{1,0:T(8,128)(2,1)S(1)} %collective-permute-done.13, bf16[256,256]{1,0:T(8,128)(2,1)S(1)} %collective-permute-done.12, f32[256,256]{1,0:T(8,128)S(1)} %copy-done.3, f32[256,256]{1,0:T(8,128)S(1)} %copy-done.1, f32[256,256]{1,0:T(8,128)S(1)} %get-tuple-element.36, ...), kind=kLoop, calls=%fused_computation | loop fusion | flops 1376256 | bytes 1441792 | tf_op jit(solution)/shard_map/sub | solution.py:19
  46.2 3.7 %collective-permute-done.10 = bf16[256,256]{1,0:T(8,128)(2,1)S(1)} collective-permute-done((bf16[256,256]{1,0:T(8,128)(2,1)S(1)}, bf16[256,256]{1,0:T(8,128)(2,1)S(1)}, u32[]{:S(2)}, u32[]{:S(2)}) %collective-permute-start.10) | collective-permute-done | bytes 131104 | tf_op jit(solution)/shard_map/ppermute | solution.py:25
  49.9 1.0 %divide_subtract_fusion.1 = f32[256,256]{1,0:T(8,128)} fusion(f32[256,256]{1,0:T(8,128)S(1)} %get-tuple-element.45, bf16[256,256]{1,0:T(8,128)(2,1)S(1)} %collective-permute-done.10, f32[256,256]{1,0:T(8,128)S(1)} %copy-done.4, f32[256,256]{1,0:T(8,128)S(1)} %get-tuple-element.35, bf16[256,256]{1,0:T(8,128)(2,1)S(1)} %collective-permute-done.3, ...), kind=kLoop, calls=%fused_computation.1 | loop fusion | flops 1310720 | bytes 1572864 | tf_op jit(solution)/shard_map/sub | solution.py:19
  (2 shorter events, 0.0 us)
Async XLA Ops:
  0.6 9.2 %copy-start = (s32[2,1024,256]{2,1,0:T(8,128)S(1)}, s32[2,1024,256]{2,1,0:T(8,128)}, u32[]{:S(2)}) copy-start(s32[2,1024,256]{2,1,0:T(8,128)} %ratings.1) | copy-start | bytes 6291460
  2.1 10.0 %collective-permute-start.2 = (bf16[272,256]{1,0:T(8,128)(2,1)S(1)}, bf16[272,256]{1,0:T(8,128)(2,1)S(1)}, u32[]{:S(2)}, u32[]{:S(2)}) collective-permute-start(bf16[272,256]{1,0:T(8,128)(2,1)S(1)} %get-tuple-element.28), channel_id=1, source_target_pairs={{0,1},{1,0},{2,3},{3,2},{4,5},{5,4},{6,7},{7,6},{8,9},{9,8},{10,11... | collective-permute-start | bytes 417800 | tf_op jit(solution)/shard_map/ppermute | solution.py:25
  5.2 7.0 %collective-permute-start = (bf16[256,256]{1,0:T(8,128)(2,1)S(1)}, bf16[256,256]{1,0:T(8,128)(2,1)S(1)}, u32[]{:S(2)}, u32[]{:S(2)}) collective-permute-start(bf16[256,256]{1,0:T(8,128)(2,1)S(1)} %get-tuple-element.25.refs_0_), channel_id=1, source_target_pairs={{0,2},{1,3},{2,0},{3,1},{4,6},{5,7},{6,4},{7,5},{8,10},{9,11},{10,... | collective-permute-start | bytes 393224 | tf_op jit(solution)/shard_map/ppermute | solution.py:25
  7.8 7.2 %collective-permute-start.1 = (bf16[256,256]{1,0:T(8,128)(2,1)S(1)}, bf16[256,256]{1,0:T(8,128)(2,1)S(1)}, u32[]{:S(2)}, u32[]{:S(2)}) collective-permute-start(bf16[256,256]{1,0:T(8,128)(2,1)S(1)} %get-tuple-element.26.refs_1_), channel_id=1, source_target_pairs={{0,1},{1,0},{2,3},{3,2},{4,5},{5,4},{6,7},{7,6},{8,9},{9,8},{10,11... | collective-permute-start | bytes 393224 | tf_op jit(solution)/shard_map/ppermute | solution.py:25
  8.2 18.9 %copy-start.1 = (f32[256,256]{1,0:T(8,128)S(1)}, f32[256,256]{1,0:T(8,128)}, u32[]{:S(2)}) copy-start(f32[256,256]{1,0:T(8,128)} %refs_1_.1) | copy-start | bytes 786436
  8.2 18.9 %copy-start.3 = (f32[256,256]{1,0:T(8,128)S(1)}, f32[256,256]{1,0:T(8,128)}, u32[]{:S(2)}) copy-start(f32[256,256]{1,0:T(8,128)} %param.9) | copy-start | bytes 786436
  8.2 9.1 %collective-permute-start.4 = (bf16[256,256]{1,0:T(8,128)(2,1)S(1)}, bf16[256,256]{1,0:T(8,128)(2,1)S(1)}, u32[]{:S(2)}, u32[]{:S(2)}) collective-permute-start(bf16[256,256]{1,0:T(8,128)(2,1)S(1)} %get-tuple-element.32), channel_id=1, source_target_pairs={{0,1},{1,0},{2,3},{3,2},{4,5},{5,4},{6,7},{7,6},{8,9},{9,8},{10,11... | collective-permute-start | bytes 393224 | tf_op jit(solution)/shard_map/ppermute | solution.py:25
  10.1 17.9 %copy-start.2 = (f32[256,256]{1,0:T(8,128)S(1)}, f32[256,256]{1,0:T(8,128)}, u32[]{:S(2)}) copy-start(f32[256,256]{1,0:T(8,128)} %refs_0_.1) | copy-start | bytes 786436
  10.1 17.9 %copy-start.4 = (f32[256,256]{1,0:T(8,128)S(1)}, f32[256,256]{1,0:T(8,128)}, u32[]{:S(2)}) copy-start(f32[256,256]{1,0:T(8,128)} %param.7) | copy-start | bytes 786436
  17.9 9.2 %collective-permute-start.6 = (bf16[256,256]{1,0:T(8,128)(2,1)S(1)}, bf16[256,256]{1,0:T(8,128)(2,1)S(1)}, u32[]{:S(2)}, u32[]{:S(2)}) collective-permute-start(bf16[256,256]{1,0:T(8,128)(2,1)S(1)} %get-tuple-element.37), channel_id=1, source_target_pairs={{0,1},{1,0},{2,3},{3,2},{4,5},{5,4},{6,7},{7,6},{8,9},{9,8},{10,11... | collective-permute-start | bytes 393224 | tf_op jit(solution)/shard_map/ppermute | solution.py:25
  19.7 13.3 %collective-permute-start.9 = (bf16[256,256]{1,0:T(8,128)(2,1)S(1)}, bf16[256,256]{1,0:T(8,128)(2,1)S(1)}, u32[]{:S(2)}, u32[]{:S(2)}) collective-permute-start(bf16[256,256]{1,0:T(8,128)(2,1)S(1)} %get-tuple-element.39), channel_id=1, source_target_pairs={{0,1},{1,0},{2,3},{3,2},{4,5},{5,4},{6,7},{7,6},{8,9},{9,8},{10,11... | collective-permute-start | bytes 393224 | tf_op jit(solution)/shard_map/ppermute | solution.py:25
  20.0 8.0 %collective-permute-start.3 = (bf16[256,256]{1,0:T(8,128)(2,1)S(1)}, bf16[256,256]{1,0:T(8,128)(2,1)S(1)}, u32[]{:S(2)}, u32[]{:S(2)}) collective-permute-start(bf16[256,256]{1,0:T(8,128)(2,1)S(1)} %get-tuple-element.30), channel_id=1, source_target_pairs={{0,2},{1,3},{2,0},{3,1},{4,6},{5,7},{6,4},{7,5},{8,10},{9,11},{10,... | collective-permute-start | bytes 393224 | tf_op jit(solution)/shard_map/ppermute | solution.py:25
  27.3 6.3 %collective-permute-start.8 = (bf16[256,256]{1,0:T(8,128)(2,1)S(1)}, bf16[256,256]{1,0:T(8,128)(2,1)S(1)}, u32[]{:S(2)}, u32[]{:S(2)}) collective-permute-start(bf16[256,256]{1,0:T(8,128)(2,1)S(1)} %fusion.1), channel_id=1, source_target_pairs={{0,5},{1,4},{2,7},{3,6},{4,9},{5,8},{6,11},{7,10},{8,13},{9,12},{1... | collective-permute-start | bytes 393224 | tf_op jit(solution)/shard_map/ppermute | solution.py:31
  27.4 6.7 %collective-permute-start.7 = (bf16[256,256]{1,0:T(8,128)(2,1)S(1)}, bf16[256,256]{1,0:T(8,128)(2,1)S(1)}, u32[]{:S(2)}, u32[]{:S(2)}) collective-permute-start(bf16[256,256]{1,0:T(8,128)(2,1)S(1)} %fusion.1), channel_id=1, source_target_pairs={{0,4},{1,5},{2,6},{3,7},{4,8},{5,9},{6,10},{7,11},{8,12},{9,13},{1... | collective-permute-start | bytes 393224 | tf_op jit(solution)/shard_map/ppermute | solution.py:31
  28.2 10.3 %collective-permute-start.5 = (bf16[256,256]{1,0:T(8,128)(2,1)S(1)}, bf16[256,256]{1,0:T(8,128)(2,1)S(1)}, u32[]{:S(2)}, u32[]{:S(2)}) collective-permute-start(bf16[256,256]{1,0:T(8,128)(2,1)S(1)} %fusion.refs_0_), channel_id=1, source_target_pairs={{0,2},{1,3},{2,0},{3,1},{4,6},{5,7},{6,4},{7,5},{8,10},{9,11},{10,... | collective-permute-start | bytes 393224 | tf_op jit(solution)/shard_map/ppermute | solution.py:25
  31.7 7.4 %collective-permute-start.11 = (bf16[256,256]{1,0:T(8,128)(2,1)S(1)}, bf16[256,256]{1,0:T(8,128)(2,1)S(1)}, u32[]{:S(2)}, u32[]{:S(2)}) collective-permute-start(bf16[256,256]{1,0:T(8,128)(2,1)S(1)} %get-tuple-element.42), channel_id=1, source_target_pairs={{0,1},{1,0},{2,3},{3,2},{4,5},{5,4},{6,7},{7,6},{8,9},{9,8},{10,11... | collective-permute-start | bytes 393224 | tf_op jit(solution)/shard_map/ppermute | solution.py:25
  39.7 4.1 %collective-permute-start.12 = (bf16[256,256]{1,0:T(8,128)(2,1)S(1)}, bf16[256,256]{1,0:T(8,128)(2,1)S(1)}, u32[]{:S(2)}, u32[]{:S(2)}) collective-permute-start(bf16[256,256]{1,0:T(8,128)(2,1)S(1)} %get-tuple-element.46), channel_id=1, source_target_pairs={{0,28},{1,29},{2,30},{3,31},{4,0},{5,1},{6,2},{7,3},{8,4},{9,5},{1... | collective-permute-start | bytes 393224 | tf_op jit(solution)/shard_map/ppermute | solution.py:31
  39.8 5.4 %collective-permute-start.13 = (bf16[256,256]{1,0:T(8,128)(2,1)S(1)}, bf16[256,256]{1,0:T(8,128)(2,1)S(1)}, u32[]{:S(2)}, u32[]{:S(2)}) collective-permute-start(bf16[256,256]{1,0:T(8,128)(2,1)S(1)} %get-tuple-element.47), channel_id=1, source_target_pairs={{0,29},{1,28},{2,31},{3,30},{4,1},{5,0},{6,3},{7,2},{8,5},{9,4},{1... | collective-permute-start | bytes 393224 | tf_op jit(solution)/shard_map/ppermute | solution.py:31
  41.6 8.3 %collective-permute-start.10 = (bf16[256,256]{1,0:T(8,128)(2,1)S(1)}, bf16[256,256]{1,0:T(8,128)(2,1)S(1)}, u32[]{:S(2)}, u32[]{:S(2)}) collective-permute-start(bf16[256,256]{1,0:T(8,128)(2,1)S(1)} %get-tuple-element.40), channel_id=1, source_target_pairs={{0,2},{1,3},{2,0},{3,1},{4,6},{5,7},{6,4},{7,5},{8,10},{9,11},{10,... | collective-permute-start | bytes 393224 | tf_op jit(solution)/shard_map/ppermute | solution.py:25

commit v3 on v2

--- a/solution.py
+++ b/solution.py
@@ -10,8 +10,7 @@
 
 BF = jnp.bfloat16
 F32 = jnp.float32
-FIRST_PARAMS = pltpu.CompilerParams(vmem_limit_bytes=16<<20)
-REST_PARAMS = pltpu.CompilerParams(vmem_limit_bytes=16 << 20)
+SMALL = pltpu.CompilerParams(vmem_limit_bytes=16 << 20)
 
 
 def adagrad(param, accum, grad):
@@ -85,7 +84,7 @@
         ),
         in_specs=[spec] * len(operands),
         out_specs=(spec,) * 3,
-        compiler_params=pltpu.CompilerParams(vmem_limit_bytes=16 << 20),
+        compiler_params=SMALL,
         cost_estimate=pl.CostEstimate(
             flops=12 * rows * cols * rank, bytes_accessed=0, transcendentals=2 * rows * cols
         ),
@@ -108,65 +107,74 @@
     return ratings.at[s, pl.ds(at, rows), :]
 
 
+def rows_kernel(*refs):
+    count = (len(refs) - 1) // 3
+    sources, outs, bufs, sems = refs[:count], refs[count : 2 * count], refs[2 * count : -1], refs[-1]
+    for copy, buf, out in zip(fetch(sources, bufs, sems), bufs, outs):
+        copy.wait()
+        out[...] = buf[...].astype(BF)
+
+
+def first_rows(*arrays):
+    return pl.pallas_call(
+        rows_kernel,
+        out_shape=tuple(jax.ShapeDtypeStruct(a.shape, BF) for a in arrays),
+        in_specs=[pl.BlockSpec(memory_space=pltpu.HBM)] * len(arrays),
+        out_specs=(pl.BlockSpec(memory_space=pltpu.VMEM),) * len(arrays),
+        scratch_shapes=[pltpu.VMEM(a.shape, a.dtype) for a in arrays]
+        + [pltpu.SemaphoreType.DMA((len(arrays),))],
+        compiler_params=SMALL,
+        name="first_rows",
+    )(*(pltpu.with_memory_space_constraint(a, pltpu.HBM) for a in arrays))
+
+
 def first_kernel(group, rows, side, *refs):
-    users, items, ratings, masks = refs[:4]
-    users_bf, items_bf, wide = refs[4:7]
-    sent = refs[7 : 7 + group]
-    scratch = refs[7 + group :]
-    sems = scratch[-1]
+    ratings, masks, wide = refs[:3]
+    sent = refs[3 : 3 + group]
+    scratch = refs[3 + group :]
     n = lax.axis_size("item")
     other = lax.axis_index("item") ^ 1
     order = list(range(1, group)) + [0]
-    sources = [items, users, masks] + [share(ratings, 0, other, k, rows, n) for k in order]
-    copies = fetch(sources, scratch[:-1], sems)
-    for i, out in enumerate((items_bf, users_bf)):
-        copies[i].wait()
-        out[...] = scratch[i][...].astype(BF)
-    copies[2].wait()
+    sources = [masks] + [share(ratings, 0, other, k, rows, n) for k in order]
+    copies = fetch(sources, scratch[:-1], scratch[-1])
+    copies[0].wait()
     strata, across, tiles = masks.shape
     eye = lax.broadcasted_iota(jnp.int32, (tiles, tiles), 0) == lax.broadcasted_iota(
         jnp.int32, (tiles, tiles), 1
     )
     for s in range(strata):
-        band = scratch[2][s].astype(F32)
+        band = scratch[0][s].astype(F32)
         parts = []
         for c in range(across):
             spread = jnp.where(eye, jnp.broadcast_to(band[c : c + 1], (tiles, tiles)), 0.0)
             parts.append(jnp.broadcast_to(jnp.sum(spread, axis=1, keepdims=True), (tiles, side)))
         wide[pl.ds(s * tiles, tiles), :] = jnp.concatenate(parts, axis=1)
     for i, out in enumerate(sent):
-        copies[3 + i].wait()
-        out[pl.ds(0, rows), :] = scratch[3 + i][...].astype(F32).astype(BF)
+        copies[1 + i].wait()
+        out[pl.ds(0, rows), :] = scratch[1 + i][...].astype(F32).astype(BF)
     sent[0][pl.ds(rows, strata * tiles), :] = wide[...].astype(BF)
 
 
-def first_sends(users, items, ratings, tile_mask, group, side):
-    rows, _ = users.shape
+def first_sends(ratings, tile_mask, rows, group, side):
     cols = ratings.shape[2]
     masks = tile_mask.transpose(0, 2, 1)
     wide = (tile_mask.shape[0] * tile_mask.shape[1], cols)
     vmem = pl.BlockSpec(memory_space=pltpu.VMEM)
     out_shape = [
-        jax.ShapeDtypeStruct(users.shape, BF),
-        jax.ShapeDtypeStruct(items.shape, BF),
         jax.ShapeDtypeStruct(wide, F32),
         jax.ShapeDtypeStruct((rows + wide[0], cols), BF),
     ] + [jax.ShapeDtypeStruct((rows, cols), BF)] * (group - 1)
     return pl.pallas_call(
         functools.partial(first_kernel, group, rows, side),
         out_shape=tuple(out_shape),
-        in_specs=[pl.BlockSpec(memory_space=pltpu.HBM)] * 4,
+        in_specs=[pl.BlockSpec(memory_space=pltpu.HBM)] * 2,
         out_specs=(vmem,) * len(out_shape),
-        scratch_shapes=[
-            pltpu.VMEM(items.shape, F32),
-            pltpu.VMEM(users.shape, F32),
-            pltpu.VMEM(masks.shape, jnp.int32),
-        ]
+        scratch_shapes=[pltpu.VMEM(masks.shape, jnp.int32)]
         + [pltpu.VMEM((rows, cols), jnp.int32)] * group
-        + [pltpu.SemaphoreType.DMA((3 + group,))],
-        compiler_params=FIRST_PARAMS,
+        + [pltpu.SemaphoreType.DMA((1 + group,))],
+        compiler_params=SMALL,
         name="first_sends",
-    )(*(pltpu.with_memory_space_constraint(a, pltpu.HBM) for a in (users, items, ratings, masks)))
+    )(*(pltpu.with_memory_space_constraint(a, pltpu.HBM) for a in (ratings, masks)))
 
 
 def rest_kernel(picks, rows, ratings, *refs):
@@ -191,9 +199,41 @@
         out_specs=(vmem,) * len(picks),
         scratch_shapes=[pltpu.VMEM((rows, cols), jnp.int32)] * len(picks)
         + [pltpu.SemaphoreType.DMA((len(picks),))],
-        compiler_params=REST_PARAMS,
+        compiler_params=SMALL,
         name="rest_of_ratings",
-    )(ratings)
+    )(pltpu.with_memory_space_constraint(ratings, pltpu.HBM))
+
+
+def last_kernel(count, *refs):
+    param, accum = refs[:2]
+    grads, out, buf, sems = refs[2:-3], refs[-3], refs[-2], refs[-1]
+    band = param.shape[0] // count
+    copies = []
+    for i in range(count):
+        here = pl.ds(i * band, band)
+        old = param[here, :]
+        grad = 0.1 * old
+        for share in grads:
+            grad = grad + share[here, :].astype(F32)
+        buf[here, :] = adagrad(old, accum[here, :], grad)[0]
+        copies.append(pltpu.make_async_copy(buf.at[here, :], out.at[here, :], sems.at[i]))
+        copies[-1].start()
+    for copy in copies:
+        copy.wait()
+
+
+def last_update(param, accum, *grads):
+    count = 4
+    vmem = pl.BlockSpec(memory_space=pltpu.VMEM)
+    return pl.pallas_call(
+        functools.partial(last_kernel, count),
+        out_shape=jax.ShapeDtypeStruct(param.shape, F32),
+        in_specs=[vmem] * (2 + len(grads)),
+        out_specs=pl.BlockSpec(memory_space=pltpu.HBM),
+        scratch_shapes=[pltpu.VMEM(param.shape, F32), pltpu.SemaphoreType.DMA((count,))],
+        compiler_params=SMALL,
+        name="last_update",
+    )(param, accum, *grads)
 
 
 def body(users, user_accum, items, item_accum, ratings, tile_mask):
@@ -205,9 +245,8 @@
     side = block_users // tiles
     order = list(range(1, group)) + [0]
 
-    first_users, first_items, wide, *sends = first_sends(
-        users, items, ratings, tile_mask, group, side
-    )
+    first_items, first_users = first_rows(items, users)
+    wide, *sends = first_sends(ratings, tile_mask, rows, group, side)
     shards = {0: first_users}
     for k in range(1, group):
         shards[k] = move(first_users, 0, lambda i: (i - 2 * k) % n)
@@ -234,11 +273,10 @@
             items_bf = items.astype(BF)
             near = move(items_bf, s, lambda i: i)
             far = move(items_bf, s, lambda i: i ^ 1)
-        user_grad = 0.1 * users
+        user_shares = []
         carry = ()
-        turn = order
-        for k in turn:
-            last = k == turn[-1]
+        for k in order:
+            last = k == order[-1]
             part, g_near, g_far = shard_grads(
                 k,
                 s * tiles,
@@ -250,15 +288,20 @@
             )
             carry = (g_near, g_far)
             if k:
-                part = move(part, 0, lambda i: (i + 2 * k) % n).astype(F32)
-            user_grad = user_grad + part
+                part = move(part, 0, lambda i: (i + 2 * k) % n)
+            user_shares.append(part)
         g_near, g_far = carry
         if s:
-            g_near = move(g_near, -s, lambda i: i).astype(F32)
-        g_far = move(g_far, -s, lambda i: i ^ 1).astype(F32)
-        item_grad = g_near + g_far + 0.1 * items
-        users, user_accum = adagrad(users, user_accum, user_grad)
-        items, item_accum = adagrad(items, item_accum, item_grad)
+            g_near = move(g_near, -s, lambda i: i)
+        g_far = move(g_far, -s, lambda i: i ^ 1)
+        if s == strata - 1:
+            users = last_update(users, user_accum, *user_shares)
+            items = last_update(items, item_accum, g_near, g_far)
+        else:
+            user_grad = sum((t.astype(F32) for t in user_shares), 0.1 * users)
+            item_grad = sum((t.astype(F32) for t in (g_near, g_far)), 0.1 * items)
+            users, user_accum = adagrad(users, user_accum, user_grad)
+            items, item_accum = adagrad(items, item_accum, item_grad)
     return (users, items)
 
 

time: 51.1 us -> 50.5 us (0.988)
  waiting for transfers between devices: 21.6 us -> 18 us
  Pallas kernels: 4.02 us -> 7.55 us
  other arithmetic: 2.46 us -> 0.36 us
  starting transfers between devices: 22.1 us -> 23.6 us
    ppermute x10, waiting for transfers between devices: 19.1 us -> 9.73 us  [move(): lax.ppermute(array, 'item', [(z, item_map(z)) for z in range(n_item)])]
    ppermute x4, waiting for transfers between devices: 2.52 us -> 8.28 us  [move(): return lax.ppermute(array, ('user', 'item'), pairs)]
    pallas_call x0 -> x3, Pallas kernels: none -> 2.73 us  [the longest x2 1.67 us: last_update(): pl.pallas_call(functools.partial(last_kernel, count), out_shape=jax.Shape...]
    sub x2 -> x0, other arithmetic: 2.09 us -> none  [adagrad(): return (param - 0.25 * grad / (jnp.sqrt(accum) + 1e-06), accum)]
    ppermute x4, starting transfers between devices: 2.58 us -> 3.84 us  [move(): return lax.ppermute(array, ('user', 'item'), pairs)]
    pallas_call x1, Pallas kernels: 0.26 us -> 1.41 us  [rest_of_ratings(): pl.pallas_call(functools.partial(rest_kernel, picks, rows), out_shape=(ja...]
  transfers between devices with their start and end apart: 14 -> 14, of which waited for: 10 -> 7; matrix products, arithmetic and copies ran while one was open for 3% -> 1% of each run, Pallas kernels for 3% -> 10%
where the time goes in v3:
time: 50.5 us; the launch traced here: 50.3 us
  starting transfers between devices  23.6 us (47%)
  waiting for transfers between devices  18 us (36%)
  Pallas kernels  7.55 us (15%)
  between operations  0.75 us (1%)
    ppermute x10, starting transfers between devices, move(): lax.ppermute(array, 'item', [(z, item_map(z)) for z in range(n_item)])  19.7 us
    ppermute x10, waiting for transfers between devices, move(): lax.ppermute(array, 'item', [(z, item_map(z)) for z in range(n_item)])  9.73 us
    ppermute x4, waiting for transfers between devices, move(): return lax.ppermute(array, ('user', 'item'), pairs)  8.28 us
    ppermute x4, starting transfers between devices, move(): return lax.ppermute(array, ('user', 'item'), pairs)  3.84 us
    pallas_call x4, Pallas kernels, shard_grads(): pl.pallas_call(functools.partial(shard_kernel, k, first_tile, side, bool(...  2.33 us
    pallas_call x2, Pallas kernels, last_update(): pl.pallas_call(functools.partial(last_kernel, count), out_shape=jax.Shape...  1.67 us
    pallas_call x1, Pallas kernels, rest_of_ratings(): pl.pallas_call(functools.partial(rest_kernel, picks, rows), out_shape=(ja...  1.41 us
    pallas_call x1, Pallas kernels, first_sends(): pl.pallas_call(functools.partial(first_kernel, group, rows, side), out_sh...  1.09 us
  transfers between devices with their start and end apart: 14, of which 7 were waited for; matrix products, arithmetic and copies ran while one was open for 1% of the time, Pallas kernels for 10%

profile of v3, /device:TPU:0, one launch (start us, length us, event | category | flops | bytes accessed | tf_op | source)
XLA Modules:
  0.0 50.3 jit_solution(2251028895403952953)
XLA Ops:
  0.6 1.1 %first_sends.1 = (f32[16,256]{1,0:T(8,128)S(1)}, bf16[272,256]{1,0:T(8,128)(2,1)S(1)}, bf16[256,256]{1,0:T(8,128)(2,1)S(1)}) custom-call(s32[2,1024,256]{2,1,0:T(8,128)} %refs_0_.3, s32[2,2,8]{2,1,0:T(2,128)} %bitcast.1), custom_call_target="tpu_custom_call" | custom-call | tf_op jit(solution)/shard_map/first_sends/pallas_call | solution.py:167
  1.7 3.1 %collective-permute-start.2 = (bf16[272,256]{1,0:T(8,128)(2,1)S(1)}, bf16[272,256]{1,0:T(8,128)(2,1)S(1)}, u32[]{:S(2)}, u32[]{:S(2)}) collective-permute-start(bf16[272,256]{1,0:T(8,128)(2,1)S(1)} %get-tuple-element.28), channel_id=1, source_target_pairs={{0,1},{1,0},{2,3},{3,2},{4,5},{5,4},{6,7},{7,6},{8,9},{9,8},{10,11... | collective-permute-start | bytes 417800 | tf_op jit(solution)/shard_map/ppermute | solution.py:24
  4.8 1.1 %first_rows.1 = (bf16[256,256]{1,0:T(8,128)(2,1)S(1)}, bf16[256,256]{1,0:T(8,128)(2,1)S(1)}) custom-call(f32[256,256]{1,0:T(8,128)} %refs_0_.2, f32[256,256]{1,0:T(8,128)} %refs_1_.1), custom_call_target="tpu_custom_call" | custom-call | tf_op jit(solution)/shard_map/first_rows/pallas_call | solution.py:119
  5.9 2.7 %collective-permute-start = (bf16[256,256]{1,0:T(8,128)(2,1)S(1)}, bf16[256,256]{1,0:T(8,128)(2,1)S(1)}, u32[]{:S(2)}, u32[]{:S(2)}) collective-permute-start(bf16[256,256]{1,0:T(8,128)(2,1)S(1)} %get-tuple-element.25.refs_0_), channel_id=1, source_target_pairs={{0,2},{1,3},{2,0},{3,1},{4,6},{5,7},{6,4},{7,5},{8,10},{9,11},{10,... | collective-permute-start | bytes 393224 | tf_op jit(solution)/shard_map/ppermute | solution.py:24
  8.6 0.4 collective-permute-start.1
  9.0 0.0 copy-start
  9.0 0.0 copy-start.2
  9.0 1.6 %collective-permute-start.4 = (bf16[256,256]{1,0:T(8,128)(2,1)S(1)}, bf16[256,256]{1,0:T(8,128)(2,1)S(1)}, u32[]{:S(2)}, u32[]{:S(2)}) collective-permute-start(bf16[256,256]{1,0:T(8,128)(2,1)S(1)} %get-tuple-element.32), channel_id=1, source_target_pairs={{0,1},{1,0},{2,3},{3,2},{4,5},{5,4},{6,7},{7,6},{8,9},{9,8},{10,11... | collective-permute-start | bytes 393224 | tf_op jit(solution)/shard_map/ppermute | solution.py:24
  10.6 1.4 %rest_of_ratings.1 = (bf16[256,256]{1,0:T(8,128)(2,1)S(1)}, bf16[256,256]{1,0:T(8,128)(2,1)S(1)}, bf16[256,256]{1,0:T(8,128)(2,1)S(1)}, bf16[256,256]{1,0:T(8,12...) custom-call(s32[2,1024,256]{2,1,0:T(8,128)} %refs_0_.3), custom_call_target="tpu_custom_call" | custom-call | tf_op jit(solution)/shard_map/rest_of_ratings/pallas_call | solution.py:195
  12.0 0.0 copy-start.1
  12.0 0.0 copy-start.3
  12.0 0.0 collective-permute-done.2
  12.1 2.6 %collective-permute-done.refs_0_ = bf16[256,256]{1,0:T(8,128)(2,1)S(1)} collective-permute-done((bf16[256,256]{1,0:T(8,128)(2,1)S(1)}, bf16[256,256]{1,0:T(8,128)(2,1)S(1)}, u32[]{:S(2)}, u32[]{:S(2)}) %collective-permute-start) | collective-permute-done | bytes 131104 | tf_op jit(solution)/shard_map/ppermute | solution.py:24
  14.6 1.3 %collective-permute-done.1.refs_2_ = bf16[256,256]{1,0:T(8,128)(2,1)S(1)} collective-permute-done((bf16[256,256]{1,0:T(8,128)(2,1)S(1)}, bf16[256,256]{1,0:T(8,128)(2,1)S(1)}, u32[]{:S(2)}, u32[]{:S(2)}) %collective-permute-start.1) | collective-permute-done | bytes 131104 | tf_op jit(solution)/shard_map/ppermute | solution.py:24
  16.0 0.6 %shard_grads.4 = (bf16[256,256]{1,0:T(8,128)(2,1)S(1)}, f32[256,256]{1,0:T(8,128)S(1)}, f32[256,256]{1,0:T(8,128)S(1)}) custom-call(bf16[256,256]{1,0:T(8,128)(2,1)S(1)} %collective-permute-done.refs_0_, bf16[256,256]{1,0:T(8,128)(2,1)S(1)} %get-tuple-element.26.refs_1_, bf16[256,256]{1,0:T(8,128)(2,1)S(1)} %collective-permute-done.1.refs_2_, ...), custom_call_target="tpu_custom_call" | custom-call | flops 201326592 | tf_op jit(solution)/shard_map/shard_grads/pallas_call | solution.py:78
  16.5 2.1 %collective-permute-start.3 = (bf16[256,256]{1,0:T(8,128)(2,1)S(1)}, bf16[256,256]{1,0:T(8,128)(2,1)S(1)}, u32[]{:S(2)}, u32[]{:S(2)}) collective-permute-start(bf16[256,256]{1,0:T(8,128)(2,1)S(1)} %get-tuple-element.30), channel_id=1, source_target_pairs={{0,2},{1,3},{2,0},{3,1},{4,6},{5,7},{6,4},{7,5},{8,10},{9,11},{10,... | collective-permute-start | bytes 393224 | tf_op jit(solution)/shard_map/ppermute | solution.py:24
  18.7 1.6 %collective-permute-start.9 = (bf16[256,256]{1,0:T(8,128)(2,1)S(1)}, bf16[256,256]{1,0:T(8,128)(2,1)S(1)}, u32[]{:S(2)}, u32[]{:S(2)}) collective-permute-start(bf16[256,256]{1,0:T(8,128)(2,1)S(1)} %get-tuple-element.39), channel_id=1, source_target_pairs={{0,1},{1,0},{2,3},{3,2},{4,5},{5,4},{6,7},{7,6},{8,9},{9,8},{10,11... | collective-permute-start | bytes 393224 | tf_op jit(solution)/shard_map/ppermute | solution.py:24
  20.2 0.0 collective-permute-done.4.refs_4_
  20.2 0.6 %shard_grads.5 = (f32[256,256]{1,0:T(8,128)S(1)}, f32[256,256]{1,0:T(8,128)S(1)}, bf16[256,256]{1,0:T(8,128)(2,1)S(1)}) custom-call(bf16[256,256]{1,0:T(8,128)(2,1)S(1)} %get-tuple-element.25.refs_0_, bf16[256,256]{1,0:T(8,128)(2,1)S(1)} %get-tuple-element.26.refs_1_, bf16[256,256]{1,0:T(8,128)(2,1)S(1)} %collective-permute-done.1.refs_2_, ...), custom_call_target="tpu_custom_call" | custom-call | flops 201326592 | tf_op jit(solution)/shard_map/shard_grads/pallas_call | solution.py:78
  20.8 0.5 %collective-permute-start.6 = (bf16[256,256]{1,0:T(8,128)(2,1)S(1)}, bf16[256,256]{1,0:T(8,128)(2,1)S(1)}, u32[]{:S(2)}, u32[]{:S(2)}) collective-permute-start(bf16[256,256]{1,0:T(8,128)(2,1)S(1)} %get-tuple-element.37), channel_id=1, source_target_pairs={{0,1},{1,0},{2,3},{3,2},{4,5},{5,4},{6,7},{7,6},{8,9},{9,8},{10,11... | collective-permute-start | bytes 393224 | tf_op jit(solution)/shard_map/ppermute | solution.py:24
  21.3 1.3 %collective-permute-done.3 = bf16[256,256]{1,0:T(8,128)(2,1)S(1)} collective-permute-done((bf16[256,256]{1,0:T(8,128)(2,1)S(1)}, bf16[256,256]{1,0:T(8,128)(2,1)S(1)}, u32[]{:S(2)}, u32[]{:S(2)}) %collective-permute-start.3) | collective-permute-done | bytes 131104 | tf_op jit(solution)/shard_map/ppermute | solution.py:24
  22.7 0.0 copy-done
  22.7 0.0 copy-done.2
  22.7 0.2 fusion.1
  22.9 3.4 %collective-permute-start.5 = (bf16[256,256]{1,0:T(8,128)(2,1)S(1)}, bf16[256,256]{1,0:T(8,128)(2,1)S(1)}, u32[]{:S(2)}, u32[]{:S(2)}) collective-permute-start(bf16[256,256]{1,0:T(8,128)(2,1)S(1)} %get-tuple-element.50.refs_0_), channel_id=1, source_target_pairs={{0,2},{1,3},{2,0},{3,1},{4,6},{5,7},{6,4},{7,5},{8,10},{9,11},{10,... | collective-permute-start | bytes 393224 | tf_op jit(solution)/shard_map/ppermute | solution.py:24
  26.3 3.0 %collective-permute-done.6 = bf16[256,256]{1,0:T(8,128)(2,1)S(1)} collective-permute-done((bf16[256,256]{1,0:T(8,128)(2,1)S(1)}, bf16[256,256]{1,0:T(8,128)(2,1)S(1)}, u32[]{:S(2)}, u32[]{:S(2)}) %collective-permute-start.6) | collective-permute-done | bytes 131104 | tf_op jit(solution)/shard_map/ppermute | solution.py:24
  29.3 0.0 copy-done.1
  29.3 0.0 copy-done.3
  29.3 0.2 fusion
  29.4 0.1 collective-permute-start.8
  29.5 0.8 %collective-permute-start.7 = (bf16[256,256]{1,0:T(8,128)(2,1)S(1)}, bf16[256,256]{1,0:T(8,128)(2,1)S(1)}, u32[]{:S(2)}, u32[]{:S(2)}) collective-permute-start(bf16[256,256]{1,0:T(8,128)(2,1)S(1)} %get-tuple-element.48), channel_id=1, source_target_pairs={{0,4},{1,5},{2,6},{3,7},{4,8},{5,9},{6,10},{7,11},{8,12},{9,13},{1... | collective-permute-start | bytes 393224 | tf_op jit(solution)/shard_map/ppermute | solution.py:30
  30.3 2.2 %collective-permute-start.11 = (bf16[256,256]{1,0:T(8,128)(2,1)S(1)}, bf16[256,256]{1,0:T(8,128)(2,1)S(1)}, u32[]{:S(2)}, u32[]{:S(2)}) collective-permute-start(bf16[256,256]{1,0:T(8,128)(2,1)S(1)} %get-tuple-element.42), channel_id=1, source_target_pairs={{0,1},{1,0},{2,3},{3,2},{4,5},{5,4},{6,7},{7,6},{8,9},{9,8},{10,11... | collective-permute-start | bytes 393224 | tf_op jit(solution)/shard_map/ppermute | solution.py:24
  32.6 0.0 collective-permute-done.9.refs_4_
  32.6 0.0 collective-permute-done.5.refs_0_
  32.6 3.7 %collective-permute-done.8.refs_2_ = bf16[256,256]{1,0:T(8,128)(2,1)S(1)} collective-permute-done((bf16[256,256]{1,0:T(8,128)(2,1)S(1)}, bf16[256,256]{1,0:T(8,128)(2,1)S(1)}, u32[]{:S(2)}, u32[]{:S(2)}) %collective-permute-start.8) | collective-permute-done | bytes 131104 | tf_op jit(solution)/shard_map/ppermute | solution.py:30
  36.3 0.0 collective-permute-done.7.refs_1_
  36.3 0.6 %shard_grads.6 = (bf16[256,256]{1,0:T(8,128)(2,1)S(1)}, f32[256,256]{1,0:T(8,128)S(1)}, f32[256,256]{1,0:T(8,128)S(1)}) custom-call(bf16[256,256]{1,0:T(8,128)(2,1)S(1)} %collective-permute-done.5.refs_0_, bf16[256,256]{1,0:T(8,128)(2,1)S(1)} %collective-permute-done.7.refs_1_, bf16[256,256]{1,0:T(8,128)(2,1)S(1)} %collective-permute-done.8.refs_2_, ...), custom_call_target="tpu_custom_call" | custom-call | flops 201326592 | tf_op jit(solution)/shard_map/shard_grads/pallas_call | solution.py:78
  36.9 0.0 collective-permute-done.11.refs_4_
  36.9 0.6 %shard_grads.7 = (f32[256,256]{1,0:T(8,128)S(1)}, bf16[256,256]{1,0:T(8,128)(2,1)S(1)}, bf16[256,256]{1,0:T(8,128)(2,1)S(1)}) custom-call(bf16[256,256]{1,0:T(8,128)(2,1)S(1)} %get-tuple-element.50.refs_0_, bf16[256,256]{1,0:T(8,128)(2,1)S(1)} %collective-permute-done.7.refs_1_, bf16[256,256]{1,0:T(8,128)(2,1)S(1)} %collective-permute-done.8.refs_2_, ...), custom_call_target="tpu_custom_call" | custom-call | flops 201326592 | tf_op jit(solution)/shard_map/shard_grads/pallas_call | solution.py:78
  37.5 1.6 %collective-permute-start.12 = (bf16[256,256]{1,0:T(8,128)(2,1)S(1)}, bf16[256,256]{1,0:T(8,128)(2,1)S(1)}, u32[]{:S(2)}, u32[]{:S(2)}) collective-permute-start(bf16[256,256]{1,0:T(8,128)(2,1)S(1)} %get-tuple-element.46), channel_id=1, source_target_pairs={{0,28},{1,29},{2,30},{3,31},{4,0},{5,1},{6,2},{7,3},{8,4},{9,5},{1... | collective-permute-start | bytes 393224 | tf_op jit(solution)/shard_map/ppermute | solution.py:30
  39.1 1.3 %collective-permute-start.13 = (bf16[256,256]{1,0:T(8,128)(2,1)S(1)}, bf16[256,256]{1,0:T(8,128)(2,1)S(1)}, u32[]{:S(2)}, u32[]{:S(2)}) collective-permute-start(bf16[256,256]{1,0:T(8,128)(2,1)S(1)} %get-tuple-element.47), channel_id=1, source_target_pairs={{0,29},{1,28},{2,31},{3,30},{4,1},{5,0},{6,3},{7,2},{8,5},{9,4},{1... | collective-permute-start | bytes 393224 | tf_op jit(solution)/shard_map/ppermute | solution.py:30
  40.5 2.1 %collective-permute-start.10 = (bf16[256,256]{1,0:T(8,128)(2,1)S(1)}, bf16[256,256]{1,0:T(8,128)(2,1)S(1)}, u32[]{:S(2)}, u32[]{:S(2)}) collective-permute-start(bf16[256,256]{1,0:T(8,128)(2,1)S(1)} %get-tuple-element.40), channel_id=1, source_target_pairs={{0,2},{1,3},{2,0},{3,1},{4,6},{5,7},{6,4},{7,5},{8,10},{9,11},{10,... | collective-permute-start | bytes 393224 | tf_op jit(solution)/shard_map/ppermute | solution.py:24
  42.5 0.0 collective-permute-done.12.refs_2_
  42.5 4.6 %collective-permute-done.13.refs_3_ = bf16[256,256]{1,0:T(8,128)(2,1)S(1)} collective-permute-done((bf16[256,256]{1,0:T(8,128)(2,1)S(1)}, bf16[256,256]{1,0:T(8,128)(2,1)S(1)}, u32[]{:S(2)}, u32[]{:S(2)}) %collective-permute-start.13) | collective-permute-done | bytes 131104 | tf_op jit(solution)/shard_map/ppermute | solution.py:30
  47.1 0.8 %last_update.3 = f32[256,256]{1,0:T(8,128)} custom-call(f32[256,256]{1,0:T(8,128)S(1)} %get-tuple-element.49.refs_0_, f32[256,256]{1,0:T(8,128)S(1)} %get-tuple-element.52.refs_1_, bf16[256,256]{1,0:T(8,128)(2,1)S(1)} %collective-permute-done.12.refs_2_, bf16[256,256]{1,0:T(8,128)(2,1)S(1)} %collective-permute-done.13.refs_3_), custom_call_target="tpu_custom_call" | custom-call | tf_op jit(solution)/shard_map/last_update/pallas_call | solution.py:228
  48.0 1.5 %collective-permute-done.10.refs_2_ = bf16[256,256]{1,0:T(8,128)(2,1)S(1)} collective-permute-done((bf16[256,256]{1,0:T(8,128)(2,1)S(1)}, bf16[256,256]{1,0:T(8,128)(2,1)S(1)}, u32[]{:S(2)}, u32[]{:S(2)}) %collective-permute-start.10) | collective-permute-done | bytes 131104 | tf_op jit(solution)/shard_map/ppermute | solution.py:24
  49.5 0.8 %last_update.2 = f32[256,256]{1,0:T(8,128)} custom-call(f32[256,256]{1,0:T(8,128)S(1)} %get-tuple-element.51.refs_0_, f32[256,256]{1,0:T(8,128)S(1)} %get-tuple-element.53.refs_1_, bf16[256,256]{1,0:T(8,128)(2,1)S(1)} %collective-permute-done.10.refs_2_, f32[256,256]{1,0:T(8,128)S(1)} %get-tuple-element.45.refs_3_), custom_call_target="tpu_custom_call" | custom-call | tf_op jit(solution)/shard_map/last_update/pallas_call | solution.py:228
  (2 shorter events, 0.0 us)
Async XLA Ops:
  1.7 10.3 %collective-permute-start.2 = (bf16[272,256]{1,0:T(8,128)(2,1)S(1)}, bf16[272,256]{1,0:T(8,128)(2,1)S(1)}, u32[]{:S(2)}, u32[]{:S(2)}) collective-permute-start(bf16[272,256]{1,0:T(8,128)(2,1)S(1)} %get-tuple-element.28), channel_id=1, source_target_pairs={{0,1},{1,0},{2,3},{3,2},{4,5},{5,4},{6,7},{7,6},{8,9},{9,8},{10,11... | collective-permute-start | bytes 417800 | tf_op jit(solution)/shard_map/ppermute | solution.py:24
  5.9 8.7 %collective-permute-start = (bf16[256,256]{1,0:T(8,128)(2,1)S(1)}, bf16[256,256]{1,0:T(8,128)(2,1)S(1)}, u32[]{:S(2)}, u32[]{:S(2)}) collective-permute-start(bf16[256,256]{1,0:T(8,128)(2,1)S(1)} %get-tuple-element.25.refs_0_), channel_id=1, source_target_pairs={{0,2},{1,3},{2,0},{3,1},{4,6},{5,7},{6,4},{7,5},{8,10},{9,11},{10,... | collective-permute-start | bytes 393224 | tf_op jit(solution)/shard_map/ppermute | solution.py:24
  8.6 7.4 %collective-permute-start.1 = (bf16[256,256]{1,0:T(8,128)(2,1)S(1)}, bf16[256,256]{1,0:T(8,128)(2,1)S(1)}, u32[]{:S(2)}, u32[]{:S(2)}) collective-permute-start(bf16[256,256]{1,0:T(8,128)(2,1)S(1)} %get-tuple-element.26.refs_1_), channel_id=1, source_target_pairs={{0,1},{1,0},{2,3},{3,2},{4,5},{5,4},{6,7},{7,6},{8,9},{9,8},{10,11... | collective-permute-start | bytes 393224 | tf_op jit(solution)/shard_map/ppermute | solution.py:24
  9.0 13.6 %copy-start = (f32[256,256]{1,0:T(8,128)S(1)}, f32[256,256]{1,0:T(8,128)}, u32[]{:S(2)}) copy-start(f32[256,256]{1,0:T(8,128)} %refs_1_.1) | copy-start | bytes 786436
  9.0 13.6 %copy-start.2 = (f32[256,256]{1,0:T(8,128)S(1)}, f32[256,256]{1,0:T(8,128)}, u32[]{:S(2)}) copy-start(f32[256,256]{1,0:T(8,128)} %param.7) | copy-start | bytes 786436
  9.0 11.2 %collective-permute-start.4 = (bf16[256,256]{1,0:T(8,128)(2,1)S(1)}, bf16[256,256]{1,0:T(8,128)(2,1)S(1)}, u32[]{:S(2)}, u32[]{:S(2)}) collective-permute-start(bf16[256,256]{1,0:T(8,128)(2,1)S(1)} %get-tuple-element.32), channel_id=1, source_target_pairs={{0,1},{1,0},{2,3},{3,2},{4,5},{5,4},{6,7},{7,6},{8,9},{9,8},{10,11... | collective-permute-start | bytes 393224 | tf_op jit(solution)/shard_map/ppermute | solution.py:24
  12.0 17.2 %copy-start.1 = (f32[256,256]{1,0:T(8,128)S(1)}, f32[256,256]{1,0:T(8,128)}, u32[]{:S(2)}) copy-start(f32[256,256]{1,0:T(8,128)} %refs_0_.2) | copy-start | bytes 786436
  12.0 17.2 %copy-start.3 = (f32[256,256]{1,0:T(8,128)S(1)}, f32[256,256]{1,0:T(8,128)}, u32[]{:S(2)}) copy-start(f32[256,256]{1,0:T(8,128)} %param.9) | copy-start | bytes 786436
  16.5 6.1 %collective-permute-start.3 = (bf16[256,256]{1,0:T(8,128)(2,1)S(1)}, bf16[256,256]{1,0:T(8,128)(2,1)S(1)}, u32[]{:S(2)}, u32[]{:S(2)}) collective-permute-start(bf16[256,256]{1,0:T(8,128)(2,1)S(1)} %get-tuple-element.30), channel_id=1, source_target_pairs={{0,2},{1,3},{2,0},{3,1},{4,6},{5,7},{6,4},{7,5},{8,10},{9,11},{10,... | collective-permute-start | bytes 393224 | tf_op jit(solution)/shard_map/ppermute | solution.py:24
  18.7 13.9 %collective-permute-start.9 = (bf16[256,256]{1,0:T(8,128)(2,1)S(1)}, bf16[256,256]{1,0:T(8,128)(2,1)S(1)}, u32[]{:S(2)}, u32[]{:S(2)}) collective-permute-start(bf16[256,256]{1,0:T(8,128)(2,1)S(1)} %get-tuple-element.39), channel_id=1, source_target_pairs={{0,1},{1,0},{2,3},{3,2},{4,5},{5,4},{6,7},{7,6},{8,9},{9,8},{10,11... | collective-permute-start | bytes 393224 | tf_op jit(solution)/shard_map/ppermute | solution.py:24
  20.8 8.4 %collective-permute-start.6 = (bf16[256,256]{1,0:T(8,128)(2,1)S(1)}, bf16[256,256]{1,0:T(8,128)(2,1)S(1)}, u32[]{:S(2)}, u32[]{:S(2)}) collective-permute-start(bf16[256,256]{1,0:T(8,128)(2,1)S(1)} %get-tuple-element.37), channel_id=1, source_target_pairs={{0,1},{1,0},{2,3},{3,2},{4,5},{5,4},{6,7},{7,6},{8,9},{9,8},{10,11... | collective-permute-start | bytes 393224 | tf_op jit(solution)/shard_map/ppermute | solution.py:24
  22.9 9.7 %collective-permute-start.5 = (bf16[256,256]{1,0:T(8,128)(2,1)S(1)}, bf16[256,256]{1,0:T(8,128)(2,1)S(1)}, u32[]{:S(2)}, u32[]{:S(2)}) collective-permute-start(bf16[256,256]{1,0:T(8,128)(2,1)S(1)} %get-tuple-element.50.refs_0_), channel_id=1, source_target_pairs={{0,2},{1,3},{2,0},{3,1},{4,6},{5,7},{6,4},{7,5},{8,10},{9,11},{10,... | collective-permute-start | bytes 393224 | tf_op jit(solution)/shard_map/ppermute | solution.py:24
  29.4 6.8 %collective-permute-start.8 = (bf16[256,256]{1,0:T(8,128)(2,1)S(1)}, bf16[256,256]{1,0:T(8,128)(2,1)S(1)}, u32[]{:S(2)}, u32[]{:S(2)}) collective-permute-start(bf16[256,256]{1,0:T(8,128)(2,1)S(1)} %get-tuple-element.48), channel_id=1, source_target_pairs={{0,5},{1,4},{2,7},{3,6},{4,9},{5,8},{6,11},{7,10},{8,13},{9,12},{1... | collective-permute-start | bytes 393224 | tf_op jit(solution)/shard_map/ppermute | solution.py:30
  29.5 6.8 %collective-permute-start.7 = (bf16[256,256]{1,0:T(8,128)(2,1)S(1)}, bf16[256,256]{1,0:T(8,128)(2,1)S(1)}, u32[]{:S(2)}, u32[]{:S(2)}) collective-permute-start(bf16[256,256]{1,0:T(8,128)(2,1)S(1)} %get-tuple-element.48), channel_id=1, source_target_pairs={{0,4},{1,5},{2,6},{3,7},{4,8},{5,9},{6,10},{7,11},{8,12},{9,13},{1... | collective-permute-start | bytes 393224 | tf_op jit(solution)/shard_map/ppermute | solution.py:30
  30.3 6.6 %collective-permute-start.11 = (bf16[256,256]{1,0:T(8,128)(2,1)S(1)}, bf16[256,256]{1,0:T(8,128)(2,1)S(1)}, u32[]{:S(2)}, u32[]{:S(2)}) collective-permute-start(bf16[256,256]{1,0:T(8,128)(2,1)S(1)} %get-tuple-element.42), channel_id=1, source_target_pairs={{0,1},{1,0},{2,3},{3,2},{4,5},{5,4},{6,7},{7,6},{8,9},{9,8},{10,11... | collective-permute-start | bytes 393224 | tf_op jit(solution)/shard_map/ppermute | solution.py:24
  37.5 5.0 %collective-permute-start.12 = (bf16[256,256]{1,0:T(8,128)(2,1)S(1)}, bf16[256,256]{1,0:T(8,128)(2,1)S(1)}, u32[]{:S(2)}, u32[]{:S(2)}) collective-permute-start(bf16[256,256]{1,0:T(8,128)(2,1)S(1)} %get-tuple-element.46), channel_id=1, source_target_pairs={{0,28},{1,29},{2,30},{3,31},{4,0},{5,1},{6,2},{7,3},{8,4},{9,5},{1... | collective-permute-start | bytes 393224 | tf_op jit(solution)/shard_map/ppermute | solution.py:30
  39.1 8.0 %collective-permute-start.13 = (bf16[256,256]{1,0:T(8,128)(2,1)S(1)}, bf16[256,256]{1,0:T(8,128)(2,1)S(1)}, u32[]{:S(2)}, u32[]{:S(2)}) collective-permute-start(bf16[256,256]{1,0:T(8,128)(2,1)S(1)} %get-tuple-element.47), channel_id=1, source_target_pairs={{0,29},{1,28},{2,31},{3,30},{4,1},{5,0},{6,3},{7,2},{8,5},{9,4},{1... | collective-permute-start | bytes 393224 | tf_op jit(solution)/shard_map/ppermute | solution.py:30
  40.5 9.0 %collective-permute-start.10 = (bf16[256,256]{1,0:T(8,128)(2,1)S(1)}, bf16[256,256]{1,0:T(8,128)(2,1)S(1)}, u32[]{:S(2)}, u32[]{:S(2)}) collective-permute-start(bf16[256,256]{1,0:T(8,128)(2,1)S(1)} %get-tuple-element.40), channel_id=1, source_target_pairs={{0,2},{1,3},{2,0},{3,1},{4,6},{5,7},{6,4},{7,5},{8,10},{9,11},{10,... | collective-permute-start | bytes 393224 | tf_op jit(solution)/shard_map/ppermute | solution.py:24

commit v4 on v3

--- a/solution.py
+++ b/solution.py
@@ -34,61 +34,62 @@
     return lax.dot_general(a, b, (((ca,), (cb,)), ((), ())), preferred_element_type=F32)
 
 
-def shard_kernel(k, first_tile, side, carried, *refs):
-    if carried:
-        u, near, far, rate_near, rate_far, seen_near, seen_far, near_in, far_in = refs[:9]
-    else:
-        u, near, far, rate_near, rate_far, seen_near, seen_far = refs[:7]
-    part, near_out, far_out = refs[-3:]
+def tile_errors(k, first_tile, side, u, items, rates, seen):
     rows = u.shape[0]
     shard = lax.rem(lax.axis_index("item") + 2 * k, lax.axis_size("item"))
     chunk = min(rows, side)
-
-    def errors(items, rates, seen):
-        tiles, cols = seen.shape
-        masks = seen[...].astype(F32)
-        at = lax.broadcasted_iota(jnp.int32, (tiles, cols), 0)
-        bands = []
-        for t in range(0, rows, chunk):
-            tile = first_tile + (shard * rows + t) // side
-            row = jnp.sum(jnp.where(at == tile, masks, 0.0), axis=0, keepdims=True)
-            bands.append(jnp.broadcast_to(row, (chunk, cols)))
-        observed = jnp.concatenate(bands, axis=0) if len(bands) > 1 else bands[0]
-        logits = dot(u[...], items[...], 1, 1)
-        return (observed * (jax.nn.sigmoid(logits) - rates[...].astype(F32))).astype(BF)
-
-    e_near = errors(near, rate_near, seen_near)
-    e_far = errors(far, rate_far, seen_far)
-    part[...] = (dot(e_near, near[...], 1, 0) + dot(e_far, far[...], 1, 0)).astype(part.dtype)
-    g_near = dot(e_near, u[...], 0, 0)
-    g_far = dot(e_far, u[...], 0, 0)
-    if carried:
-        g_near = g_near + near_in[...]
-        g_far = g_far + far_in[...]
-    near_out[...] = g_near.astype(near_out.dtype)
-    far_out[...] = g_far.astype(far_out.dtype)
-
-
-def shard_grads(k, first_tile, side, part_type, item_types, args, carry):
-    u, near = args[0], args[1]
-    rows, rank = u.shape
-    cols = near.shape[0]
+    tiles, cols = seen.shape
+    masks = seen[...].astype(F32)
+    at = lax.broadcasted_iota(jnp.int32, (tiles, cols), 0)
+    out = []
+    for t in range(0, rows, chunk):
+        tile = first_tile + (shard * rows + t) // side
+        row = jnp.sum(jnp.where(at == tile, masks, 0.0), axis=0, keepdims=True)
+        here = pl.ds(t, chunk)
+        logits = dot(u[here, :], items[...], 1, 1)
+        out.append((row * (jax.nn.sigmoid(logits) - rates[here, :].astype(F32))).astype(BF))
+    return jnp.concatenate(out, axis=0) if len(out) > 1 else out[0]
+
+
+def near_kernel(group, first_tile, side, *refs):
+    shards, rates = refs[:group], refs[group : 2 * group]
+    near, seen = refs[2 * group : 2 * group + 2]
+    parts, grad = refs[2 * group + 2 : -1], refs[-1]
+    total = None
+    for k in range(group):
+        errors = tile_errors(k, first_tile, side, shards[k], near, rates[k], seen)
+        parts[k][...] = dot(errors, near[...], 1, 0)
+        share = dot(errors, shards[k][...], 0, 0)
+        total = share if total is None else total + share
+    grad[...] = total.astype(grad.dtype)
+
+
+def far_kernel(k, first_tile, side, *refs):
+    u, far, rates, seen, part_in = refs[:5]
+    carried, (part, grad) = refs[5:-2], refs[-2:]
+    errors = tile_errors(k, first_tile, side, u, far, rates, seen)
+    part[...] = (part_in[...] + dot(errors, far[...], 1, 0)).astype(part.dtype)
+    share = dot(errors, u[...], 0, 0)
+    for before in carried:
+        share = share + before[...]
+    grad[...] = share.astype(grad.dtype)
+
+
+def tile_call(kernel, tiles, operands, out_shape):
+    rows, rank = operands[0].shape
+    cols = out_shape[-1].shape[0]
     spec = pl.BlockSpec(memory_space=pltpu.VMEM)
-    operands = args + carry
-    return pl.pallas_call(
-        functools.partial(shard_kernel, k, first_tile, side, bool(carry)),
-        out_shape=(
-            jax.ShapeDtypeStruct((rows, rank), part_type),
-            jax.ShapeDtypeStruct((cols, rank), item_types[0]),
-            jax.ShapeDtypeStruct((cols, rank), item_types[1]),
+    return pl.pallas_call(
+        kernel,
+        out_shape=out_shape,
+        in_specs=[spec] * len(operands),
+        out_specs=(spec,) * len(out_shape),
+        compiler_params=SMALL,
+        cost_estimate=pl.CostEstimate(
+            flops=6 * tiles * rows * cols * rank,
+            bytes_accessed=0,
+            transcendentals=2 * tiles * rows * cols,
         ),
-        in_specs=[spec] * len(operands),
-        out_specs=(spec,) * 3,
-        compiler_params=SMALL,
-        cost_estimate=pl.CostEstimate(
-            flops=12 * rows * cols * rank, bytes_accessed=0, transcendentals=2 * rows * cols
-        ),
-        name="shard_grads",
     )(*operands)
 
 
@@ -237,8 +238,8 @@
 
 
 def body(users, user_accum, items, item_accum, ratings, tile_mask):
-    strata, block_users, _ = ratings.shape
-    rows, _ = users.shape
+    strata, block_users, cols = ratings.shape
+    rows, rank = users.shape
     n = lax.axis_size("item")
     group = n // 2
     tiles = tile_mask.shape[1]
@@ -273,26 +274,33 @@
             items_bf = items.astype(BF)
             near = move(items_bf, s, lambda i: i)
             far = move(items_bf, s, lambda i: i ^ 1)
+        block = jax.ShapeDtypeStruct
+        *parts, g_near = tile_call(
+            functools.partial(near_kernel, group, s * tiles, side),
+            group,
+            [shards[k] for k in range(group)]
+            + [rates[s, k][0] for k in range(group)]
+            + [near, wide],
+            (block((rows, rank), F32),) * group + (block((cols, rank), BF if s else F32),),
+        )
+        if s:
+            g_near = move(g_near, -s, lambda i: i)
         user_shares = []
-        carry = ()
+        carry = []
         for k in order:
-            last = k == order[-1]
-            part, g_near, g_far = shard_grads(
-                k,
-                s * tiles,
-                side,
-                BF if k else F32,
-                (BF if last and s else F32, BF if last else F32),
-                (shards[k], near, far, *rates[s, k], wide, far_wide),
-                carry,
+            part, g_far = tile_call(
+                functools.partial(far_kernel, k, s * tiles, side),
+                1,
+                [shards[k], far, rates[s, k][1], far_wide, parts[k]] + carry,
+                (
+                    block((rows, rank), BF if k else F32),
+                    block((cols, rank), BF if k == order[-1] else F32),
+                ),
             )
-            carry = (g_near, g_far)
+            carry = [g_far]
             if k:
                 part = move(part, 0, lambda i: (i + 2 * k) % n)
             user_shares.append(part)
-        g_near, g_far = carry
-        if s:
-            g_near = move(g_near, -s, lambda i: i)
         g_far = move(g_far, -s, lambda i: i ^ 1)
         if s == strata - 1:
             users = last_update(users, user_accum, *user_shares)

time: 50.5 us -> 50 us (0.990)
  starting transfers between devices: 23.6 us -> 22 us
  Pallas kernels: 7.55 us -> 8.46 us
    ppermute x4, waiting for transfers between devices: 8.28 us -> 5 us  [move(): return lax.ppermute(array, ('user', 'item'), pairs)]
    ppermute x10, waiting for transfers between devices: 9.73 us -> 12.8 us  [move(): lax.ppermute(array, 'item', [(z, item_map(z)) for z in range(n_item)])]
    ppermute x10, starting transfers between devices: 19.7 us -> 16.9 us  [move(): lax.ppermute(array, 'item', [(z, item_map(z)) for z in range(n_item)])]
    ppermute x4, starting transfers between devices: 3.84 us -> 5.03 us  [move(): return lax.ppermute(array, ('user', 'item'), pairs)]
    pallas_call x4 -> x6, Pallas kernels: 2.33 us -> 3.23 us  [tile_call(): pl.pallas_call(kernel, out_shape=out_shape, in_specs=[spec] * len(operand...]
  transfers between devices with their start and end apart: 14 -> 14, of which waited for: 7 -> 10; matrix products, arithmetic and copies ran while one was open for 1% -> 1% of each run, Pallas kernels for 10% -> 13%
where the time goes in v4:
time: 50 us; the launch traced here: 49.3 us
  starting transfers between devices  22 us (44%)
  waiting for transfers between devices  17.8 us (36%)
  Pallas kernels  8.46 us (17%)
  between operations  0.75 us (2%)
    ppermute x10, starting transfers between devices, move(): lax.ppermute(array, 'item', [(z, item_map(z)) for z in range(n_item)])  16.9 us
    ppermute x10, waiting for transfers between devices, move(): lax.ppermute(array, 'item', [(z, item_map(z)) for z in range(n_item)])  12.8 us
    ppermute x4, starting transfers between devices, move(): return lax.ppermute(array, ('user', 'item'), pairs)  5.03 us
    ppermute x4, waiting for transfers between devices, move(): return lax.ppermute(array, ('user', 'item'), pairs)  5 us
    pallas_call x6, Pallas kernels, tile_call(): pl.pallas_call(kernel, out_shape=out_shape, in_specs=[spec] * len(operand...  3.23 us
    pallas_call x2, Pallas kernels, last_update(): pl.pallas_call(functools.partial(last_kernel, count), out_shape=jax.Shape...  1.67 us
    pallas_call x1, Pallas kernels, rest_of_ratings(): pl.pallas_call(functools.partial(rest_kernel, picks, rows), out_shape=(ja...  1.41 us
    pallas_call x1, Pallas kernels, first_sends(): pl.pallas_call(functools.partial(first_kernel, group, rows, side), out_sh...  1.08 us
  transfers between devices with their start and end apart: 14, of which 10 were waited for; matrix products, arithmetic and copies ran while one was open for 1% of the time, Pallas kernels for 13%

profile of v4, /device:TPU:0, one launch (start us, length us, event | category | flops | bytes accessed | tf_op | source)
XLA Modules:
  0.0 49.3 jit_solution(11953662106969124006)
XLA Ops:
  0.6 1.1 %first_rows.1 = (bf16[256,256]{1,0:T(8,128)(2,1)S(1)}, bf16[256,256]{1,0:T(8,128)(2,1)S(1)}) custom-call(f32[256,256]{1,0:T(8,128)} %refs_0_.2, f32[256,256]{1,0:T(8,128)} %refs_1_.1), custom_call_target="tpu_custom_call" | custom-call | tf_op jit(solution)/shard_map/first_rows/pallas_call | solution.py:120
  1.7 4.1 %collective-permute-start = (bf16[256,256]{1,0:T(8,128)(2,1)S(1)}, bf16[256,256]{1,0:T(8,128)(2,1)S(1)}, u32[]{:S(2)}, u32[]{:S(2)}) collective-permute-start(bf16[256,256]{1,0:T(8,128)(2,1)S(1)} %get-tuple-element.27.refs_0_), channel_id=1, source_target_pairs={{0,2},{1,3},{2,0},{3,1},{4,6},{5,7},{6,4},{7,5},{8,10},{9,11},{10,... | collective-permute-start | bytes 393224 | tf_op jit(solution)/shard_map/ppermute | solution.py:24
  5.8 1.1 %first_sends.1 = (f32[16,256]{1,0:T(8,128)S(1)}, bf16[272,256]{1,0:T(8,128)(2,1)S(1)}, bf16[256,256]{1,0:T(8,128)(2,1)S(1)}) custom-call(s32[2,1024,256]{2,1,0:T(8,128)} %ratings.1, s32[2,2,8]{2,1,0:T(2,128)} %bitcast.1), custom_call_target="tpu_custom_call" | custom-call | tf_op jit(solution)/shard_map/first_sends/pallas_call | solution.py:168
  6.9 1.6 %collective-permute-start.2 = (bf16[272,256]{1,0:T(8,128)(2,1)S(1)}, bf16[272,256]{1,0:T(8,128)(2,1)S(1)}, u32[]{:S(2)}, u32[]{:S(2)}) collective-permute-start(bf16[272,256]{1,0:T(8,128)(2,1)S(1)} %get-tuple-element.29), channel_id=1, source_target_pairs={{0,1},{1,0},{2,3},{3,2},{4,5},{5,4},{6,7},{7,6},{8,9},{9,8},{10,11... | collective-permute-start | bytes 417800 | tf_op jit(solution)/shard_map/ppermute | solution.py:24
  8.6 0.4 collective-permute-start.1
  9.0 0.0 copy-start
  9.0 0.0 copy-start.2
  9.0 1.6 %collective-permute-start.4 = (bf16[256,256]{1,0:T(8,128)(2,1)S(1)}, bf16[256,256]{1,0:T(8,128)(2,1)S(1)}, u32[]{:S(2)}, u32[]{:S(2)}) collective-permute-start(bf16[256,256]{1,0:T(8,128)(2,1)S(1)} %get-tuple-element.35), channel_id=1, source_target_pairs={{0,1},{1,0},{2,3},{3,2},{4,5},{5,4},{6,7},{7,6},{8,9},{9,8},{10,11... | collective-permute-start | bytes 393224 | tf_op jit(solution)/shard_map/ppermute | solution.py:24
  10.6 1.4 %rest_of_ratings.1 = (bf16[256,256]{1,0:T(8,128)(2,1)S(1)}, bf16[256,256]{1,0:T(8,128)(2,1)S(1)}, bf16[256,256]{1,0:T(8,128)(2,1)S(1)}, bf16[256,256]{1,0:T(8,12...) custom-call(s32[2,1024,256]{2,1,0:T(8,128)} %ratings.1), custom_call_target="tpu_custom_call" | custom-call | tf_op jit(solution)/shard_map/rest_of_ratings/pallas_call | solution.py:196
  12.0 0.2 collective-permute-done.refs_1_.refs_0_
  12.2 0.0 copy-start.1
  12.2 0.7 %shard_map.77 = (f32[256,256]{1,0:T(8,128)S(1)}, f32[256,256]{1,0:T(8,128)S(1)}, f32[256,256]{1,0:T(8,128)S(1)}) custom-call(bf16[256,256]{1,0:T(8,128)(2,1)S(1)} %get-tuple-element.27.refs_0_, bf16[256,256]{1,0:T(8,128)(2,1)S(1)} %collective-permute-done.refs_1_.refs_0_, bf16[256,256]{1,0:T(8,128)(2,1)S(1)} %get-tuple-element.30.refs_2_, ...), custom_call_target="tpu_custom_call" | custom-call | flops 201326592 | tf_op jit(solution)/shard_map/pallas_call | solution.py:82
  12.9 1.7 %collective-permute-done.2 = bf16[272,256]{1,0:T(8,128)(2,1)S(1)} collective-permute-done((bf16[272,256]{1,0:T(8,128)(2,1)S(1)}, bf16[272,256]{1,0:T(8,128)(2,1)S(1)}, u32[]{:S(2)}, u32[]{:S(2)}) %collective-permute-start.2) | collective-permute-done | bytes 139296 | tf_op jit(solution)/shard_map/ppermute | solution.py:24
  14.6 2.8 %collective-permute-done.1.refs_1_ = bf16[256,256]{1,0:T(8,128)(2,1)S(1)} collective-permute-done((bf16[256,256]{1,0:T(8,128)(2,1)S(1)}, bf16[256,256]{1,0:T(8,128)(2,1)S(1)}, u32[]{:S(2)}, u32[]{:S(2)}) %collective-permute-start.1) | collective-permute-done | bytes 131104 | tf_op jit(solution)/shard_map/ppermute | solution.py:24
  17.4 0.5 shard_map.78
  17.9 1.1 %collective-permute-start.3 = (bf16[256,256]{1,0:T(8,128)(2,1)S(1)}, bf16[256,256]{1,0:T(8,128)(2,1)S(1)}, u32[]{:S(2)}, u32[]{:S(2)}) collective-permute-start(bf16[256,256]{1,0:T(8,128)(2,1)S(1)} %get-tuple-element.34), channel_id=1, source_target_pairs={{0,2},{1,3},{2,0},{3,1},{4,6},{5,7},{6,4},{7,5},{8,10},{9,11},{10,... | collective-permute-start | bytes 393224 | tf_op jit(solution)/shard_map/ppermute | solution.py:24
  19.0 0.4 collective-permute-done.4.refs_2_
  19.4 0.5 shard_map.79
  19.8 2.2 %collective-permute-start.6 = (bf16[256,256]{1,0:T(8,128)(2,1)S(1)}, bf16[256,256]{1,0:T(8,128)(2,1)S(1)}, u32[]{:S(2)}, u32[]{:S(2)}) collective-permute-start(bf16[256,256]{1,0:T(8,128)(2,1)S(1)} %get-tuple-element.40), channel_id=1, source_target_pairs={{0,1},{1,0},{2,3},{3,2},{4,5},{5,4},{6,7},{7,6},{8,9},{9,8},{10,11... | collective-permute-start | bytes 393224 | tf_op jit(solution)/shard_map/ppermute | solution.py:24
  22.0 3.2 %collective-permute-done.3 = bf16[256,256]{1,0:T(8,128)(2,1)S(1)} collective-permute-done((bf16[256,256]{1,0:T(8,128)(2,1)S(1)}, bf16[256,256]{1,0:T(8,128)(2,1)S(1)}, u32[]{:S(2)}, u32[]{:S(2)}) %collective-permute-start.3) | collective-permute-done | bytes 131104 | tf_op jit(solution)/shard_map/ppermute | solution.py:24
  25.2 0.0 copy-done
  25.2 0.0 copy-done.2
  25.2 0.2 fusion.1
  25.4 0.7 %collective-permute-start.5 = (bf16[256,256]{1,0:T(8,128)(2,1)S(1)}, bf16[256,256]{1,0:T(8,128)(2,1)S(1)}, u32[]{:S(2)}, u32[]{:S(2)}) collective-permute-start(bf16[256,256]{1,0:T(8,128)(2,1)S(1)} %get-tuple-element.54.refs_0_), channel_id=1, source_target_pairs={{0,2},{1,3},{2,0},{3,1},{4,6},{5,7},{6,4},{7,5},{8,10},{9,11},{10,... | collective-permute-start | bytes 393224 | tf_op jit(solution)/shard_map/ppermute | solution.py:24
  26.1 1.0 %collective-permute-done.6 = bf16[256,256]{1,0:T(8,128)(2,1)S(1)} collective-permute-done((bf16[256,256]{1,0:T(8,128)(2,1)S(1)}, bf16[256,256]{1,0:T(8,128)(2,1)S(1)}, u32[]{:S(2)}, u32[]{:S(2)}) %collective-permute-start.6) | collective-permute-done | bytes 131104 | tf_op jit(solution)/shard_map/ppermute | solution.py:24
  27.1 0.0 copy-done.1
  27.1 0.0 copy-done.3
  27.1 0.2 fusion
  27.2 0.1 collective-permute-start.9
  27.3 3.2 %collective-permute-start.8 = (bf16[256,256]{1,0:T(8,128)(2,1)S(1)}, bf16[256,256]{1,0:T(8,128)(2,1)S(1)}, u32[]{:S(2)}, u32[]{:S(2)}) collective-permute-start(bf16[256,256]{1,0:T(8,128)(2,1)S(1)} %get-tuple-element.41), channel_id=1, source_target_pairs={{0,1},{1,0},{2,3},{3,2},{4,5},{5,4},{6,7},{7,6},{8,9},{9,8},{10,11... | collective-permute-start | bytes 393224 | tf_op jit(solution)/shard_map/ppermute | solution.py:24
  30.5 1.1 %collective-permute-start.7 = (bf16[256,256]{1,0:T(8,128)(2,1)S(1)}, bf16[256,256]{1,0:T(8,128)(2,1)S(1)}, u32[]{:S(2)}, u32[]{:S(2)}) collective-permute-start(bf16[256,256]{1,0:T(8,128)(2,1)S(1)} %get-tuple-element.52), channel_id=1, source_target_pairs={{0,5},{1,4},{2,7},{3,6},{4,9},{5,8},{6,11},{7,10},{8,13},{9,12},{1... | collective-permute-start | bytes 393224 | tf_op jit(solution)/shard_map/ppermute | solution.py:30
  31.6 1.7 %collective-permute-start.11 = (bf16[256,256]{1,0:T(8,128)(2,1)S(1)}, bf16[256,256]{1,0:T(8,128)(2,1)S(1)}, u32[]{:S(2)}, u32[]{:S(2)}) collective-permute-start(bf16[256,256]{1,0:T(8,128)(2,1)S(1)} %get-tuple-element.46), channel_id=1, source_target_pairs={{0,1},{1,0},{2,3},{3,2},{4,5},{5,4},{6,7},{7,6},{8,9},{9,8},{10,11... | collective-permute-start | bytes 393224 | tf_op jit(solution)/shard_map/ppermute | solution.py:24
  33.4 0.0 collective-permute-done.5.refs_1_.refs_0_
  33.4 0.0 collective-permute-done.9.refs_4_
  33.4 0.7 %shard_map.80 = (f32[256,256]{1,0:T(8,128)S(1)}, f32[256,256]{1,0:T(8,128)S(1)}, bf16[256,256]{1,0:T(8,128)(2,1)S(1)}) custom-call(bf16[256,256]{1,0:T(8,128)(2,1)S(1)} %get-tuple-element.54.refs_0_, bf16[256,256]{1,0:T(8,128)(2,1)S(1)} %collective-permute-done.5.refs_1_.refs_0_, bf16[256,256]{1,0:T(8,128)(2,1)S(1)} %get-tuple-element.42.refs_2_, ...), custom_call_target="tpu_custom_call" | custom-call | flops 201326592 | tf_op jit(solution)/shard_map/pallas_call | solution.py:82
  34.1 0.2 collective-permute-done.8.refs_2_
  34.2 5.0 %collective-permute-done.7.refs_1_ = bf16[256,256]{1,0:T(8,128)(2,1)S(1)} collective-permute-done((bf16[256,256]{1,0:T(8,128)(2,1)S(1)}, bf16[256,256]{1,0:T(8,128)(2,1)S(1)}, u32[]{:S(2)}, u32[]{:S(2)}) %collective-permute-start.7) | collective-permute-done | bytes 131104 | tf_op jit(solution)/shard_map/ppermute | solution.py:30
  39.2 0.5 shard_map.81
  39.7 0.2 collective-permute-start.10
  39.9 0.6 %collective-permute-done.11.refs_2_ = bf16[256,256]{1,0:T(8,128)(2,1)S(1)} collective-permute-done((bf16[256,256]{1,0:T(8,128)(2,1)S(1)}, bf16[256,256]{1,0:T(8,128)(2,1)S(1)}, u32[]{:S(2)}, u32[]{:S(2)}) %collective-permute-start.11) | collective-permute-done | bytes 131104 | tf_op jit(solution)/shard_map/ppermute | solution.py:24
  40.5 0.5 shard_map.82
  41.0 2.7 %collective-permute-start.13 = (bf16[256,256]{1,0:T(8,128)(2,1)S(1)}, bf16[256,256]{1,0:T(8,128)(2,1)S(1)}, u32[]{:S(2)}, u32[]{:S(2)}) collective-permute-start(bf16[256,256]{1,0:T(8,128)(2,1)S(1)} %get-tuple-element.51), channel_id=1, source_target_pairs={{0,29},{1,28},{2,31},{3,30},{4,1},{5,0},{6,3},{7,2},{8,5},{9,4},{1... | collective-permute-start | bytes 393224 | tf_op jit(solution)/shard_map/ppermute | solution.py:30
  43.7 1.1 %collective-permute-start.12 = (bf16[256,256]{1,0:T(8,128)(2,1)S(1)}, bf16[256,256]{1,0:T(8,128)(2,1)S(1)}, u32[]{:S(2)}, u32[]{:S(2)}) collective-permute-start(bf16[256,256]{1,0:T(8,128)(2,1)S(1)} %get-tuple-element.50), channel_id=1, source_target_pairs={{0,28},{1,29},{2,30},{3,31},{4,0},{5,1},{6,2},{7,3},{8,4},{9,5},{1... | collective-permute-start | bytes 393224 | tf_op jit(solution)/shard_map/ppermute | solution.py:30
  44.8 2.8 %collective-permute-done.10.refs_2_ = bf16[256,256]{1,0:T(8,128)(2,1)S(1)} collective-permute-done((bf16[256,256]{1,0:T(8,128)(2,1)S(1)}, bf16[256,256]{1,0:T(8,128)(2,1)S(1)}, u32[]{:S(2)}, u32[]{:S(2)}) %collective-permute-start.10) | collective-permute-done | bytes 131104 | tf_op jit(solution)/shard_map/ppermute | solution.py:24
  47.6 0.8 %last_update.2 = f32[256,256]{1,0:T(8,128)} custom-call(f32[256,256]{1,0:T(8,128)S(1)} %get-tuple-element.55.refs_0_, f32[256,256]{1,0:T(8,128)S(1)} %get-tuple-element.57.refs_1_, bf16[256,256]{1,0:T(8,128)(2,1)S(1)} %collective-permute-done.10.refs_2_, f32[256,256]{1,0:T(8,128)S(1)} %get-tuple-element.49.refs_3_), custom_call_target="tpu_custom_call" | custom-call | tf_op jit(solution)/shard_map/last_update/pallas_call | solution.py:229
  48.4 0.0 collective-permute-done.13.refs_3_
  48.4 0.0 collective-permute-done.12.refs_2_
  48.5 0.8 %last_update.3 = f32[256,256]{1,0:T(8,128)} custom-call(f32[256,256]{1,0:T(8,128)S(1)} %get-tuple-element.53.refs_0_, f32[256,256]{1,0:T(8,128)S(1)} %get-tuple-element.56.refs_1_, bf16[256,256]{1,0:T(8,128)(2,1)S(1)} %collective-permute-done.12.refs_2_, bf16[256,256]{1,0:T(8,128)(2,1)S(1)} %collective-permute-done.13.refs_3_), custom_call_target="tpu_custom_call" | custom-call | tf_op jit(solution)/shard_map/last_update/pallas_call | solution.py:229
  (3 shorter events, 0.0 us)
Async XLA Ops:
  1.7 10.5 %collective-permute-start = (bf16[256,256]{1,0:T(8,128)(2,1)S(1)}, bf16[256,256]{1,0:T(8,128)(2,1)S(1)}, u32[]{:S(2)}, u32[]{:S(2)}) collective-permute-start(bf16[256,256]{1,0:T(8,128)(2,1)S(1)} %get-tuple-element.27.refs_0_), channel_id=1, source_target_pairs={{0,2},{1,3},{2,0},{3,1},{4,6},{5,7},{6,4},{7,5},{8,10},{9,11},{10,... | collective-permute-start | bytes 393224 | tf_op jit(solution)/shard_map/ppermute | solution.py:24
  6.9 7.7 %collective-permute-start.2 = (bf16[272,256]{1,0:T(8,128)(2,1)S(1)}, bf16[272,256]{1,0:T(8,128)(2,1)S(1)}, u32[]{:S(2)}, u32[]{:S(2)}) collective-permute-start(bf16[272,256]{1,0:T(8,128)(2,1)S(1)} %get-tuple-element.29), channel_id=1, source_target_pairs={{0,1},{1,0},{2,3},{3,2},{4,5},{5,4},{6,7},{7,6},{8,9},{9,8},{10,11... | collective-permute-start | bytes 417800 | tf_op jit(solution)/shard_map/ppermute | solution.py:24
  8.6 8.9 %collective-permute-start.1 = (bf16[256,256]{1,0:T(8,128)(2,1)S(1)}, bf16[256,256]{1,0:T(8,128)(2,1)S(1)}, u32[]{:S(2)}, u32[]{:S(2)}) collective-permute-start(bf16[256,256]{1,0:T(8,128)(2,1)S(1)} %get-tuple-element.28.refs_4_), channel_id=1, source_target_pairs={{0,1},{1,0},{2,3},{3,2},{4,5},{5,4},{6,7},{7,6},{8,9},{9,8},{10,11... | collective-permute-start | bytes 393224 | tf_op jit(solution)/shard_map/ppermute | solution.py:24
  9.0 16.2 %copy-start = (f32[256,256]{1,0:T(8,128)S(1)}, f32[256,256]{1,0:T(8,128)}, u32[]{:S(2)}) copy-start(f32[256,256]{1,0:T(8,128)} %refs_1_.1) | copy-start | bytes 786436
  9.0 16.2 %copy-start.2 = (f32[256,256]{1,0:T(8,128)S(1)}, f32[256,256]{1,0:T(8,128)}, u32[]{:S(2)}) copy-start(f32[256,256]{1,0:T(8,128)} %param.7) | copy-start | bytes 786436
  9.0 10.4 %collective-permute-start.4 = (bf16[256,256]{1,0:T(8,128)(2,1)S(1)}, bf16[256,256]{1,0:T(8,128)(2,1)S(1)}, u32[]{:S(2)}, u32[]{:S(2)}) collective-permute-start(bf16[256,256]{1,0:T(8,128)(2,1)S(1)} %get-tuple-element.35), channel_id=1, source_target_pairs={{0,1},{1,0},{2,3},{3,2},{4,5},{5,4},{6,7},{7,6},{8,9},{9,8},{10,11... | collective-permute-start | bytes 393224 | tf_op jit(solution)/shard_map/ppermute | solution.py:24
  12.2 14.8 %copy-start.1 = (f32[256,256]{1,0:T(8,128)S(1)}, f32[256,256]{1,0:T(8,128)}, u32[]{:S(2)}) copy-start(f32[256,256]{1,0:T(8,128)} %refs_0_.2) | copy-start | bytes 786436
  12.2 14.8 %copy-start.3 = (f32[256,256]{1,0:T(8,128)S(1)}, f32[256,256]{1,0:T(8,128)}, u32[]{:S(2)}) copy-start(f32[256,256]{1,0:T(8,128)} %param.9) | copy-start | bytes 786436
  17.9 7.3 %collective-permute-start.3 = (bf16[256,256]{1,0:T(8,128)(2,1)S(1)}, bf16[256,256]{1,0:T(8,128)(2,1)S(1)}, u32[]{:S(2)}, u32[]{:S(2)}) collective-permute-start(bf16[256,256]{1,0:T(8,128)(2,1)S(1)} %get-tuple-element.34), channel_id=1, source_target_pairs={{0,2},{1,3},{2,0},{3,1},{4,6},{5,7},{6,4},{7,5},{8,10},{9,11},{10,... | collective-permute-start | bytes 393224 | tf_op jit(solution)/shard_map/ppermute | solution.py:24
  19.8 7.2 %collective-permute-start.6 = (bf16[256,256]{1,0:T(8,128)(2,1)S(1)}, bf16[256,256]{1,0:T(8,128)(2,1)S(1)}, u32[]{:S(2)}, u32[]{:S(2)}) collective-permute-start(bf16[256,256]{1,0:T(8,128)(2,1)S(1)} %get-tuple-element.40), channel_id=1, source_target_pairs={{0,1},{1,0},{2,3},{3,2},{4,5},{5,4},{6,7},{7,6},{8,9},{9,8},{10,11... | collective-permute-start | bytes 393224 | tf_op jit(solution)/shard_map/ppermute | solution.py:24
  25.4 7.9 %collective-permute-start.5 = (bf16[256,256]{1,0:T(8,128)(2,1)S(1)}, bf16[256,256]{1,0:T(8,128)(2,1)S(1)}, u32[]{:S(2)}, u32[]{:S(2)}) collective-permute-start(bf16[256,256]{1,0:T(8,128)(2,1)S(1)} %get-tuple-element.54.refs_0_), channel_id=1, source_target_pairs={{0,2},{1,3},{2,0},{3,1},{4,6},{5,7},{6,4},{7,5},{8,10},{9,11},{10,... | collective-permute-start | bytes 393224 | tf_op jit(solution)/shard_map/ppermute | solution.py:24
  27.2 6.1 %collective-permute-start.9 = (bf16[256,256]{1,0:T(8,128)(2,1)S(1)}, bf16[256,256]{1,0:T(8,128)(2,1)S(1)}, u32[]{:S(2)}, u32[]{:S(2)}) collective-permute-start(bf16[256,256]{1,0:T(8,128)(2,1)S(1)} %get-tuple-element.52), channel_id=1, source_target_pairs={{0,4},{1,5},{2,6},{3,7},{4,8},{5,9},{6,10},{7,11},{8,12},{9,13},{1... | collective-permute-start | bytes 393224 | tf_op jit(solution)/shard_map/ppermute | solution.py:30
  27.3 6.9 %collective-permute-start.8 = (bf16[256,256]{1,0:T(8,128)(2,1)S(1)}, bf16[256,256]{1,0:T(8,128)(2,1)S(1)}, u32[]{:S(2)}, u32[]{:S(2)}) collective-permute-start(bf16[256,256]{1,0:T(8,128)(2,1)S(1)} %get-tuple-element.41), channel_id=1, source_target_pairs={{0,1},{1,0},{2,3},{3,2},{4,5},{5,4},{6,7},{7,6},{8,9},{9,8},{10,11... | collective-permute-start | bytes 393224 | tf_op jit(solution)/shard_map/ppermute | solution.py:24
  30.5 8.7 %collective-permute-start.7 = (bf16[256,256]{1,0:T(8,128)(2,1)S(1)}, bf16[256,256]{1,0:T(8,128)(2,1)S(1)}, u32[]{:S(2)}, u32[]{:S(2)}) collective-permute-start(bf16[256,256]{1,0:T(8,128)(2,1)S(1)} %get-tuple-element.52), channel_id=1, source_target_pairs={{0,5},{1,4},{2,7},{3,6},{4,9},{5,8},{6,11},{7,10},{8,13},{9,12},{1... | collective-permute-start | bytes 393224 | tf_op jit(solution)/shard_map/ppermute | solution.py:30
  31.6 8.9 %collective-permute-start.11 = (bf16[256,256]{1,0:T(8,128)(2,1)S(1)}, bf16[256,256]{1,0:T(8,128)(2,1)S(1)}, u32[]{:S(2)}, u32[]{:S(2)}) collective-permute-start(bf16[256,256]{1,0:T(8,128)(2,1)S(1)} %get-tuple-element.46), channel_id=1, source_target_pairs={{0,1},{1,0},{2,3},{3,2},{4,5},{5,4},{6,7},{7,6},{8,9},{9,8},{10,11... | collective-permute-start | bytes 393224 | tf_op jit(solution)/shard_map/ppermute | solution.py:24
  39.7 7.9 %collective-permute-start.10 = (bf16[256,256]{1,0:T(8,128)(2,1)S(1)}, bf16[256,256]{1,0:T(8,128)(2,1)S(1)}, u32[]{:S(2)}, u32[]{:S(2)}) collective-permute-start(bf16[256,256]{1,0:T(8,128)(2,1)S(1)} %get-tuple-element.45), channel_id=1, source_target_pairs={{0,2},{1,3},{2,0},{3,1},{4,6},{5,7},{6,4},{7,5},{8,10},{9,11},{10,... | collective-permute-start | bytes 393224 | tf_op jit(solution)/shard_map/ppermute | solution.py:24
  41.0 7.5 %collective-permute-start.13 = (bf16[256,256]{1,0:T(8,128)(2,1)S(1)}, bf16[256,256]{1,0:T(8,128)(2,1)S(1)}, u32[]{:S(2)}, u32[]{:S(2)}) collective-permute-start(bf16[256,256]{1,0:T(8,128)(2,1)S(1)} %get-tuple-element.51), channel_id=1, source_target_pairs={{0,29},{1,28},{2,31},{3,30},{4,1},{5,0},{6,3},{7,2},{8,5},{9,4},{1... | collective-permute-start | bytes 393224 | tf_op jit(solution)/shard_map/ppermute | solution.py:30
  43.7 4.7 %collective-permute-start.12 = (bf16[256,256]{1,0:T(8,128)(2,1)S(1)}, bf16[256,256]{1,0:T(8,128)(2,1)S(1)}, u32[]{:S(2)}, u32[]{:S(2)}) collective-permute-start(bf16[256,256]{1,0:T(8,128)(2,1)S(1)} %get-tuple-element.50), channel_id=1, source_target_pairs={{0,28},{1,29},{2,30},{3,31},{4,0},{5,1},{6,2},{7,3},{8,4},{9,5},{1... | collective-permute-start | bytes 393224 | tf_op jit(solution)/shard_map/ppermute | solution.py:30

commit v5 on v4

--- a/solution.py
+++ b/solution.py
@@ -68,7 +68,10 @@
     u, far, rates, seen, part_in = refs[:5]
     carried, (part, grad) = refs[5:-2], refs[-2:]
     errors = tile_errors(k, first_tile, side, u, far, rates, seen)
-    part[...] = (part_in[...] + dot(errors, far[...], 1, 0)).astype(part.dtype)
+    if k:
+        part[...] = (part_in[...] + dot(errors, far[...], 1, 0)).astype(part.dtype)
+    else:
+        part[...] = errors
     share = dot(errors, u[...], 0, 0)
     for before in carried:
         share = share + before[...]
@@ -153,7 +156,7 @@
     for i, out in enumerate(sent):
         copies[1 + i].wait()
         out[pl.ds(0, rows), :] = scratch[1 + i][...].astype(F32).astype(BF)
-    sent[0][pl.ds(rows, strata * tiles), :] = wide[...].astype(BF)
+    sent[0][pl.ds(rows, tiles), :] = wide[pl.ds(0, tiles), :].astype(BF)
 
 
 def first_sends(ratings, tile_mask, rows, group, side):
@@ -163,7 +166,7 @@
     vmem = pl.BlockSpec(memory_space=pltpu.VMEM)
     out_shape = [
         jax.ShapeDtypeStruct(wide, F32),
-        jax.ShapeDtypeStruct((rows + wide[0], cols), BF),
+        jax.ShapeDtypeStruct((rows + tile_mask.shape[1], cols), BF),
     ] + [jax.ShapeDtypeStruct((rows, cols), BF)] * (group - 1)
     return pl.pallas_call(
         functools.partial(first_kernel, group, rows, side),
@@ -257,12 +260,15 @@
     picks += [(s, k, False) for s in range(strata) for k in order]
     rest = dict(zip(picks, rest_of_ratings(ratings, picks, rows)))
     rest.update({(0, k, True): t for k, t in zip(order, sends)})
-    rates = {}
+    rates, far_wide = {}, {}
     for s in range(strata):
         for k in order:
-            got = move(rest[s, k, True], 0, lambda i: i ^ 1)
-            if s == 0 and k == order[0]:
-                got, far_wide = got[:rows], got[rows:]
+            sent = rest[s, k, True]
+            if s and k == order[0]:
+                sent = jnp.concatenate((sent, wide[s * tiles : (s + 1) * tiles].astype(BF)))
+            got = move(sent, 0, lambda i: i ^ 1)
+            if k == order[0]:
+                got, far_wide[s] = got[:rows], got[rows:]
             rates[s, k] = (rest[s, k, False], got)
 
     for s in range(strata):
@@ -289,17 +295,19 @@
         carry = []
         for k in order:
             part, g_far = tile_call(
-                functools.partial(far_kernel, k, s * tiles, side),
+                functools.partial(far_kernel, k, 0, side),
                 1,
-                [shards[k], far, rates[s, k][1], far_wide, parts[k]] + carry,
+                [shards[k], far, rates[s, k][1], far_wide[s], parts[k]] + carry,
                 (
-                    block((rows, rank), BF if k else F32),
+                    block((rows, rank if k else cols), BF),
                     block((cols, rank), BF if k == order[-1] else F32),
                 ),
             )
             carry = [g_far]
             if k:
                 part = move(part, 0, lambda i: (i + 2 * k) % n)
+            else:
+                part = parts[k] + dot(part, far, 1, 0)
             user_shares.append(part)
         g_far = move(g_far, -s, lambda i: i ^ 1)
         if s == strata - 1:

time: 50 us -> 55 us (1.10)
  waiting for transfers between devices: 17.8 us -> 26.1 us
  starting transfers between devices: 22 us -> 18.8 us
    ppermute x10, waiting for transfers between devices: 12.8 us -> 22.1 us  [move(): lax.ppermute(array, 'item', [(z, item_map(z)) for z in range(n_item)])]
    ppermute x4, starting transfers between devices: 5.03 us -> 2.62 us  [move(): return lax.ppermute(array, ('user', 'item'), pairs)]
    ppermute x4, waiting for transfers between devices: 5 us -> 4.06 us  [move(): return lax.ppermute(array, ('user', 'item'), pairs)]
    ppermute x10, starting transfers between devices: 16.9 us -> 16.1 us  [move(): lax.ppermute(array, 'item', [(z, item_map(z)) for z in range(n_item)])]
  transfers between devices with their start and end apart: 14 -> 14, of which waited for: 10 -> 13; matrix products, arithmetic and copies ran while one was open for 1% -> 1% of each run, Pallas kernels for 13% -> 10%
where the time goes in v5:
time: 55 us; the launch traced here: 54.8 us
  waiting for transfers between devices  26.1 us (47%)
  starting transfers between devices  18.8 us (34%)
  Pallas kernels  8.42 us (15%)
  between operations  0.75 us (1%)
    ppermute x10, waiting for transfers between devices, move(): lax.ppermute(array, 'item', [(z, item_map(z)) for z in range(n_item)])  22.1 us
    ppermute x10, starting transfers between devices, move(): lax.ppermute(array, 'item', [(z, item_map(z)) for z in range(n_item)])  16.1 us
    ppermute x4, waiting for transfers between devices, move(): return lax.ppermute(array, ('user', 'item'), pairs)  4.06 us
    pallas_call x6, Pallas kernels, tile_call(): pl.pallas_call(kernel, out_shape=out_shape, in_specs=[spec] * len(operand...  3.19 us
    ppermute x4, starting transfers between devices, move(): return lax.ppermute(array, ('user', 'item'), pairs)  2.62 us
    pallas_call x2, Pallas kernels, last_update(): pl.pallas_call(functools.partial(last_kernel, count), out_shape=jax.Shape...  1.67 us
    pallas_call x1, Pallas kernels, rest_of_ratings(): pl.pallas_call(functools.partial(rest_kernel, picks, rows), out_shape=(ja...  1.41 us
  transfers between devices with their start and end apart: 14, of which 13 were waited for; matrix products, arithmetic and copies ran while one was open for 1% of the time, Pallas kernels for 10%

profile of v5, /device:TPU:0, one launch (start us, length us, event | category | flops | bytes accessed | tf_op | source)
XLA Modules:
  0.0 54.8 jit_solution(5734753139083869407)
XLA Ops:
  0.6 1.1 %first_rows.1 = (bf16[256,256]{1,0:T(8,128)(2,1)S(1)}, bf16[256,256]{1,0:T(8,128)(2,1)S(1)}) custom-call(f32[256,256]{1,0:T(8,128)} %refs_0_.2, f32[256,256]{1,0:T(8,128)} %refs_1_.1), custom_call_target="tpu_custom_call" | custom-call | tf_op jit(solution)/shard_map/first_rows/pallas_call | solution.py:123
  1.7 4.1 %collective-permute-start = (bf16[256,256]{1,0:T(8,128)(2,1)S(1)}, bf16[256,256]{1,0:T(8,128)(2,1)S(1)}, u32[]{:S(2)}, u32[]{:S(2)}) collective-permute-start(bf16[256,256]{1,0:T(8,128)(2,1)S(1)} %get-tuple-element.27.refs_0_), channel_id=1, source_target_pairs={{0,2},{1,3},{2,0},{3,1},{4,6},{5,7},{6,4},{7,5},{8,10},{9,11},{10,... | collective-permute-start | bytes 393224 | tf_op jit(solution)/shard_map/ppermute | solution.py:24
  5.8 1.1 %first_sends.1 = (f32[16,256]{1,0:T(8,128)S(1)}, bf16[264,256]{1,0:T(8,128)(2,1)S(1)}, bf16[256,256]{1,0:T(8,128)(2,1)S(1)}) custom-call(s32[2,1024,256]{2,1,0:T(8,128)} %ratings.1, s32[2,2,8]{2,1,0:T(2,128)} %bitcast.5), custom_call_target="tpu_custom_call" | custom-call | tf_op jit(solution)/shard_map/first_sends/pallas_call | solution.py:171
  6.9 1.6 %collective-permute-start.2 = (bf16[264,256]{1,0:T(8,128)(2,1)S(1)}, bf16[264,256]{1,0:T(8,128)(2,1)S(1)}, u32[]{:S(2)}, u32[]{:S(2)}) collective-permute-start(bf16[264,256]{1,0:T(8,128)(2,1)S(1)} %get-tuple-element.29), channel_id=1, source_target_pairs={{0,1},{1,0},{2,3},{3,2},{4,5},{5,4},{6,7},{7,6},{8,9},{9,8},{10,11... | collective-permute-start | bytes 405512 | tf_op jit(solution)/shard_map/ppermute | solution.py:24
  8.6 0.4 collective-permute-start.1
  9.0 0.0 copy-start.1
  9.0 0.0 copy-start.3
  9.0 1.6 %collective-permute-start.4 = (bf16[256,256]{1,0:T(8,128)(2,1)S(1)}, bf16[256,256]{1,0:T(8,128)(2,1)S(1)}, u32[]{:S(2)}, u32[]{:S(2)}) collective-permute-start(bf16[256,256]{1,0:T(8,128)(2,1)S(1)} %get-tuple-element.36), channel_id=1, source_target_pairs={{0,1},{1,0},{2,3},{3,2},{4,5},{5,4},{6,7},{7,6},{8,9},{9,8},{10,11... | collective-permute-start | bytes 393224 | tf_op jit(solution)/shard_map/ppermute | solution.py:24
  10.6 1.4 %rest_of_ratings.1 = (bf16[256,256]{1,0:T(8,128)(2,1)S(1)}, bf16[256,256]{1,0:T(8,128)(2,1)S(1)}, bf16[256,256]{1,0:T(8,128)(2,1)S(1)}, bf16[256,256]{1,0:T(8,12...) custom-call(s32[2,1024,256]{2,1,0:T(8,128)} %ratings.1), custom_call_target="tpu_custom_call" | custom-call | tf_op jit(solution)/shard_map/rest_of_ratings/pallas_call | solution.py:199
  12.0 0.2 collective-permute-done.refs_1_.refs_0_
  12.2 0.7 %shard_map.77 = (f32[256,256]{1,0:T(8,128)S(1)}, f32[256,256]{1,0:T(8,128)S(1)}, f32[256,256]{1,0:T(8,128)S(1)}) custom-call(bf16[256,256]{1,0:T(8,128)(2,1)S(1)} %get-tuple-element.27.refs_0_, bf16[256,256]{1,0:T(8,128)(2,1)S(1)} %collective-permute-done.refs_1_.refs_0_, bf16[256,256]{1,0:T(8,128)(2,1)S(1)} %get-tuple-element.30.refs_2_, ...), custom_call_target="tpu_custom_call" | custom-call | flops 201326592 | tf_op jit(solution)/shard_map/pallas_call | solution.py:85
  12.9 1.6 %collective-permute-done.2 = bf16[264,256]{1,0:T(8,128)(2,1)S(1)} collective-permute-done((bf16[264,256]{1,0:T(8,128)(2,1)S(1)}, bf16[264,256]{1,0:T(8,128)(2,1)S(1)}, u32[]{:S(2)}, u32[]{:S(2)}) %collective-permute-start.2) | collective-permute-done | bytes 135200 | tf_op jit(solution)/shard_map/ppermute | solution.py:24
  14.6 2.8 %collective-permute-done.1.refs_1_ = bf16[256,256]{1,0:T(8,128)(2,1)S(1)} collective-permute-done((bf16[256,256]{1,0:T(8,128)(2,1)S(1)}, bf16[256,256]{1,0:T(8,128)(2,1)S(1)}, u32[]{:S(2)}, u32[]{:S(2)}) %collective-permute-start.1) | collective-permute-done | bytes 131104 | tf_op jit(solution)/shard_map/ppermute | solution.py:24
  17.3 0.5 shard_map.78
  17.8 1.5 %collective-permute-done.4.refs_2_ = bf16[256,256]{1,0:T(8,128)(2,1)S(1)} collective-permute-done((bf16[256,256]{1,0:T(8,128)(2,1)S(1)}, bf16[256,256]{1,0:T(8,128)(2,1)S(1)}, u32[]{:S(2)}, u32[]{:S(2)}) %collective-permute-start.4) | collective-permute-done | bytes 131104 | tf_op jit(solution)/shard_map/ppermute | solution.py:24
  19.3 0.4 shard_map.79
  19.7 0.4 collective-permute-start.6
  20.2 1.8 %collective-permute-start.8 = (bf16[264,256]{1,0:T(8,128)(2,1)S(1)}, bf16[264,256]{1,0:T(8,128)(2,1)S(1)}, u32[]{:S(2)}, u32[]{:S(2)}) collective-permute-start(bf16[264,256]{1,0:T(8,128)(2,1)S(1)} %pad_maximum_fusion), channel_id=1, source_target_pairs={{0,1},{1,0},{2,3},{3,2},{4,5},{5,4},{6,7},{7,6},{8,9},{9,8},{10,11... | collective-permute-start | bytes 405512 | tf_op jit(solution)/shard_map/ppermute | solution.py:24
  21.9 1.1 %collective-permute-start.3 = (bf16[256,256]{1,0:T(8,128)(2,1)S(1)}, bf16[256,256]{1,0:T(8,128)(2,1)S(1)}, u32[]{:S(2)}, u32[]{:S(2)}) collective-permute-start(bf16[256,256]{1,0:T(8,128)(2,1)S(1)} %get-tuple-element.34), channel_id=1, source_target_pairs={{0,2},{1,3},{2,0},{3,1},{4,6},{5,7},{6,4},{7,5},{8,10},{9,11},{10,... | collective-permute-start | bytes 393224 | tf_op jit(solution)/shard_map/ppermute | solution.py:24
  23.0 5.2 %collective-permute-done.6 = bf16[256,256]{1,0:T(8,128)(2,1)S(1)} collective-permute-done((bf16[256,256]{1,0:T(8,128)(2,1)S(1)}, bf16[256,256]{1,0:T(8,128)(2,1)S(1)}, u32[]{:S(2)}, u32[]{:S(2)}) %collective-permute-start.6) | collective-permute-done | bytes 131104 | tf_op jit(solution)/shard_map/ppermute | solution.py:24
  28.3 0.0 copy-done.1
  28.3 0.0 copy-done.3
  28.3 0.2 fusion
  28.4 0.1 collective-permute-start.9
  28.5 0.6 %collective-permute-done.3 = bf16[256,256]{1,0:T(8,128)(2,1)S(1)} collective-permute-done((bf16[256,256]{1,0:T(8,128)(2,1)S(1)}, bf16[256,256]{1,0:T(8,128)(2,1)S(1)}, u32[]{:S(2)}, u32[]{:S(2)}) %collective-permute-start.3) | collective-permute-done | bytes 131104 | tf_op jit(solution)/shard_map/ppermute | solution.py:24
  29.1 0.0 copy-done
  29.1 0.0 copy-done.2
  29.1 0.3 fusion.1
  29.4 2.6 %collective-permute-start.5 = (bf16[256,256]{1,0:T(8,128)(2,1)S(1)}, bf16[256,256]{1,0:T(8,128)(2,1)S(1)}, u32[]{:S(2)}, u32[]{:S(2)}) collective-permute-start(bf16[256,256]{1,0:T(8,128)(2,1)S(1)} %get-tuple-element.54.refs_0_), channel_id=1, source_target_pairs={{0,2},{1,3},{2,0},{3,1},{4,6},{5,7},{6,4},{7,5},{8,10},{9,11},{10,... | collective-permute-start | bytes 393224 | tf_op jit(solution)/shard_map/ppermute | solution.py:24
  32.0 0.0 collective-permute-start.7
  32.0 1.6 %collective-permute-start.11 = (bf16[256,256]{1,0:T(8,128)(2,1)S(1)}, bf16[256,256]{1,0:T(8,128)(2,1)S(1)}, u32[]{:S(2)}, u32[]{:S(2)}) collective-permute-start(bf16[256,256]{1,0:T(8,128)(2,1)S(1)} %get-tuple-element.47), channel_id=1, source_target_pairs={{0,1},{1,0},{2,3},{3,2},{4,5},{5,4},{6,7},{7,6},{8,9},{9,8},{10,11... | collective-permute-start | bytes 393224 | tf_op jit(solution)/shard_map/ppermute | solution.py:24
  33.6 0.0 collective-permute-done.8
  33.6 0.2 collective-permute-done.9.refs_4_
  33.8 4.7 %collective-permute-done.5.refs_1_.refs_0_ = bf16[256,256]{1,0:T(8,128)(2,1)S(1)} collective-permute-done((bf16[256,256]{1,0:T(8,128)(2,1)S(1)}, bf16[256,256]{1,0:T(8,128)(2,1)S(1)}, u32[]{:S(2)}, u32[]{:S(2)}) %collective-permute-start.5) | collective-permute-done | bytes 131104 | tf_op jit(solution)/shard_map/ppermute | solution.py:24
  38.5 0.7 %shard_map.80 = (f32[256,256]{1,0:T(8,128)S(1)}, f32[256,256]{1,0:T(8,128)S(1)}, bf16[256,256]{1,0:T(8,128)(2,1)S(1)}) custom-call(bf16[256,256]{1,0:T(8,128)(2,1)S(1)} %get-tuple-element.54.refs_0_, bf16[256,256]{1,0:T(8,128)(2,1)S(1)} %collective-permute-done.5.refs_1_.refs_0_, bf16[256,256]{1,0:T(8,128)(2,1)S(1)} %get-tuple-element.42.refs_2_, ...), custom_call_target="tpu_custom_call" | custom-call | flops 201326592 | tf_op jit(solution)/shard_map/pallas_call | solution.py:85
  39.2 2.2 %collective-permute-done.7.refs_1_ = bf16[256,256]{1,0:T(8,128)(2,1)S(1)} collective-permute-done((bf16[256,256]{1,0:T(8,128)(2,1)S(1)}, bf16[256,256]{1,0:T(8,128)(2,1)S(1)}, u32[]{:S(2)}, u32[]{:S(2)}) %collective-permute-start.7) | collective-permute-done | bytes 131104 | tf_op jit(solution)/shard_map/ppermute | solution.py:30
  41.4 0.5 shard_map.81
  41.8 0.5 collective-permute-done.11.refs_2_
  42.3 0.4 shard_map.82
  42.7 1.5 %collective-permute-start.13 = (bf16[256,256]{1,0:T(8,128)(2,1)S(1)}, bf16[256,256]{1,0:T(8,128)(2,1)S(1)}, u32[]{:S(2)}, u32[]{:S(2)}) collective-permute-start(bf16[256,256]{1,0:T(8,128)(2,1)S(1)} %get-tuple-element.51), channel_id=1, source_target_pairs={{0,29},{1,28},{2,31},{3,30},{4,1},{5,0},{6,3},{7,2},{8,5},{9,4},{1... | collective-permute-start | bytes 393224 | tf_op jit(solution)/shard_map/ppermute | solution.py:30
  44.2 1.1 %collective-permute-start.12 = (bf16[256,256]{1,0:T(8,128)(2,1)S(1)}, bf16[256,256]{1,0:T(8,128)(2,1)S(1)}, u32[]{:S(2)}, u32[]{:S(2)}) collective-permute-start(bf16[256,256]{1,0:T(8,128)(2,1)S(1)} %get-tuple-element.50), channel_id=1, source_target_pairs={{0,28},{1,29},{2,30},{3,31},{4,0},{5,1},{6,2},{7,3},{8,4},{9,5},{1... | collective-permute-start | bytes 393224 | tf_op jit(solution)/shard_map/ppermute | solution.py:30
  45.3 0.9 %collective-permute-start.10 = (bf16[256,256]{1,0:T(8,128)(2,1)S(1)}, bf16[256,256]{1,0:T(8,128)(2,1)S(1)}, u32[]{:S(2)}, u32[]{:S(2)}) collective-permute-start(bf16[256,256]{1,0:T(8,128)(2,1)S(1)} %get-tuple-element.45), channel_id=1, source_target_pairs={{0,2},{1,3},{2,0},{3,1},{4,6},{5,7},{6,4},{7,5},{8,10},{9,11},{10,... | collective-permute-start | bytes 393224 | tf_op jit(solution)/shard_map/ppermute | solution.py:24
  46.2 0.2 convolution_add_fusion.refs_3_
  46.4 0.8 %collective-permute-done.13.refs_3_ = bf16[256,256]{1,0:T(8,128)(2,1)S(1)} collective-permute-done((bf16[256,256]{1,0:T(8,128)(2,1)S(1)}, bf16[256,256]{1,0:T(8,128)(2,1)S(1)}, u32[]{:S(2)}, u32[]{:S(2)}) %collective-permute-start.13) | collective-permute-done | bytes 131104 | tf_op jit(solution)/shard_map/ppermute | solution.py:30
  47.2 0.9 %collective-permute-done.12.refs_2_ = bf16[256,256]{1,0:T(8,128)(2,1)S(1)} collective-permute-done((bf16[256,256]{1,0:T(8,128)(2,1)S(1)}, bf16[256,256]{1,0:T(8,128)(2,1)S(1)}, u32[]{:S(2)}, u32[]{:S(2)}) %collective-permute-start.12) | collective-permute-done | bytes 131104 | tf_op jit(solution)/shard_map/ppermute | solution.py:30
  48.1 0.8 %last_update.3 = f32[256,256]{1,0:T(8,128)} custom-call(f32[256,256]{1,0:T(8,128)S(1)} %get-tuple-element.53.refs_0_, f32[256,256]{1,0:T(8,128)S(1)} %get-tuple-element.56.refs_1_, bf16[256,256]{1,0:T(8,128)(2,1)S(1)} %collective-permute-done.12.refs_2_, bf16[256,256]{1,0:T(8,128)(2,1)S(1)} %collective-permute-done.13.refs_3_), custom_call_target="tpu_custom_call" | custom-call | tf_op jit(solution)/shard_map/last_update/pallas_call | solution.py:232
  49.0 5.0 %collective-permute-done.10.refs_2_ = bf16[256,256]{1,0:T(8,128)(2,1)S(1)} collective-permute-done((bf16[256,256]{1,0:T(8,128)(2,1)S(1)}, bf16[256,256]{1,0:T(8,128)(2,1)S(1)}, u32[]{:S(2)}, u32[]{:S(2)}) %collective-permute-start.10) | collective-permute-done | bytes 131104 | tf_op jit(solution)/shard_map/ppermute | solution.py:24
  54.0 0.8 %last_update.2 = f32[256,256]{1,0:T(8,128)} custom-call(f32[256,256]{1,0:T(8,128)S(1)} %get-tuple-element.55.refs_0_, f32[256,256]{1,0:T(8,128)S(1)} %get-tuple-element.57.refs_1_, bf16[256,256]{1,0:T(8,128)(2,1)S(1)} %collective-permute-done.10.refs_2_, f32[256,256]{1,0:T(8,128)S(1)} %convolution_add_fusion.refs_3_), custom_call_target="tpu_custom_call" | custom-call | tf_op jit(solution)/shard_map/last_update/pallas_call | solution.py:232
  (8 shorter events, 0.0 us)
Async XLA Ops:
  1.7 10.5 %collective-permute-start = (bf16[256,256]{1,0:T(8,128)(2,1)S(1)}, bf16[256,256]{1,0:T(8,128)(2,1)S(1)}, u32[]{:S(2)}, u32[]{:S(2)}) collective-permute-start(bf16[256,256]{1,0:T(8,128)(2,1)S(1)} %get-tuple-element.27.refs_0_), channel_id=1, source_target_pairs={{0,2},{1,3},{2,0},{3,1},{4,6},{5,7},{6,4},{7,5},{8,10},{9,11},{10,... | collective-permute-start | bytes 393224 | tf_op jit(solution)/shard_map/ppermute | solution.py:24
  6.9 7.6 %collective-permute-start.2 = (bf16[264,256]{1,0:T(8,128)(2,1)S(1)}, bf16[264,256]{1,0:T(8,128)(2,1)S(1)}, u32[]{:S(2)}, u32[]{:S(2)}) collective-permute-start(bf16[264,256]{1,0:T(8,128)(2,1)S(1)} %get-tuple-element.29), channel_id=1, source_target_pairs={{0,1},{1,0},{2,3},{3,2},{4,5},{5,4},{6,7},{7,6},{8,9},{9,8},{10,11... | collective-permute-start | bytes 405512 | tf_op jit(solution)/shard_map/ppermute | solution.py:24
  8.6 8.8 %collective-permute-start.1 = (bf16[256,256]{1,0:T(8,128)(2,1)S(1)}, bf16[256,256]{1,0:T(8,128)(2,1)S(1)}, u32[]{:S(2)}, u32[]{:S(2)}) collective-permute-start(bf16[256,256]{1,0:T(8,128)(2,1)S(1)} %get-tuple-element.28.refs_4_), channel_id=1, source_target_pairs={{0,1},{1,0},{2,3},{3,2},{4,5},{5,4},{6,7},{7,6},{8,9},{9,8},{10,11... | collective-permute-start | bytes 393224 | tf_op jit(solution)/shard_map/ppermute | solution.py:24
  9.0 19.2 %copy-start.1 = (f32[256,256]{1,0:T(8,128)S(1)}, f32[256,256]{1,0:T(8,128)}, u32[]{:S(2)}) copy-start(f32[256,256]{1,0:T(8,128)} %refs_0_.2) | copy-start | bytes 786436
  9.0 19.2 %copy-start.3 = (f32[256,256]{1,0:T(8,128)S(1)}, f32[256,256]{1,0:T(8,128)}, u32[]{:S(2)}) copy-start(f32[256,256]{1,0:T(8,128)} %param.9) | copy-start | bytes 786436
  9.0 10.3 %collective-permute-start.4 = (bf16[256,256]{1,0:T(8,128)(2,1)S(1)}, bf16[256,256]{1,0:T(8,128)(2,1)S(1)}, u32[]{:S(2)}, u32[]{:S(2)}) collective-permute-start(bf16[256,256]{1,0:T(8,128)(2,1)S(1)} %get-tuple-element.36), channel_id=1, source_target_pairs={{0,1},{1,0},{2,3},{3,2},{4,5},{5,4},{6,7},{7,6},{8,9},{9,8},{10,11... | collective-permute-start | bytes 393224 | tf_op jit(solution)/shard_map/ppermute | solution.py:24
  12.2 16.9 %copy-start = (f32[256,256]{1,0:T(8,128)S(1)}, f32[256,256]{1,0:T(8,128)}, u32[]{:S(2)}) copy-start(f32[256,256]{1,0:T(8,128)} %refs_1_.1) | copy-start | bytes 786436
  12.2 16.9 %copy-start.2 = (f32[256,256]{1,0:T(8,128)S(1)}, f32[256,256]{1,0:T(8,128)}, u32[]{:S(2)}) copy-start(f32[256,256]{1,0:T(8,128)} %param.7) | copy-start | bytes 786436
  19.7 8.5 %collective-permute-start.6 = (bf16[256,256]{1,0:T(8,128)(2,1)S(1)}, bf16[256,256]{1,0:T(8,128)(2,1)S(1)}, u32[]{:S(2)}, u32[]{:S(2)}) collective-permute-start(bf16[256,256]{1,0:T(8,128)(2,1)S(1)} %get-tuple-element.40), channel_id=1, source_target_pairs={{0,1},{1,0},{2,3},{3,2},{4,5},{5,4},{6,7},{7,6},{8,9},{9,8},{10,11... | collective-permute-start | bytes 393224 | tf_op jit(solution)/shard_map/ppermute | solution.py:24
  20.2 13.4 %collective-permute-start.8 = (bf16[264,256]{1,0:T(8,128)(2,1)S(1)}, bf16[264,256]{1,0:T(8,128)(2,1)S(1)}, u32[]{:S(2)}, u32[]{:S(2)}) collective-permute-start(bf16[264,256]{1,0:T(8,128)(2,1)S(1)} %pad_maximum_fusion), channel_id=1, source_target_pairs={{0,1},{1,0},{2,3},{3,2},{4,5},{5,4},{6,7},{7,6},{8,9},{9,8},{10,11... | collective-permute-start | bytes 405512 | tf_op jit(solution)/shard_map/ppermute | solution.py:24
  21.9 7.2 %collective-permute-start.3 = (bf16[256,256]{1,0:T(8,128)(2,1)S(1)}, bf16[256,256]{1,0:T(8,128)(2,1)S(1)}, u32[]{:S(2)}, u32[]{:S(2)}) collective-permute-start(bf16[256,256]{1,0:T(8,128)(2,1)S(1)} %get-tuple-element.34), channel_id=1, source_target_pairs={{0,2},{1,3},{2,0},{3,1},{4,6},{5,7},{6,4},{7,5},{8,10},{9,11},{10,... | collective-permute-start | bytes 393224 | tf_op jit(solution)/shard_map/ppermute | solution.py:24
  28.4 5.3 %collective-permute-start.9 = (bf16[256,256]{1,0:T(8,128)(2,1)S(1)}, bf16[256,256]{1,0:T(8,128)(2,1)S(1)}, u32[]{:S(2)}, u32[]{:S(2)}) collective-permute-start(bf16[256,256]{1,0:T(8,128)(2,1)S(1)} %get-tuple-element.52), channel_id=1, source_target_pairs={{0,4},{1,5},{2,6},{3,7},{4,8},{5,9},{6,10},{7,11},{8,12},{9,13},{1... | collective-permute-start | bytes 393224 | tf_op jit(solution)/shard_map/ppermute | solution.py:30
  29.4 9.1 %collective-permute-start.5 = (bf16[256,256]{1,0:T(8,128)(2,1)S(1)}, bf16[256,256]{1,0:T(8,128)(2,1)S(1)}, u32[]{:S(2)}, u32[]{:S(2)}) collective-permute-start(bf16[256,256]{1,0:T(8,128)(2,1)S(1)} %get-tuple-element.54.refs_0_), channel_id=1, source_target_pairs={{0,2},{1,3},{2,0},{3,1},{4,6},{5,7},{6,4},{7,5},{8,10},{9,11},{10,... | collective-permute-start | bytes 393224 | tf_op jit(solution)/shard_map/ppermute | solution.py:24
  32.0 9.4 %collective-permute-start.7 = (bf16[256,256]{1,0:T(8,128)(2,1)S(1)}, bf16[256,256]{1,0:T(8,128)(2,1)S(1)}, u32[]{:S(2)}, u32[]{:S(2)}) collective-permute-start(bf16[256,256]{1,0:T(8,128)(2,1)S(1)} %get-tuple-element.52), channel_id=1, source_target_pairs={{0,5},{1,4},{2,7},{3,6},{4,9},{5,8},{6,11},{7,10},{8,13},{9,12},{1... | collective-permute-start | bytes 393224 | tf_op jit(solution)/shard_map/ppermute | solution.py:30
  32.0 10.3 %collective-permute-start.11 = (bf16[256,256]{1,0:T(8,128)(2,1)S(1)}, bf16[256,256]{1,0:T(8,128)(2,1)S(1)}, u32[]{:S(2)}, u32[]{:S(2)}) collective-permute-start(bf16[256,256]{1,0:T(8,128)(2,1)S(1)} %get-tuple-element.47), channel_id=1, source_target_pairs={{0,1},{1,0},{2,3},{3,2},{4,5},{5,4},{6,7},{7,6},{8,9},{9,8},{10,11... | collective-permute-start | bytes 393224 | tf_op jit(solution)/shard_map/ppermute | solution.py:24
  42.7 4.4 %collective-permute-start.13 = (bf16[256,256]{1,0:T(8,128)(2,1)S(1)}, bf16[256,256]{1,0:T(8,128)(2,1)S(1)}, u32[]{:S(2)}, u32[]{:S(2)}) collective-permute-start(bf16[256,256]{1,0:T(8,128)(2,1)S(1)} %get-tuple-element.51), channel_id=1, source_target_pairs={{0,29},{1,28},{2,31},{3,30},{4,1},{5,0},{6,3},{7,2},{8,5},{9,4},{1... | collective-permute-start | bytes 393224 | tf_op jit(solution)/shard_map/ppermute | solution.py:30
  44.2 3.9 %collective-permute-start.12 = (bf16[256,256]{1,0:T(8,128)(2,1)S(1)}, bf16[256,256]{1,0:T(8,128)(2,1)S(1)}, u32[]{:S(2)}, u32[]{:S(2)}) collective-permute-start(bf16[256,256]{1,0:T(8,128)(2,1)S(1)} %get-tuple-element.50), channel_id=1, source_target_pairs={{0,28},{1,29},{2,30},{3,31},{4,0},{5,1},{6,2},{7,3},{8,4},{9,5},{1... | collective-permute-start | bytes 393224 | tf_op jit(solution)/shard_map/ppermute | solution.py:30
  45.3 8.7 %collective-permute-start.10 = (bf16[256,256]{1,0:T(8,128)(2,1)S(1)}, bf16[256,256]{1,0:T(8,128)(2,1)S(1)}, u32[]{:S(2)}, u32[]{:S(2)}) collective-permute-start(bf16[256,256]{1,0:T(8,128)(2,1)S(1)} %get-tuple-element.45), channel_id=1, source_target_pairs={{0,2},{1,3},{2,0},{3,1},{4,6},{5,7},{6,4},{7,5},{8,10},{9,11},{10,... | collective-permute-start | bytes 393224 | tf_op jit(solution)/shard_map/ppermute | solution.py:24
